TPU v7x, 256 devices: a whole 4x4x8 slice. The times are simulated.
256 devices in a mesh: rows: 32 (over x, z), mem: 8 (over y, core).
Axes of the slice: x: 4, y: 4, z: 8, core: 2. Of those that a mesh axis runs over, the one named last changes fastest.
Arguments:
- factor_panel: float32 [8, 32, 128, 2048], P(None, 'rows'), may hold values from -0.125 to 0.125
- right_side: float32 [8, 32, 128, 256], P(None, 'rows', None, 'mem'), may hold values from -6 to 6
- inverses: float32 [4, 512, 512], replicated, may hold values from -0.125 to 1.5, as said below
Outputs:
- solved: float32 [2048, 256], P(None, 'mem')
- remainder: float32 [8, 32, 128, 256], P(None, 'rows', None, 'mem')
- spread: float32 [8, 32, 128], P(None, 'rows')
Inputs may be any that keep to these rules, and one draw needn't show every extreme that they name: `inverses`: each block is lower triangular with its diagonal between 0.5 and 1.5 and its entries below the diagonal between -0.125 and 0.125.
All inputs are finite; a program needn't handle non-finite values.
Results may differ from a plain program's by a relative error of at most 0.0001.
Values sent between devices are 32-bit elements; how exact they have to be, the bound alone decides.
No kernel may reach another device: no remote copies, remote signals or barrier semaphores. Data moves between devices by JAX's collectives and lax.ppermute only.
A program may use at most 64 MiB of HBM per device.

v0:
```python
import jax
import jax.numpy as jnp
from jax import lax
from jax.sharding import PartitionSpec as P

highest = lax.Precision.HIGHEST


def solve_block(inverse, residual_piece, first_owner, tiles_step, tile_rows):
    gathered = lax.all_gather(residual_piece, "rows", axis=0, tiled=True)
    window = lax.slice_in_dim(
        gathered, first_owner * tile_rows, (first_owner + tiles_step) * tile_rows, axis=0
    )
    return jnp.dot(inverse, window, precision=highest, preferred_element_type=jnp.float32)


def shards(factor_panel, right_side, inverses):
    row_devices = lax.axis_size("rows")
    position = lax.axis_index("rows")
    tile_blocks, tile_rows, columns = (
        factor_panel.shape[0],
        factor_panel.shape[2],
        factor_panel.shape[3],
    )
    member_cols = right_side.shape[3]
    lower_rows = factor_panel.reshape(tile_blocks, tile_rows, columns)
    right_rows = right_side.reshape(tile_blocks, tile_rows, member_cols)
    section_count, step_width = (inverses.shape[0], inverses.shape[1])
    tiles_step = step_width // tile_rows
    head_count = min(tile_blocks, -(-(columns // tile_rows) // row_devices))
    global_block = jnp.arange(head_count, dtype=jnp.int32) * row_devices + position
    cutoff = jnp.where(
        global_block * tile_rows < columns, global_block // tiles_step * step_width, columns
    )
    column_ids = jnp.arange(columns, dtype=jnp.int32)
    keep_mask = column_ids[None, None, :] < cutoff[:, None, None]
    masked_head = jnp.where(keep_mask, lower_rows[:head_count], jnp.float32(0.0))
    tail_panel = lower_rows[head_count:]
    blocks = []
    head_left = right_rows[:head_count]
    tail_left = right_rows[head_count:]
    for section in range(section_count):
        first_tile = section * tiles_step
        block_slot = first_tile // row_devices
        first_owner = first_tile % row_devices
        solved_block = solve_block(
            inverses[section], head_left[block_slot], first_owner, tiles_step, tile_rows
        )
        blocks.append(solved_block)
        start = section * step_width
        head_left = head_left - jnp.einsum(
            "jrc,cm->jrm",
            masked_head[:, :, start : start + step_width],
            solved_block,
            precision=highest,
            preferred_element_type=jnp.float32,
        )
        tail_left = tail_left - jnp.einsum(
            "jrc,cm->jrm",
            tail_panel[:, :, start : start + step_width],
            solved_block,
            precision=highest,
            preferred_element_type=jnp.float32,
        )
    solved = jnp.concatenate(blocks, axis=0)
    remainder = jnp.concatenate([head_left, tail_left], axis=0)
    member_total = jnp.sum(remainder, axis=2)
    squares = jnp.sum(remainder * remainder, axis=2)
    member_total, squares = lax.psum((member_total, squares), "mem")
    member_count = member_cols * lax.axis_size("mem")
    member_mean = member_total / member_count
    spread = squares / member_count - member_mean * member_mean
    return (solved, remainder.reshape(right_side.shape), spread.reshape(tile_blocks, 1, tile_rows))


def solution(mesh):
    return jax.shard_map(
        shards,
        mesh=mesh,
        in_specs=(P(None, "rows", None, None), P(None, "rows", None, "mem"), P()),
        out_specs=(P(None, "mem"), P(None, "rows", None, "mem"), P(None, "rows", None)),
        check_vma=False,
    )
```

profile of v0, /device:TPU:1, one launch (start us, length us, event | category | flops | bytes accessed | tf_op | source)
XLA Modules:
  0.0 212.6 jit_solution(3758968072523036752)
XLA Ops:
  0.7 0.7 slice.71
  1.4 39.1 %all-gather = f32[1,1,4096,32]{2,3,1,0:T(8,128)S(1)} all-gather(f32[1,1,128,32]{2,3,1,0:T(8,128)S(1)} %slice.71), channel_id=2, replica_groups=mesh['rows'=32,'mem'=8] {'rows'}, dimensions={2}, use_global_device_ids=true | all-gather | bytes 540672 | tf_op jit(solution)/shard_map/all_gather | solution.py:10
  40.4 2.3 %fusion.39 = f32[512,32]{0,1:T(8,128)S(1)} fusion(f32[4,512,512]{2,1,0:T(8,128)} %param.5, f32[1,1,4096,32]{2,3,1,0:T(8,128)S(1)} %all-gather), kind=kOutput, calls=%fused_computation.29 | convolution fusion | flops 100663296 | bytes 1179648 | tf_op jit(solution)/shard_map/dot_general | solution.py:14
  42.7 0.0 copy-start
  42.7 1.5 bitcast_select_fusion
  44.2 1.3 convolution_subtract_fusion.3
  45.6 32.8 %all_gather.13 = f32[4096,32]{0,1:T(8,128)S(1)} all-gather(f32[128,32]{0,1:T(8,128)S(1)} %convolution_subtract_fusion.3), channel_id=1, replica_groups=mesh['rows'=32,'mem'=8] {'rows'}, dimensions={0}, use_global_device_ids=true | all-gather | bytes 540672 | tf_op jit(solution)/shard_map/all_gather | solution.py:10
  78.3 2.3 %fusion.37 = f32[32,512]{1,0:T(8,128)S(1)} fusion(f32[4,512,512]{2,1,0:T(8,128)} %param.5, f32[4096,32]{0,1:T(8,128)S(1)} %all_gather.13), kind=kOutput, calls=%fused_computation.26 | convolution fusion | flops 100663296 | bytes 1179648 | tf_op jit(solution)/shard_map/dot_general | solution.py:14
  80.6 0.4 convolution_subtract_fusion.2
  81.0 32.8 %all_gather.14 = f32[4096,32]{0,1:T(8,128)S(1)} all-gather(f32[128,32]{0,1:T(8,128)S(1)} %convolution_subtract_fusion.2), channel_id=1, replica_groups=mesh['rows'=32,'mem'=8] {'rows'}, dimensions={0}, use_global_device_ids=true | all-gather | bytes 540672 | tf_op jit(solution)/shard_map/all_gather | solution.py:10
  113.8 2.3 %fusion.35 = f32[32,512]{1,0:T(8,128)S(1)} fusion(f32[4,512,512]{2,1,0:T(8,128)} %param.5, f32[4096,32]{0,1:T(8,128)S(1)} %all_gather.14), kind=kOutput, calls=%fused_computation.24 | convolution fusion | flops 100663296 | bytes 1179648 | tf_op jit(solution)/shard_map/dot_general | solution.py:14
  116.1 0.4 convolution_subtract_fusion.1
  116.4 34.4 %all_gather.15 = f32[4096,32]{0,1:T(8,128)S(1)} all-gather(f32[128,32]{0,1:T(8,128)S(1)} %convolution_subtract_fusion.1), channel_id=1, replica_groups=mesh['rows'=32,'mem'=8] {'rows'}, dimensions={0}, use_global_device_ids=true | all-gather | bytes 540672 | tf_op jit(solution)/shard_map/all_gather | solution.py:10
  150.8 2.3 %fusion.33 = f32[32,512]{1,0:T(8,128)S(1)} fusion(f32[4,512,512]{2,1,0:T(8,128)} %param.5, f32[4096,32]{0,1:T(8,128)S(1)} %all_gather.15), kind=kOutput, calls=%fused_computation.22 | convolution fusion | flops 100663296 | bytes 1179648 | tf_op jit(solution)/shard_map/dot_general | solution.py:14
  153.1 0.4 fusion.32
  153.5 0.7 pad_maximum_fusion
  154.2 0.0 copy-done
  154.2 0.0 copy-start.1
  154.2 0.9 slice_bitcast_fusion
  155.1 1.8 fusion.23
  156.9 1.8 fusion.20
  158.7 0.0 copy-done.1
  158.7 1.8 fusion.17
  160.5 1.8 fusion.29
  162.3 0.7 multiply_reduce_fusion
  162.9 49.1 %all-reduce = (f32[8,128]{1,0:T(8,128)S(1)}, f32[8,128]{1,0:T(8,128)S(1)}) all-reduce(f32[8,128]{1,0:T(8,128)S(1)} %get-tuple-element.7, f32[8,128]{1,0:T(8,128)S(1)} %get-tuple-element.6), channel_id=1, replica_groups=mesh['rows'=32,'mem'=8] {'mem'}, use_global_device_ids=true, to_apply=%region_3.4 | all-reduce | flops 2048 | bytes 16384 | tf_op jit(solution)/shard_map/psum | solution.py:69
  212.0 0.6 multiply_subtract_fusion
  (1 shorter events, 0.0 us)
Async XLA Ops:
  42.7 111.5 %copy-start = (f32[8,1,128,2048]{3,2,1,0:T(8,128)S(1)}, f32[8,1,128,2048]{3,2,1,0:T(8,128)}, u32[]{:S(2)}) copy-start(f32[8,1,128,2048]{3,2,1,0:T(8,128)} %param.3) | copy-start | bytes 25165828
  154.2 4.5 %copy-start.1 = (f32[8,1,128,32]{2,3,1,0:T(8,128)S(1)}, f32[8,1,128,32]{2,3,1,0:T(8,128)}, u32[]{:S(2)}) copy-start(f32[8,1,128,32]{2,3,1,0:T(8,128)} %param.4) | copy-start | bytes 393220
where the time goes:
time: 213 us
  blocking collectives  188 us (88%)
  matrix products  18.6 us (9%)
  other arithmetic  3.47 us (2%)
    all_gather x4, blocking collectives, solve_block(): gathered = lax.all_gather(residual_piece, 'rows', axis=0, tiled=True)  139 us
    psum x1, blocking collectives, shards(): member_total, squares = lax.psum((member_total, squares), 'mem')  49.1 us
    dot_general x4, matrix products, solve_block(): jnp.dot(inverse, window, precision=highest, preferred_element_type=jnp.fl...  9.06 us
    dot_general x4, matrix products, shards(): jnp.einsum('jrc,cm->jrm', tail_panel[:, :, start:start + step_width], sol...  7.07 us

commit v1 on v0

v1 whole, which is shorter than its diff:
```python
import jax
import jax.numpy as jnp
from jax import lax
from jax.sharding import Mesh, PartitionSpec as P

highest = lax.Precision.HIGHEST
AXES = ("xh", "xl", "zh", "zl", "y", "core")
SIZES = (2, 2, 2, 4, 4, 2)
ROWS = AXES[:4]
OWNERS = AXES[1:4]
MEM = AXES[4:]
TILES = 4
STEPS = 4


def spread_tile(tile, axes, count):
    copies = jnp.broadcast_to(tile[None], (count,) + tile.shape)
    return lax.all_to_all(copies, axes, 0, 0)


def times_rows(left, right):
    return lax.dot_general(
        left, right, (((1,), (1,)), ((), ())),
        precision=highest, preferred_element_type=jnp.float32,
    )


def side_by_side(tiles):
    count, members, rows = tiles.shape
    return tiles.transpose(1, 0, 2).reshape(members, count * rows)


def shards(factor_panel, right_side, inverses):
    blocks, _, rows, columns = factor_panel.shape
    members = right_side.shape[3]
    width = inverses.shape[1]
    panel = factor_panel.reshape(blocks, rows, columns)
    right = right_side.reshape(blocks, rows, members).transpose(0, 2, 1)
    tile = lax.axis_index(ROWS)
    step_of = tile // TILES
    is_head = step_of < STEPS

    own = right[0]
    for step in range(STEPS - 1):
        tiles = spread_tile(own, OWNERS, 16)
        residual = side_by_side(tiles[step * TILES:(step + 1) * TILES])
        solved = times_rows(residual, inverses[step])
        change = times_rows(solved, panel[0, :, step * width:(step + 1) * width])
        own = jnp.where(is_head & (step < step_of), own - change, own)

    tiles = spread_tile(own, ROWS, 32)[:STEPS * TILES]
    residual = side_by_side(tiles).reshape(members, STEPS, width)
    solved = jnp.concatenate(
        [times_rows(residual[:, step], inverses[step]) for step in range(STEPS)], axis=1
    )
    product = times_rows(solved, panel.reshape(blocks * rows, columns))
    product = product.reshape(members, blocks, rows).transpose(1, 0, 2)
    left = right - product
    left = left.at[0].set(jnp.where(is_head, own, left[0]))

    sums = jnp.stack([jnp.sum(left, axis=1), jnp.sum(left * left, axis=1)])
    sums = jnp.sum(spread_tile(sums, MEM, 8), axis=0)
    count = members * 8
    mean = sums[0] / count
    spread = sums[1] / count - mean * mean
    return (
        solved.T,
        left.transpose(0, 2, 1).reshape(right_side.shape),
        spread.reshape(blocks, 1, rows),
    )


def solution(mesh):
    fine = Mesh(mesh.devices.reshape(SIZES), AXES)
    return jax.shard_map(
        shards,
        mesh=fine,
        in_specs=(P(None, ROWS, None, None), P(None, ROWS, None, MEM), P()),
        out_specs=(P(None, MEM), P(None, ROWS, None, MEM), P(None, ROWS, None)),
        check_vma=False,
    )
```

time: 213 us -> 117 us (0.55)
  blocking collectives: 188 us -> 20.4 us
  starting transfers between devices: 0 us -> 31.1 us
  waiting for transfers between devices: 0 us -> 28.7 us
  matrix products: 18.6 us -> 29.8 us
  local copies, waits for them, and re-layouts: 1.67 us -> 4.05 us
    all_gather x4 -> x0, blocking collectives: 139 us -> none  [solve_block(): gathered = lax.all_gather(residual_piece, 'rows', axis=0, tiled=True)]
    psum x1 -> x0, blocking collectives: 49.1 us -> none  [shards(): member_total, squares = lax.psum((member_total, squares), 'mem')]
    all_to_all x0 -> x4, starting transfers between devices: none -> 31.1 us  [spread_tile(): return lax.all_to_all(copies, axes, 0, 0)]
    all_to_all x0 -> x4, waiting for transfers between devices: none -> 28.7 us  [spread_tile(): return lax.all_to_all(copies, axes, 0, 0)]
    all_to_all x0 -> x1, blocking collectives: none -> 20.4 us  [spread_tile(): return lax.all_to_all(copies, axes, 0, 0)]
    dot_general x12 -> x11, matrix products: 18.6 us -> 29.8 us  [times_rows(): lax.dot_general(left, right, (((1,), (1,)), ((), ())), precision=highest,...]
    broadcast_in_dim x0 -> x5, local copies, waits for them, and re-layouts: none -> 2.86 us  [spread_tile(): copies = jnp.broadcast_to(tile[None], (count,) + tile.shape)]
  transfers between devices with their start and end apart: 0 -> 4, of which waited for: 0 -> 4; matrix products, arithmetic and copies ran while one was open for 0% -> 1% of each run, Pallas kernels for 0% -> 0%
where the time goes in v1:
time: 117 us; the launch traced here: 116 us
  starting transfers between devices  31.1 us (27%)
  matrix products  29.8 us (25%)
  waiting for transfers between devices  28.7 us (25%)
  blocking collectives  20.4 us (17%)
  local copies, waits for them, and re-layouts  4.05 us (3%)
  other arithmetic  1.37 us (1%)
    all_to_all x4, starting transfers between devices, spread_tile(): return lax.all_to_all(copies, axes, 0, 0)  31.1 us
    dot_general x11, matrix products, times_rows(): lax.dot_general(left, right, (((1,), (1,)), ((), ())), precision=highest,...  29.8 us
    all_to_all x4, waiting for transfers between devices, spread_tile(): return lax.all_to_all(copies, axes, 0, 0)  28.7 us
    all_to_all x1, blocking collectives, spread_tile(): return lax.all_to_all(copies, axes, 0, 0)  20.4 us
    broadcast_in_dim x5, local copies, waits for them, and re-layouts, spread_tile(): copies = jnp.broadcast_to(tile[None], (count,) + tile.shape)  2.86 us
  transfers between devices with their start and end apart: 4, of which 4 were waited for; matrix products, arithmetic and copies ran while one was open for 1% of the time, Pallas kernels for 0%

profile of v1, /device:TPU:1, one launch (start us, length us, event | category | flops | bytes accessed | tf_op | source)
XLA Modules:
  0.0 116.3 jit_solution(1104770992589893004)
XLA Ops:
  0.6 0.7 slice_bitcast_fusion.11
  1.4 0.7 broadcast_in_dim.10
  2.1 10.0 %all-to-all-start = ((f32[16,32,128]{2,1,0:T(8,128)}), f32[16,32,128]{2,1,0:T(8,128)S(1)}, u32[]{:S(2)}, u32[]{:S(2)}) async-start(f32[16,32,128]{2,1,0:T(8,128)} %broadcast_in_dim.10), calls=%async_computation | async-start | bytes 524288 | tf_op jit(solution)/shard_map/all_to_all | solution.py:18
  12.2 8.8 %all-to-all-done = f32[16,32,128]{2,1,0:T(8,128)S(1)} async-done(((f32[16,32,128]{2,1,0:T(8,128)}), f32[16,32,128]{2,1,0:T(8,128)S(1)}, u32[]{:S(2)}, u32[]{:S(2)}) %all-to-all-start) | async-done | bytes 262176 | tf_op jit(solution)/shard_map/all_to_all | solution.py:18
  20.9 2.3 %fusion.16 = f32[32,512]{1,0:T(8,128)S(1)} fusion(f32[4,512,512]{2,1,0:T(8,128)} %param.7, f32[16,32,128]{2,1,0:T(8,128)S(1)} %all-to-all-done), kind=kOutput, calls=%fused_computation.20 | convolution fusion | flops 100663296 | bytes 1179648 | tf_op jit(solution)/shard_map/dot_general | solution.py:22
  23.2 1.3 %fusion.3 = f32[32,128]{1,0:T(8,128)S(1)} fusion(f32[32,512]{1,0:T(8,128)S(1)} %fusion.16, f32[8,128,2048]{2,1,0:T(8,128)} %bitcast.110, pred[]{:T(512)S(6)} %and.24, f32[8,32,128]{2,1,0:T(8,128)} %bitcast.115), kind=kOutput, calls=%fused_computation.7 | convolution fusion | flops 25174016 | bytes 360449 | tf_op jit(solution)/shard_map/dot_general | solution.py:22
  24.5 0.7 broadcast_in_dim.11
  25.2 5.4 %all-to-all-start.1 = ((f32[16,32,128]{2,1,0:T(8,128)}), f32[16,32,128]{2,1,0:T(8,128)S(1)}, u32[]{:S(2)}, u32[]{:S(2)}) async-start(f32[16,32,128]{2,1,0:T(8,128)} %broadcast_in_dim.11), calls=%async_computation.1 | async-start | bytes 524288 | tf_op jit(solution)/shard_map/all_to_all | solution.py:18
  30.7 7.9 %all-to-all-done.1 = f32[16,32,128]{2,1,0:T(8,128)S(1)} async-done(((f32[16,32,128]{2,1,0:T(8,128)}), f32[16,32,128]{2,1,0:T(8,128)S(1)}, u32[]{:S(2)}, u32[]{:S(2)}) %all-to-all-start.1) | async-done | bytes 262176 | tf_op jit(solution)/shard_map/all_to_all | solution.py:18
  38.6 2.3 %fusion.12 = f32[32,512]{1,0:T(8,128)S(1)} fusion(f32[4,512,512]{2,1,0:T(8,128)} %param.7, f32[16,32,128]{2,1,0:T(8,128)S(1)} %all-to-all-done.1), kind=kOutput, calls=%fused_computation.16 | convolution fusion | flops 100663296 | bytes 1179648 | tf_op jit(solution)/shard_map/dot_general | solution.py:22
  40.8 1.3 %fusion.2 = f32[32,128]{1,0:T(8,128)S(1)} fusion(f32[32,128]{1,0:T(8,128)S(1)} %fusion.3, f32[32,512]{1,0:T(8,128)S(1)} %fusion.12, f32[8,128,2048]{2,1,0:T(8,128)} %bitcast.111, pred[]{:T(512)S(6)} %and.23), kind=kOutput, calls=%fused_computation.5 | convolution fusion | flops 25174016 | bytes 360449 | tf_op jit(solution)/shard_map/dot_general | solution.py:22
  42.2 0.7 broadcast_in_dim.12
  42.9 6.2 %all-to-all-start.2 = ((f32[16,32,128]{2,1,0:T(8,128)}), f32[16,32,128]{2,1,0:T(8,128)S(1)}, u32[]{:S(2)}, u32[]{:S(2)}) async-start(f32[16,32,128]{2,1,0:T(8,128)} %broadcast_in_dim.12), calls=%async_computation.2 | async-start | bytes 524288 | tf_op jit(solution)/shard_map/all_to_all | solution.py:18
  49.1 7.9 %all-to-all-done.2 = f32[16,32,128]{2,1,0:T(8,128)S(1)} async-done(((f32[16,32,128]{2,1,0:T(8,128)}), f32[16,32,128]{2,1,0:T(8,128)S(1)}, u32[]{:S(2)}, u32[]{:S(2)}) %all-to-all-start.2) | async-done | bytes 262176 | tf_op jit(solution)/shard_map/all_to_all | solution.py:18
  57.0 2.3 %fusion.8 = f32[32,512]{1,0:T(8,128)S(1)} fusion(f32[4,512,512]{2,1,0:T(8,128)} %param.7, f32[16,32,128]{2,1,0:T(8,128)S(1)} %all-to-all-done.2), kind=kOutput, calls=%fused_computation.12 | convolution fusion | flops 100663296 | bytes 1179648 | tf_op jit(solution)/shard_map/dot_general | solution.py:22
  59.3 1.3 %fusion.1 = f32[32,128]{1,0:T(8,128)S(1)} fusion(f32[32,128]{1,0:T(8,128)S(1)} %fusion.2, f32[32,512]{1,0:T(8,128)S(1)} %fusion.8, f32[8,128,2048]{2,1,0:T(8,128)} %bitcast.112, pred[]{:T(512)S(6)} %and.22), kind=kOutput, calls=%fused_computation.3 | convolution fusion | flops 25174016 | bytes 360449 | tf_op jit(solution)/shard_map/dot_general | solution.py:22
  60.6 0.0 copy-start.1
  60.6 0.1 broadcast_in_dim.13
  60.7 20.4 %all_to_all.25 = f32[32,32,128]{2,1,0:T(8,128)S(1)} all-to-all(f32[32,32,128]{2,1,0:T(8,128)S(1)} %broadcast_in_dim.13), channel_id=1, replica_groups=mesh['xh'=2,'xl'=2,'zh'=2,'zl'=4,'y'=4,'core'=2] {'xh','xl','zh','zl'}, dimensions={0} | all-to-all | bytes 1048576 | tf_op jit(solution)/shard_map/all_to_all | solution.py:18
  81.1 0.2 copy.16
  81.3 0.1 reshape_reshape.4
  81.4 0.2 fusion.49
  81.6 2.3 %fusion.14 = f32[32,512]{1,0:T(8,128)S(1)} fusion(f32[4,512,512]{2,1,0:T(8,128)} %param.7, f32[32,1,512]{2,1,0:T(1,128)S(1)} %get-tuple-element.29), kind=kOutput, calls=%fused_computation.18 | convolution fusion | flops 100663296 | bytes 1179648 | tf_op jit(solution)/shard_map/dot_general | solution.py:22
  83.9 2.3 %fusion.4 = f32[32,512]{1,0:T(8,128)S(1)} fusion(f32[4,512,512]{2,1,0:T(8,128)} %param.7, f32[32,1,512]{2,1,0:T(1,128)S(1)} %get-tuple-element.30), kind=kOutput, calls=%fused_computation.8 | convolution fusion | flops 100663296 | bytes 1179648 | tf_op jit(solution)/shard_map/dot_general | solution.py:22
  86.1 2.3 %fusion.6 = f32[32,512]{1,0:T(8,128)S(1)} fusion(f32[4,512,512]{2,1,0:T(8,128)} %param.7, f32[32,1,512]{2,1,0:T(1,128)S(1)} %get-tuple-element.31), kind=kOutput, calls=%fused_computation.10 | convolution fusion | flops 100663296 | bytes 1179648 | tf_op jit(solution)/shard_map/dot_general | solution.py:22
  88.4 2.3 %fusion.10 = f32[32,512]{1,0:T(8,128)S(1)} fusion(f32[4,512,512]{2,1,0:T(8,128)} %param.7, f32[32,1,512]{2,1,0:T(1,128)S(1)} %get-tuple-element.32), kind=kOutput, calls=%fused_computation.14 | convolution fusion | flops 100663296 | bytes 1179648 | tf_op jit(solution)/shard_map/dot_general | solution.py:22
  90.7 0.0 copy-done.1
  90.7 10.0 %fusion = f32[8,32,128]{2,1,0:T(8,128)S(1)} fusion(f32[32,512]{1,0:T(8,128)S(1)} %fusion.4, f32[32,512]{1,0:T(8,128)S(1)} %fusion.6, f32[32,512]{1,0:T(8,128)S(1)} %fusion.10, f32[32,512]{1,0:T(8,128)S(1)} %fusion.14, f32[8,1,128,32]{2,3,1,0:T(8,128)S(1)} %copy-done.1, f32[8,1,128,2048]{3,2,1,0:T(8,128)} %param.5), kind=kOutput, calls=%fused_computation.1 | convolution fusion | flops 805535744 | bytes 8912896 | tf_op jit(solution)/shard_map/dot_general | solution.py:22
  100.7 0.0 copy-start
  100.7 0.6 broadcast_in_dim.14
  101.4 9.5 %all-to-all-start.4 = ((f32[8,2,8,128]{3,2,1,0:T(8,128)}), f32[8,2,8,128]{3,2,1,0:T(8,128)S(1)}, u32[]{:S(2)}, u32[]{:S(2)}) async-start(f32[8,2,8,128]{3,2,1,0:T(8,128)} %broadcast_in_dim.14), calls=%async_computation.4 | async-start | bytes 131072 | tf_op jit(solution)/shard_map/all_to_all | solution.py:18
  110.8 0.7 fusion.26
  111.5 4.1 %all-to-all-done.4 = f32[8,2,8,128]{3,2,1,0:T(8,128)S(1)} async-done(((f32[8,2,8,128]{3,2,1,0:T(8,128)}), f32[8,2,8,128]{3,2,1,0:T(8,128)S(1)}, u32[]{:S(2)}, u32[]{:S(2)}) %all-to-all-start.4) | async-done | bytes 65568 | tf_op jit(solution)/shard_map/all_to_all | solution.py:18
  115.7 0.6 fusion.45
  116.3 0.0 copy-done
  (5 shorter events, 0.1 us)
Async XLA Ops:
  2.1 18.8 %all-to-all-start = ((f32[16,32,128]{2,1,0:T(8,128)}), f32[16,32,128]{2,1,0:T(8,128)S(1)}, u32[]{:S(2)}, u32[]{:S(2)}) async-start(f32[16,32,128]{2,1,0:T(8,128)} %broadcast_in_dim.10), calls=%async_computation | async-start | bytes 524288 | tf_op jit(solution)/shard_map/all_to_all | solution.py:18
  25.2 13.3 %all-to-all-start.1 = ((f32[16,32,128]{2,1,0:T(8,128)}), f32[16,32,128]{2,1,0:T(8,128)S(1)}, u32[]{:S(2)}, u32[]{:S(2)}) async-start(f32[16,32,128]{2,1,0:T(8,128)} %broadcast_in_dim.11), calls=%async_computation.1 | async-start | bytes 524288 | tf_op jit(solution)/shard_map/all_to_all | solution.py:18
  42.9 14.1 %all-to-all-start.2 = ((f32[16,32,128]{2,1,0:T(8,128)}), f32[16,32,128]{2,1,0:T(8,128)S(1)}, u32[]{:S(2)}, u32[]{:S(2)}) async-start(f32[16,32,128]{2,1,0:T(8,128)} %broadcast_in_dim.12), calls=%async_computation.2 | async-start | bytes 524288 | tf_op jit(solution)/shard_map/all_to_all | solution.py:18
  60.6 30.0 %copy-start.1 = (f32[8,1,128,32]{2,3,1,0:T(8,128)S(1)}, f32[8,1,128,32]{2,3,1,0:T(8,128)}, u32[]{:S(2)}) copy-start(f32[8,1,128,32]{2,3,1,0:T(8,128)} %param.6) | copy-start | bytes 393220
  100.7 15.6 %copy-start = (f32[8,32,128]{2,1,0:T(8,128)}, f32[8,32,128]{2,1,0:T(8,128)S(1)}, u32[]{:S(2)}) copy-start(f32[8,32,128]{2,1,0:T(8,128)S(1)} %fusion.43) | copy-start | bytes 393220
  101.4 14.3 %all-to-all-start.4 = ((f32[8,2,8,128]{3,2,1,0:T(8,128)}), f32[8,2,8,128]{3,2,1,0:T(8,128)S(1)}, u32[]{:S(2)}, u32[]{:S(2)}) async-start(f32[8,2,8,128]{3,2,1,0:T(8,128)} %broadcast_in_dim.14), calls=%async_computation.4 | async-start | bytes 131072 | tf_op jit(solution)/shard_map/all_to_all | solution.py:18

commit v2 on v1

v2 whole, which is shorter than its diff:
```python
import jax
import jax.numpy as jnp
from jax import lax
from jax.experimental import pallas as pl
from jax.experimental.pallas import tpu as pltpu
from jax.sharding import Mesh, PartitionSpec as P

highest = lax.Precision.HIGHEST
f32 = jnp.float32
bf16 = jnp.bfloat16
AXES = ("xh", "xl", "zh", "zl", "y", "core")
SIZES = (2, 2, 2, 4, 4, 2)
ROWS = AXES[:4]
OWNERS = AXES[1:4]
MEM = AXES[4:]
TILES = 4
STEPS = 4
WIDTH = 512
ROW = 128
NT = (((1,), (1,)), ((), ()))
NN = (((1,), (0,)), ((), ()))


def dot32(left, right, dims):
    return lax.dot_general(left, right, dims, precision=highest, preferred_element_type=f32)


def split(value):
    high = value.astype(bf16)
    return high, (value - high.astype(f32)).astype(bf16)


def dot16(left, right, dims):
    return lax.dot_general(left, right, dims, preferred_element_type=f32)


def joined(ref, step):
    return jnp.concatenate([ref[step * TILES + i] for i in range(TILES)], axis=1)


def prepare_body(count_ref, panel_ref, inverses_ref, factor_ref, panel_high_ref,
                 panel_low_ref, inverse_high_ref, inverse_low_ref):
    for block in range(panel_ref.shape[0]):
        panel_high_ref[block], panel_low_ref[block] = split(panel_ref[block])
    for step in range(STEPS):
        inverse_high_ref[step], inverse_low_ref[step] = split(inverses_ref[step])
    for step in range(STEPS - 1):
        part = panel_ref[0, :, step * WIDTH:(step + 1) * WIDTH]
        part = jnp.where(count_ref[0] > step, part, 0.0)
        factor_ref[step] = dot32(part, inverses_ref[step], NN)


def round_body(step, tiles_ref, own_ref, factor_ref, copies_ref, own_out_ref):
    change = dot32(joined(tiles_ref, step), factor_ref[step], NT)
    own = own_ref[...] - change
    own_out_ref[...] = own
    for i in range(copies_ref.shape[0]):
        copies_ref[i] = own


def times_split(value, high_ref, low_ref, at):
    rows = value.shape[0]
    high, low = split(value)
    wide = dot16(jnp.concatenate([high, low], axis=0), high_ref[at], NT)
    return wide[:rows] + wide[rows:] + dot16(high, low_ref[at], NT)


def finish_body(count_ref, tiles_ref, own_ref, right_ref, panel_high_ref, panel_low_ref,
                inverse_high_ref, inverse_low_ref, solved_ref, left_ref, sums_ref):
    parts = []
    for step in range(STEPS):
        solved = times_split(joined(tiles_ref, step), inverse_high_ref, inverse_low_ref, step)
        solved_ref[:, step * WIDTH:(step + 1) * WIDTH] = solved
        parts.append(solved)
    solved = jnp.concatenate(parts, axis=1)
    for block in range(right_ref.shape[0]):
        left = right_ref[block] - times_split(solved, panel_high_ref, panel_low_ref, block)
        if block == 0:
            left = jnp.where(count_ref[0] >= 0, own_ref[...], left)
        left_ref[block] = left
        total = jnp.sum(left, axis=0, keepdims=True)
        square = jnp.sum(left * left, axis=0, keepdims=True)
        for i in range(8):
            sums_ref[i, 0, block:block + 1] = total
            sums_ref[i, 1, block:block + 1] = square


VMEM = pl.BlockSpec(memory_space=pltpu.VMEM)
SMEM = pl.BlockSpec(memory_space=pltpu.SMEM)


def shape(*dims):
    return jax.ShapeDtypeStruct(dims, f32)


def params(limit):
    return pltpu.CompilerParams(vmem_limit_bytes=limit << 20)


def cost(flops, size):
    return pl.CostEstimate(flops=flops, bytes_accessed=size, transcendentals=0)


def prepare(count, panel, inverses):
    halves = [jax.ShapeDtypeStruct(panel.shape, bf16)] * 2
    halves += [jax.ShapeDtypeStruct(inverses.shape, bf16)] * 2
    return pl.pallas_call(
        prepare_body,
        out_shape=[shape(STEPS - 1, ROW, WIDTH)] + halves,
        in_specs=[SMEM, VMEM, VMEM],
        out_specs=[VMEM] * 5,
        compiler_params=params(32),
        cost_estimate=cost(6 * 3 * 2 * ROW * WIDTH * WIDTH, 24 << 20),
        name="prepare",
    )(count, panel, inverses)


def advance(step, copies, tiles, own, factor):
    members = own.shape[0]
    return pl.pallas_call(
        lambda *refs: round_body(step, *refs),
        out_shape=(shape(copies, members, ROW), shape(members, ROW)),
        in_specs=[VMEM] * 3,
        out_specs=(VMEM, VMEM),
        compiler_params=params(8),
        name=f"advance{step}",
    )(tiles, own, factor)


def finish(count, tiles, own, right, halves):
    blocks, members, rows = right.shape
    return pl.pallas_call(
        finish_body,
        out_shape=(shape(members, STEPS * WIDTH), shape(blocks, members, rows),
                   shape(8, 2, blocks, rows)),
        in_specs=[SMEM] + [VMEM] * 7,
        out_specs=(VMEM, VMEM, VMEM),
        compiler_params=params(24),
        name="finish",
    )(count, tiles, own, right, *halves)


def shards(factor_panel, right_side, inverses):
    blocks, _, rows, columns = factor_panel.shape
    members = right_side.shape[3]
    panel = factor_panel.reshape(blocks, rows, columns)
    right = right_side.reshape(blocks, rows, members).transpose(0, 2, 1)
    step_of = lax.axis_index(ROWS) // TILES
    count = jnp.where(step_of < STEPS, step_of, -1).astype(jnp.int32).reshape(1)

    own = right[0]
    copies = jnp.broadcast_to(own[None], (16,) + own.shape)
    factor, *halves = prepare(count, panel, inverses)
    for step in range(STEPS - 1):
        tiles = lax.all_to_all(copies, OWNERS, 0, 0)
        copies, own = advance(step, 16 if step < STEPS - 2 else 32, tiles, own, factor)
    tiles = lax.all_to_all(copies, ROWS, 0, 0)
    solved, left, sums = finish(count, tiles, own, right, halves)
    sums = jnp.sum(lax.all_to_all(sums, MEM, 0, 0), axis=0)
    size = members * 8
    mean = sums[0] / size
    spread = sums[1] / size - mean * mean
    return (
        solved.T,
        left.transpose(0, 2, 1).reshape(right_side.shape),
        spread.reshape(blocks, 1, rows),
    )


def solution(mesh):
    fine = Mesh(mesh.devices.reshape(SIZES), AXES)
    return jax.shard_map(
        shards,
        mesh=fine,
        in_specs=(P(None, ROWS, None, None), P(None, ROWS, None, MEM), P()),
        out_specs=(P(None, MEM), P(None, ROWS, None, MEM), P(None, ROWS, None)),
        check_vma=False,
    )
```

time: 117 us -> 103 us (0.88)
  blocking collectives: 20.4 us -> 63.6 us
  matrix products: 29.8 us -> 0 us
  waiting for transfers between devices: 28.7 us -> 0.01 us
  starting transfers between devices: 31.1 us -> 10 us
  Pallas kernels: 0 us -> 14.5 us
  local copies, waits for them, and re-layouts: 4.05 us -> 12.7 us
    all_to_all x1 -> x4, blocking collectives: 20.4 us -> 63.6 us  [the longest x2 29.2 us: shards(): tiles = lax.all_to_all(copies, OWNERS, 0, 0)]
    dot_general x11 -> x0, matrix products: 29.8 us -> none  [times_rows(): lax.dot_general(left, right, (((1,), (1,)), ((), ())), precision=highest,...]
    all_to_all x4 -> x1, waiting for transfers between devices: 28.7 us -> 0.01 us  [shards(): tiles = lax.all_to_all(copies, OWNERS, 0, 0)]
    all_to_all x4 -> x1, starting transfers between devices: 31.1 us -> 10 us  [shards(): tiles = lax.all_to_all(copies, OWNERS, 0, 0)]
    pallas_call x0 -> x5, Pallas kernels: none -> 14.5 us  [the longest x1 8.57 us: prepare(): pl.pallas_call(prepare_body, out_shape=[shape(STEPS - 1, ROW, WIDTH)] + h...]
    unnamed x4 -> x16, local copies, waits for them, and re-layouts: 0.01 us -> 11.2 us
    broadcast_in_dim x5 -> x2, local copies, waits for them, and re-layouts: 2.86 us -> 1.45 us  [shards(): copies = jnp.broadcast_to(own[None], (16,) + own.shape)]
  transfers between devices with their start and end apart: 4 -> 1, of which waited for: 4 -> 0; matrix products, arithmetic and copies ran while one was open for 1% -> 0% of each run, Pallas kernels for 0% -> 8%
where the time goes in v2:
time: 103 us; the launch traced here: 102 us
  blocking collectives  63.6 us (62%)
  Pallas kernels  14.5 us (14%)
  local copies, waits for them, and re-layouts  12.7 us (12%)
  starting transfers between devices  10 us (10%)
    all_to_all x2, blocking collectives, shards(): tiles = lax.all_to_all(copies, OWNERS, 0, 0)  29.2 us
    all_to_all x1, blocking collectives, shards(): tiles = lax.all_to_all(copies, ROWS, 0, 0)  20.3 us
    all_to_all x1, blocking collectives, shards(): sums = jnp.sum(lax.all_to_all(sums, MEM, 0, 0), axis=0)  14.1 us
    unnamed x16, local copies, waits for them, and re-layouts  11.2 us
    all_to_all x1, starting transfers between devices, shards(): tiles = lax.all_to_all(copies, OWNERS, 0, 0)  10 us
    pallas_call x1, Pallas kernels, prepare(): pl.pallas_call(prepare_body, out_shape=[shape(STEPS - 1, ROW, WIDTH)] + h...  8.57 us
    pallas_call x1, Pallas kernels, finish(): pl.pallas_call(finish_body, out_shape=(shape(members, STEPS * WIDTH), sha...  4.84 us
  transfers between devices with their start and end apart: 1, of which 0 were waited for; matrix products, arithmetic and copies ran while one was open for 0% of the time, Pallas kernels for 8%

profile of v2, /device:TPU:1, one launch (start us, length us, event | category | flops | bytes accessed | tf_op | source)
XLA Modules:
  0.0 102.1 jit_solution(11334331404158630356)
XLA Ops:
  0.6 0.7 slice_bitcast_fusion.refs_1_
  1.4 0.7 broadcast_in_dim.8
  2.1 10.0 %all-to-all-start = ((f32[16,32,128]{2,1,0:T(8,128)}), f32[16,32,128]{2,1,0:T(8,128)S(1)}, u32[]{:S(2)}, u32[]{:S(2)}) async-start(f32[16,32,128]{2,1,0:T(8,128)} %broadcast_in_dim.8), calls=%async_computation | async-start | bytes 524288 | tf_op jit(solution)/shard_map/all_to_all | solution.py:155
  12.2 0.0 copy-start.4
  12.2 2.2 %copy-done.4 = f32[4,512,512]{2,1,0:T(8,128)S(1)} copy-done((f32[4,512,512]{2,1,0:T(8,128)S(1)}, f32[4,512,512]{2,1,0:T(8,128)}, u32[]{:S(2)}) %copy-start.4) | copy-done | bytes 4194328
  14.3 8.6 %prepare.1 = (f32[3,128,512]{2,1,0:T(8,128)S(1)}, bf16[8,128,2048]{2,1,0:T(8,128)(2,1)S(1)}, bf16[8,128,2048]{2,1,0:T(8,128)(2,1)S(1)}, bf16[4,512,512]{2,1,0:T(8,128)(2,1)S(1)}, bf16[4,512,512]{2,1,0:T(8,128)(2,1)S(1)}) custom-call(s32[1]{0:T(128)} %bitcast.count_ref, f32[8,128,2048]{2,1,0:T(8,128)} %bitcast.16, f32[4,512,512]{2,1,0:T(8,128)S(1)} %copy-done.4), custom_call_target="tpu_custom_call" | custom-call | flops 1207959552 | bytes 25165824 | tf_op jit(solution)/shard_map/prepare/pallas_call | solution.py:107
  22.9 0.0 copy-start
  22.9 1.9 %copy-done = bf16[8,128,2048]{2,1,0:T(8,128)(2,1)} copy-done((bf16[8,128,2048]{2,1,0:T(8,128)(2,1)}, bf16[8,128,2048]{2,1,0:T(8,128)(2,1)S(1)}, u32[]{:S(2)}) %copy-start) | copy-done | bytes 4194328
  24.9 0.0 copy-start.2
  24.9 2.0 %copy-done.2 = bf16[8,128,2048]{2,1,0:T(8,128)(2,1)} copy-done((bf16[8,128,2048]{2,1,0:T(8,128)(2,1)}, bf16[8,128,2048]{2,1,0:T(8,128)(2,1)S(1)}, u32[]{:S(2)}) %copy-start.2) | copy-done | bytes 4194328
  26.8 0.0 copy-start.5
  26.8 1.4 %copy-done.5 = bf16[4,512,512]{2,1,0:T(8,128)(2,1)} copy-done((bf16[4,512,512]{2,1,0:T(8,128)(2,1)}, bf16[4,512,512]{2,1,0:T(8,128)(2,1)S(1)}, u32[]{:S(2)}) %copy-start.5) | copy-done | bytes 2097176
  28.2 0.0 copy-start.7
  28.2 0.0 all-to-all-done.refs_0_
  28.2 0.0 copy-start.1
  28.2 0.4 advance0.1
  28.6 15.5 %all_to_all.25.refs_0_ = f32[16,32,128]{2,1,0:T(8,128)S(1)} all-to-all(f32[16,32,128]{2,1,0:T(8,128)S(1)} %get-tuple-element.18), channel_id=1, replica_groups=mesh['xh'=2,'xl'=2,'zh'=2,'zl'=4,'y'=4,'core'=2] {'xl','zh','zl'}, dimensions={0} | all-to-all | bytes 524288 | tf_op jit(solution)/shard_map/all_to_all | solution.py:155
  44.1 0.4 advance1.1
  44.4 13.7 %all_to_all.26.refs_0_ = f32[16,32,128]{2,1,0:T(8,128)S(1)} all-to-all(f32[16,32,128]{2,1,0:T(8,128)S(1)} %get-tuple-element.20), channel_id=1, replica_groups=mesh['xh'=2,'xl'=2,'zh'=2,'zl'=4,'y'=4,'core'=2] {'xl','zh','zl'}, dimensions={0} | all-to-all | bytes 524288 | tf_op jit(solution)/shard_map/all_to_all | solution.py:155
  58.1 0.4 advance2.1
  58.5 20.3 %all_to_all.27.tiles_ref = f32[32,32,128]{2,1,0:T(8,128)S(1)} all-to-all(f32[32,32,128]{2,1,0:T(8,128)S(1)} %get-tuple-element.22), channel_id=1, replica_groups=mesh['xh'=2,'xl'=2,'zh'=2,'zl'=4,'y'=4,'core'=2] {'xh','xl','zh','zl'}, dimensions={0} | all-to-all | bytes 1048576 | tf_op jit(solution)/shard_map/all_to_all | solution.py:157
  78.8 0.0 copy-done.7
  78.8 0.0 copy-done.1
  78.8 0.0 copy-start.3
  78.8 2.2 %copy-done.3 = bf16[8,128,2048]{2,1,0:T(8,128)(2,1)S(1)} copy-done((bf16[8,128,2048]{2,1,0:T(8,128)(2,1)S(1)}, bf16[8,128,2048]{2,1,0:T(8,128)(2,1)}, u32[]{:S(2)}) %copy-start.3) | copy-done | bytes 4194328
  81.0 0.0 copy-start.6
  81.0 1.6 %copy-done.6 = bf16[4,512,512]{2,1,0:T(8,128)(2,1)S(1)} copy-done((bf16[4,512,512]{2,1,0:T(8,128)(2,1)S(1)}, bf16[4,512,512]{2,1,0:T(8,128)(2,1)}, u32[]{:S(2)}) %copy-start.6) | copy-done | bytes 2097176
  82.6 4.8 %finish.1 = (f32[32,2048]{1,0:T(8,128)}, f32[8,32,128]{2,1,0:T(8,128)}, f32[8,2,8,128]{3,2,1,0:T(8,128)S(1)}) custom-call(s32[1]{0:T(128)} %bitcast.count_ref, f32[32,32,128]{2,1,0:T(8,128)S(1)} %all_to_all.27.tiles_ref, f32[32,128]{1,0:T(8,128)S(1)} %get-tuple-element.23.own_ref, f32[8,32,128]{2,1,0:T(8,128)S(1)} %bitcast.15, ...), custom_call_target="tpu_custom_call" | custom-call | tf_op jit(solution)/shard_map/finish/pallas_call | solution.py:132
  87.4 14.1 %all_to_all.28 = f32[8,2,8,128]{3,2,1,0:T(8,128)S(1)} all-to-all(f32[8,2,8,128]{3,2,1,0:T(8,128)S(1)} %get-tuple-element.30), channel_id=1, replica_groups=mesh['xh'=2,'xl'=2,'zh'=2,'zl'=4,'y'=4,'core'=2] {'y','core'}, dimensions={0} | all-to-all | bytes 131072 | tf_op jit(solution)/shard_map/all_to_all | solution.py:159
  101.6 0.6 fusion.1
  (1 shorter events, 0.0 us)
Async XLA Ops:
  2.1 26.1 %all-to-all-start = ((f32[16,32,128]{2,1,0:T(8,128)}), f32[16,32,128]{2,1,0:T(8,128)S(1)}, u32[]{:S(2)}, u32[]{:S(2)}) async-start(f32[16,32,128]{2,1,0:T(8,128)} %broadcast_in_dim.8), calls=%async_computation | async-start | bytes 524288 | tf_op jit(solution)/shard_map/all_to_all | solution.py:155
  12.2 2.2 %copy-start.4 = (f32[4,512,512]{2,1,0:T(8,128)S(1)}, f32[4,512,512]{2,1,0:T(8,128)}, u32[]{:S(2)}) copy-start(f32[4,512,512]{2,1,0:T(8,128)} %inverses_ref.1) | copy-start | bytes 12582916
  22.9 2.0 %copy-start = (bf16[8,128,2048]{2,1,0:T(8,128)(2,1)}, bf16[8,128,2048]{2,1,0:T(8,128)(2,1)S(1)}, u32[]{:S(2)}) copy-start(bf16[8,128,2048]{2,1,0:T(8,128)(2,1)S(1)} %get-tuple-element.24.panel_high_ref) | copy-start | bytes 12582916
  24.9 2.0 %copy-start.2 = (bf16[8,128,2048]{2,1,0:T(8,128)(2,1)}, bf16[8,128,2048]{2,1,0:T(8,128)(2,1)S(1)}, u32[]{:S(2)}) copy-start(bf16[8,128,2048]{2,1,0:T(8,128)(2,1)S(1)} %get-tuple-element.25.panel_low_ref) | copy-start | bytes 12582916
  26.8 1.4 %copy-start.5 = (bf16[4,512,512]{2,1,0:T(8,128)(2,1)}, bf16[4,512,512]{2,1,0:T(8,128)(2,1)S(1)}, u32[]{:S(2)}) copy-start(bf16[4,512,512]{2,1,0:T(8,128)(2,1)S(1)} %get-tuple-element.27.inverse_low_ref) | copy-start | bytes 6291460
  28.2 50.6 %copy-start.7 = (f32[8,1,128,32]{2,3,1,0:T(8,128)S(1)}, f32[8,1,128,32]{2,3,1,0:T(8,128)}, u32[]{:S(2)}) copy-start(f32[8,1,128,32]{2,3,1,0:T(8,128)} %param.4) | copy-start | bytes 393220
  28.2 50.6 %copy-start.1 = (bf16[8,128,2048]{2,1,0:T(8,128)(2,1)S(1)}, bf16[8,128,2048]{2,1,0:T(8,128)(2,1)}, u32[]{:S(2)}) copy-start(bf16[8,128,2048]{2,1,0:T(8,128)(2,1)} %copy-done) | copy-start | bytes 12582916
  78.8 2.2 %copy-start.3 = (bf16[8,128,2048]{2,1,0:T(8,128)(2,1)S(1)}, bf16[8,128,2048]{2,1,0:T(8,128)(2,1)}, u32[]{:S(2)}) copy-start(bf16[8,128,2048]{2,1,0:T(8,128)(2,1)} %copy-done.2) | copy-start | bytes 12582916
  81.0 1.6 %copy-start.6 = (bf16[4,512,512]{2,1,0:T(8,128)(2,1)S(1)}, bf16[4,512,512]{2,1,0:T(8,128)(2,1)}, u32[]{:S(2)}) copy-start(bf16[4,512,512]{2,1,0:T(8,128)(2,1)} %copy-done.5) | copy-start | bytes 6291460

commit v3 on v2

v3 whole, which is shorter than its diff:
```python
import jax
import jax.numpy as jnp
from jax import lax
from jax.experimental import pallas as pl
from jax.experimental.pallas import tpu as pltpu
from jax.sharding import Mesh, PartitionSpec as P

highest = lax.Precision.HIGHEST
f32 = jnp.float32
bf16 = jnp.bfloat16
AXES = ("xh", "xl", "zh", "zl", "y", "core")
SIZES = (2, 2, 2, 4, 4, 2)
ROWS = AXES[:4]
OWNERS = AXES[1:4]
MEM = AXES[4:]
TILES = 4
STEPS = 4
WIDTH = 512
ROW = 128
NT = (((1,), (1,)), ((), ()))
NN = (((1,), (0,)), ((), ()))


def dot32(left, right, dims):
    return lax.dot_general(left, right, dims, precision=highest, preferred_element_type=f32)


def split(value):
    high = value.astype(bf16)
    return high, (value - high.astype(f32)).astype(bf16)


def dot16(left, right, dims):
    return lax.dot_general(left, right, dims, preferred_element_type=f32)


def joined(ref, step):
    return jnp.concatenate([ref[step * TILES + i] for i in range(TILES)], axis=1)


def times_split(value, right):
    rows = value.shape[0]
    high, low = split(value)
    right_high, right_low = split(right)
    wide = dot16(jnp.concatenate([high, low], axis=0), right_high, NT)
    return wide[:rows] + wide[rows:] + dot16(high, right_low, NT)


def begin_body(right_ref, copies_ref, own_ref):
    own = right_ref[0]
    own_ref[...] = own
    for i in range(copies_ref.shape[0]):
        copies_ref[i] = own


def advance_body(step, count_ref, tiles_ref, own_ref, panel_ref, inverses_ref,
                 copies_ref, own_out_ref):
    solved = dot32(joined(tiles_ref, step), inverses_ref[step], NT)
    change = dot32(solved, panel_ref[0, :, step * WIDTH:(step + 1) * WIDTH], NT)
    own = jnp.where(count_ref[0] > step, own_ref[...] - change, own_ref[...])
    own_out_ref[...] = own
    for i in range(copies_ref.shape[0]):
        copies_ref[i] = own


def finish_body(count_ref, tiles_ref, own_ref, right_ref, panel_ref, inverses_ref,
                solved_ref, left_ref, sums_ref):
    parts = []
    for step in range(STEPS):
        solved = times_split(joined(tiles_ref, step), inverses_ref[step])
        solved_ref[:, step * WIDTH:(step + 1) * WIDTH] = solved
        parts.append(solved)
    solved = jnp.concatenate(parts, axis=1)
    for block in range(right_ref.shape[0]):
        left = right_ref[block] - times_split(solved, panel_ref[block])
        if block == 0:
            left = jnp.where(count_ref[0] >= 0, own_ref[...], left)
        left_ref[block] = left
        total = jnp.sum(left, axis=0, keepdims=True)
        square = jnp.sum(left * left, axis=0, keepdims=True)
        for i in range(8):
            sums_ref[i, 0, block:block + 1] = total
            sums_ref[i, 1, block:block + 1] = square


VMEM = pl.BlockSpec(memory_space=pltpu.VMEM)
SMEM = pl.BlockSpec(memory_space=pltpu.SMEM)


def shape(*dims):
    return jax.ShapeDtypeStruct(dims, f32)


def params(limit):
    return pltpu.CompilerParams(vmem_limit_bytes=limit << 20)


def cost(flops, size):
    return pl.CostEstimate(flops=flops, bytes_accessed=size, transcendentals=0)


def local(body, name, limit, outs, flops, size, *args):
    smem = [SMEM] if args[0].ndim == 1 else []
    return pl.pallas_call(
        body,
        out_shape=outs,
        in_specs=smem + [VMEM] * (len(args) - len(smem)),
        out_specs=[VMEM] * len(outs),
        compiler_params=params(limit),
        cost_estimate=cost(flops, size),
        name=name,
    )(*args)


def shards(factor_panel, right_side, inverses):
    blocks, _, rows, columns = factor_panel.shape
    members = right_side.shape[3]
    panel = factor_panel.reshape(blocks, rows, columns)
    right = right_side.reshape(blocks, rows, members).transpose(0, 2, 1)
    step_of = lax.axis_index(ROWS) // TILES
    count = jnp.where(step_of < STEPS, step_of, -1).astype(jnp.int32).reshape(1)
    tile = shape(members, rows)
    group = shape(16, members, rows)
    every = shape(32, members, rows)

    right, count = lax.optimization_barrier((right, count))
    copies, own = local(begin_body, "begin", 8, [group, tile], 1 << 34, 1 << 20, right)
    for step in range(STEPS - 1):
        last = step == STEPS - 2
        tiles = lax.all_to_all(copies, OWNERS, 0, 0)
        copies, own = local(
            lambda *refs, step=step: advance_body(step, *refs), f"advance{step}", 8,
            [every if last else group, tile], 1 << 28, 2 << 20,
            count, tiles, own, panel, inverses,
        )
    tiles = lax.all_to_all(copies, ROWS, 0, 0)
    solved, left, sums = local(
        finish_body, "finish", 16,
        [shape(members, STEPS * WIDTH), shape(blocks, members, rows), shape(8, 2, blocks, rows)],
        1 << 30, 12 << 20, count, tiles, own, right, panel, inverses,
    )
    sums = jnp.sum(lax.all_to_all(sums, MEM, 0, 0), axis=0)
    size = members * 8
    mean = sums[0] / size
    spread = sums[1] / size - mean * mean
    return (
        solved.T,
        left.transpose(0, 2, 1).reshape(right_side.shape),
        spread.reshape(blocks, 1, rows),
    )


def solution(mesh):
    fine = Mesh(mesh.devices.reshape(SIZES), AXES)
    return jax.shard_map(
        shards,
        mesh=fine,
        in_specs=(P(None, ROWS, None, None), P(None, ROWS, None, MEM), P()),
        out_specs=(P(None, MEM), P(None, ROWS, None, MEM), P(None, ROWS, None)),
        check_vma=False,
    )
```

time: 103 us -> 92.8 us (0.901)
  blocking collectives: 63.6 us -> 80.6 us
  local copies, waits for them, and re-layouts: 12.7 us -> 0.91 us
  starting transfers between devices: 10 us -> 0 us
  Pallas kernels: 14.5 us -> 9.72 us
    all_to_all x2 -> x3, blocking collectives: 29.2 us -> 46.1 us  [shards(): tiles = lax.all_to_all(copies, OWNERS, 0, 0)]
    unnamed x16 -> x8, local copies, waits for them, and re-layouts: 11.2 us -> 0.91 us
    all_to_all x1 -> x0, starting transfers between devices: 10 us -> none  [shards(): tiles = lax.all_to_all(copies, OWNERS, 0, 0)]
    pallas_call x5, Pallas kernels: 14.5 us -> 9.72 us  [local(): pl.pallas_call(body, out_shape=outs, in_specs=smem + [VMEM] * (len(args)...]
    broadcast_in_dim x2 -> x0, local copies, waits for them, and re-layouts: 1.45 us -> none  [shards(): copies = jnp.broadcast_to(own[None], (16,) + own.shape)]
  transfers between devices with their start and end apart: 1 -> 0, of which waited for: 0 -> 0; matrix products, arithmetic and copies ran while one was open for 0% -> 0% of each run, Pallas kernels for 8% -> 0%
where the time goes in v3:
time: 92.8 us; the launch traced here: 92.5 us
  blocking collectives  80.6 us (87%)
  Pallas kernels  9.72 us (10%)
    all_to_all x3, blocking collectives, shards(): tiles = lax.all_to_all(copies, OWNERS, 0, 0)  46.1 us
    all_to_all x1, blocking collectives, shards(): tiles = lax.all_to_all(copies, ROWS, 0, 0)  20.4 us
    all_to_all x1, blocking collectives, shards(): sums = jnp.sum(lax.all_to_all(sums, MEM, 0, 0), axis=0)  14.1 us
    pallas_call x5, Pallas kernels, local(): pl.pallas_call(body, out_shape=outs, in_specs=smem + [VMEM] * (len(args)...  9.72 us

profile of v3, /device:TPU:1, one launch (start us, length us, event | category | flops | bytes accessed | tf_op | source)
XLA Modules:
  0.0 92.5 jit_solution(14038792377206054379)
XLA Ops:
  0.7 0.0 copy-start.2
  0.7 0.9 copy-done.2
  1.6 0.0 copy-start
  1.6 0.0 copy-start.1
  1.6 18.9 %all_to_all.25.refs_1_ = f32[16,32,128]{2,1,0:T(8,128)S(1)} all-to-all(f32[16,32,128]{2,1,0:T(8,128)S(1)} %get-tuple-element.18), channel_id=1, replica_groups=mesh['xh'=2,'xl'=2,'zh'=2,'zl'=4,'y'=4,'core'=2] {'xl','zh','zl'}, dimensions={0} | all-to-all | bytes 524288 | tf_op jit(solution)/shard_map/all_to_all | solution.py:130
  20.5 0.0 copy-done
  20.5 0.0 copy-done.1
  20.5 1.5 %advance0.1 = (f32[16,32,128]{2,1,0:T(8,128)S(1)}, f32[32,128]{1,0:T(8,128)S(1)}) custom-call(s32[1]{0:T(128)} %bitcast.2.refs_0_.count_ref, f32[16,32,128]{2,1,0:T(8,128)S(1)} %all_to_all.25.refs_1_, f32[32,128]{1,0:T(8,128)S(1)} %get-tuple-element.19.refs_2_, f32[8,128,2048]{2,1,0:T(8,128)S(1)} %bitcast.12, f32[4,512,512]{2,1,0:T(8,128)S(1)} %copy-done.1), custom_call_target="tpu_custom_call" | custom-call | flops 268435456 | bytes 2097152 | tf_op jit(solution)/shard_map/advance0/pallas_call | solution.py:104
  22.0 13.1 %all_to_all.26.refs_1_ = f32[16,32,128]{2,1,0:T(8,128)S(1)} all-to-all(f32[16,32,128]{2,1,0:T(8,128)S(1)} %get-tuple-element.20), channel_id=1, replica_groups=mesh['xh'=2,'xl'=2,'zh'=2,'zl'=4,'y'=4,'core'=2] {'xl','zh','zl'}, dimensions={0} | all-to-all | bytes 524288 | tf_op jit(solution)/shard_map/all_to_all | solution.py:130
  35.1 1.5 %advance1.1 = (f32[16,32,128]{2,1,0:T(8,128)S(1)}, f32[32,128]{1,0:T(8,128)S(1)}) custom-call(s32[1]{0:T(128)} %bitcast.2.refs_0_.count_ref, f32[16,32,128]{2,1,0:T(8,128)S(1)} %all_to_all.26.refs_1_, f32[32,128]{1,0:T(8,128)S(1)} %get-tuple-element.21.refs_2_, f32[8,128,2048]{2,1,0:T(8,128)S(1)} %bitcast.13, f32[4,512,512]{2,1,0:T(8,128)S(1)} %copy-done.1), custom_call_target="tpu_custom_call" | custom-call | flops 268435456 | bytes 2097152 | tf_op jit(solution)/shard_map/advance1/pallas_call | solution.py:104
  36.7 0.0 copy-start.3
  36.7 14.1 %all_to_all.27.refs_1_ = f32[16,32,128]{2,1,0:T(8,128)S(1)} all-to-all(f32[16,32,128]{2,1,0:T(8,128)S(1)} %get-tuple-element.22), channel_id=1, replica_groups=mesh['xh'=2,'xl'=2,'zh'=2,'zl'=4,'y'=4,'core'=2] {'xl','zh','zl'}, dimensions={0} | all-to-all | bytes 524288 | tf_op jit(solution)/shard_map/all_to_all | solution.py:130
  50.8 1.6 %advance2.1 = (f32[32,32,128]{2,1,0:T(8,128)S(1)}, f32[32,128]{1,0:T(8,128)S(1)}) custom-call(s32[1]{0:T(128)} %bitcast.2.refs_0_.count_ref, f32[16,32,128]{2,1,0:T(8,128)S(1)} %all_to_all.27.refs_1_, f32[32,128]{1,0:T(8,128)S(1)} %get-tuple-element.23.refs_2_, f32[8,128,2048]{2,1,0:T(8,128)S(1)} %bitcast.14, f32[4,512,512]{2,1,0:T(8,128)S(1)} %copy-done.1), custom_call_target="tpu_custom_call" | custom-call | flops 268435456 | bytes 2097152 | tf_op jit(solution)/shard_map/advance2/pallas_call | solution.py:104
  52.3 20.4 %all_to_all.28.tiles_ref = f32[32,32,128]{2,1,0:T(8,128)S(1)} all-to-all(f32[32,32,128]{2,1,0:T(8,128)S(1)} %get-tuple-element.24), channel_id=1, replica_groups=mesh['xh'=2,'xl'=2,'zh'=2,'zl'=4,'y'=4,'core'=2] {'xh','xl','zh','zl'}, dimensions={0} | all-to-all | bytes 1048576 | tf_op jit(solution)/shard_map/all_to_all | solution.py:136
  72.7 0.0 copy-done.3
  72.7 5.1 %finish.1 = (f32[32,2048]{1,0:T(8,128)}, f32[8,32,128]{2,1,0:T(8,128)}, f32[8,2,8,128]{3,2,1,0:T(8,128)S(1)}) custom-call(s32[1]{0:T(128)} %bitcast.2.refs_0_.count_ref, f32[32,32,128]{2,1,0:T(8,128)S(1)} %all_to_all.28.tiles_ref, f32[32,128]{1,0:T(8,128)S(1)} %get-tuple-element.25.own_ref, f32[8,32,128]{2,1,0:T(8,128)S(1)} %bitcast.17, ...), custom_call_target="tpu_custom_call" | custom-call | flops 1073741824 | bytes 12582912 | tf_op jit(solution)/shard_map/finish/pallas_call | solution.py:104
  77.8 14.1 %all_to_all.29 = f32[8,2,8,128]{3,2,1,0:T(8,128)S(1)} all-to-all(f32[8,2,8,128]{3,2,1,0:T(8,128)S(1)} %get-tuple-element.28), channel_id=1, replica_groups=mesh['xh'=2,'xl'=2,'zh'=2,'zl'=4,'y'=4,'core'=2] {'y','core'}, dimensions={0} | all-to-all | bytes 131072 | tf_op jit(solution)/shard_map/all_to_all | solution.py:142
  91.9 0.6 fusion.1
  (2 shorter events, 0.0 us)
Async XLA Ops:
  0.7 0.9 copy-start.2
  1.6 18.9 %copy-start = (f32[8,1,128,2048]{3,2,1,0:T(8,128)S(1)}, f32[8,1,128,2048]{3,2,1,0:T(8,128)}, u32[]{:S(2)}) copy-start(f32[8,1,128,2048]{3,2,1,0:T(8,128)} %param.3) | copy-start | bytes 25165828
  1.6 18.9 %copy-start.1 = (f32[4,512,512]{2,1,0:T(8,128)S(1)}, f32[4,512,512]{2,1,0:T(8,128)}, u32[]{:S(2)}) copy-start(f32[4,512,512]{2,1,0:T(8,128)} %inverses_ref.1) | copy-start | bytes 12582916
  36.7 36.1 %copy-start.3 = (f32[8,1,128,32]{2,3,1,0:T(8,128)S(1)}, f32[8,1,128,32]{2,3,1,0:T(8,128)}, u32[]{:S(2)}) copy-start(f32[8,1,128,32]{2,3,1,0:T(8,128)} %param.4) | copy-start | bytes 393220

commit v4 on v3

v4 whole, which is shorter than its diff:
```python
import jax
import jax.numpy as jnp
from jax import lax
from jax.experimental import pallas as pl
from jax.experimental.pallas import tpu as pltpu
from jax.sharding import Mesh, PartitionSpec as P

f32 = jnp.float32
bf16 = jnp.bfloat16
AXES = ("xh", "xl", "zh", "zl", "y", "core")
SIZES = (2, 2, 2, 4, 4, 2)
ROWS = AXES[:4]
OWNERS = AXES[1:4]
MEM = AXES[4:]
TILES = 4
STEPS = 4
WIDTH = 512
NT = (((1,), (1,)), ((), ()))
SOURCES = 4
GROUP = (OWNERS, OWNERS, ROWS[2:], ROWS[2:])
NUMBER = (16, 16, 8, 8)
FIRST = (0, 4, 0, 4)


def FINAL(step):
    return step == STEPS - 2


def line_of():
    return jnp.bitwise_xor(lax.axis_index(ROWS[:2]), 1)


def crossings(value):
    return [
        lax.ppermute(value, ROWS[:2], [(i, i ^ change) for i in range(4)])
        for change in (1, 2, 3)
    ]


def split(value):
    high = value.astype(bf16)
    return high, (value - high.astype(f32)).astype(bf16)


def dot16(left, right, dims):
    return lax.dot_general(left, right, dims, preferred_element_type=f32)


def joined(ref, first):
    return jnp.concatenate([ref[first + i] for i in range(TILES)], axis=1)


def times_split(value, right):
    rows = value.shape[0]
    high, low = split(value)
    right_high, right_low = split(right)
    wide = dot16(jnp.concatenate([high, low], axis=0), right_high, NT)
    return wide[:rows] + wide[rows:] + dot16(high, right_low, NT)


def chosen(line, refs, first):
    value = joined(refs[0], first)
    for at, ref in enumerate(refs[1:]):
        value = jnp.where(line == at + 1, joined(ref, first), value)
    return value


def begin_body(right_ref, copies_ref, own_ref):
    own = right_ref[0]
    own_ref[...] = own
    for i in range(copies_ref.shape[0]):
        copies_ref[i] = own


def advance_body(step, count_ref, *refs):
    outs = refs[-3:] if FINAL(step) else refs[-2:]
    *tiles, own_ref, panel_ref, inverses_ref = refs[:-len(outs)]
    solved = times_split(joined(tiles[-1], FIRST[step]), inverses_ref[step])
    change = times_split(solved, panel_ref[0, :, step * WIDTH:(step + 1) * WIDTH])
    own = jnp.where(count_ref[0] > step, own_ref[...] - change, own_ref[...])
    outs[1][...] = own
    for i in range(outs[0].shape[0]):
        outs[0][i] = own
    if FINAL(step):
        for at, ref in enumerate(tiles):
            for i in range(TILES):
                outs[2][at * TILES + i] = ref[FIRST[at] + i]


def middle_body(count_ref, *refs):
    sources = refs[:SOURCES]
    right_ref, panel_ref, inverses_ref = refs[SOURCES:SOURCES + 3]
    solved_ref, left_ref = refs[-2:]
    parts = []
    for step in range(STEPS - 1):
        solved = times_split(chosen(count_ref[1], sources, step * TILES), inverses_ref[step])
        solved_ref[:, step * WIDTH:(step + 1) * WIDTH] = solved
        parts.append(solved)
    solved = jnp.concatenate(parts, axis=1)
    for block in range(right_ref.shape[0]):
        product = times_split(solved, panel_ref[block, :, :(STEPS - 1) * WIDTH])
        left_ref[block] = right_ref[block] - product


def finish_body(count_ref, *refs):
    sources = refs[:SOURCES]
    own_ref, partly_ref, before_ref, panel_ref, inverses_ref = refs[SOURCES:SOURCES + 5]
    solved_ref, left_ref, sums_ref = refs[-3:]
    step = STEPS - 1
    solved = times_split(chosen(count_ref[1], sources, 0), inverses_ref[step])
    solved_ref[:, :step * WIDTH] = before_ref[...]
    solved_ref[:, step * WIDTH:] = solved
    for block in range(partly_ref.shape[0]):
        product = times_split(solved, panel_ref[block, :, step * WIDTH:])
        left = partly_ref[block] - product
        if block == 0:
            left = jnp.where(count_ref[0] >= 0, own_ref[...], left)
        left_ref[block] = left
        total = jnp.sum(left, axis=0, keepdims=True)
        square = jnp.sum(left * left, axis=0, keepdims=True)
        for i in range(8):
            sums_ref[i, 0, block:block + 1] = total
            sums_ref[i, 1, block:block + 1] = square


VMEM = pl.BlockSpec(memory_space=pltpu.VMEM)
SMEM = pl.BlockSpec(memory_space=pltpu.SMEM)


def shape(*dims):
    return jax.ShapeDtypeStruct(dims, f32)


def params(limit):
    return pltpu.CompilerParams(vmem_limit_bytes=limit << 20)


def cost(flops, size):
    return pl.CostEstimate(flops=flops, bytes_accessed=size, transcendentals=0)


def local(body, limit, outs, flops, size, *args):
    smem = [SMEM] if args[0].ndim == 1 else []
    return pl.pallas_call(
        body,
        out_shape=outs,
        in_specs=smem + [VMEM] * (len(args) - len(smem)),
        out_specs=[VMEM] * len(outs),
        compiler_params=params(limit),
        cost_estimate=cost(flops, size),
    )(*args)


def shards(factor_panel, right_side, inverses):
    blocks, _, rows, columns = factor_panel.shape
    members = right_side.shape[3]
    panel = factor_panel.reshape(blocks, rows, columns)
    right = right_side.reshape(blocks, rows, members).transpose(0, 2, 1)
    step_of = lax.axis_index(ROWS) // TILES
    count = jnp.stack([jnp.where(step_of < STEPS, step_of, -1), line_of()]).astype(jnp.int32)
    tile = shape(members, rows)
    right, count = lax.optimization_barrier((right, count))

    copies, own = local(
        begin_body, 8, [shape(NUMBER[0], members, rows), tile], 1 << 34, 1 << 20, right
    )
    received = []
    for step in range(STEPS - 1):
        received.append(lax.all_to_all(copies, GROUP[step], 0, 0))
        outs = [shape(NUMBER[step + 1], members, rows), tile]
        tiles = received[-1:]
        if FINAL(step):
            tiles = received
            outs.append(shape(3 * TILES, members, rows))
        copies, own, *packed = local(
            lambda *refs, step=step: advance_body(step, *refs), 8, outs,
            1 << 28, 2 << 20, count, *tiles, own, panel, inverses,
        )
    early = crossings(packed[0])
    received = lax.all_to_all(copies, GROUP[STEPS - 1], 0, 0)
    ends = received[FIRST[STEPS - 1]:FIRST[STEPS - 1] + TILES]
    late = crossings(ends)
    own, ends, *early = lax.optimization_barrier((own, ends, packed[0], *early))
    before, partly = local(
        middle_body, 16,
        [shape(members, (STEPS - 1) * WIDTH), shape(blocks, members, rows)],
        1 << 30, 12 << 20, count, *early, right, panel, inverses,
    )
    solved, left, sums = local(
        finish_body, 16,
        [shape(members, STEPS * WIDTH), shape(blocks, members, rows), shape(8, 2, blocks, rows)],
        1 << 28, 4 << 20, count, ends, *late, own, partly, before, panel, inverses,
    )
    sums = jnp.sum(lax.all_to_all(sums, MEM, 0, 0), axis=0)
    size = members * 8
    mean = sums[0] / size
    spread = sums[1] / size - mean * mean
    return (
        solved.T,
        left.transpose(0, 2, 1).reshape(right_side.shape),
        spread.reshape(blocks, 1, rows),
    )


def solution(mesh):
    fine = Mesh(mesh.devices.reshape(SIZES), AXES)
    return jax.shard_map(
        shards,
        mesh=fine,
        in_specs=(P(None, ROWS, None, None), P(None, ROWS, None, MEM), P()),
        out_specs=(P(None, MEM), P(None, ROWS, None, MEM), P(None, ROWS, None)),
        check_vma=False,
    )
```

time: 92.8 us -> 97.4 us (1.050)
  blocking collectives: 80.6 us -> 58.5 us
  starting transfers between devices: 0 us -> 11.2 us
  local copies, waits for them, and re-layouts: 0.91 us -> 9.87 us
  waiting for transfers between devices: 0 us -> 5.24 us
  Pallas kernels: 9.72 us -> 10.7 us
    all_to_all x4 -> x3, blocking collectives: 66.5 us -> 45.2 us  [shards(): received.append(lax.all_to_all(copies, GROUP[step], 0, 0))]
    unnamed x8 -> x16, local copies, waits for them, and re-layouts: 0.91 us -> 9.87 us
    ppermute x0 -> x6, starting transfers between devices: none -> 7.8 us  [crossings(): lax.ppermute(value, ROWS[:2], [(i, i ^ change) for i in range(4)])]
    all_to_all x0 -> x1, waiting for transfers between devices: none -> 3.99 us  [shards(): received = lax.all_to_all(copies, GROUP[STEPS - 1], 0, 0)]
    all_to_all x0 -> x1, starting transfers between devices: none -> 3.37 us  [shards(): received = lax.all_to_all(copies, GROUP[STEPS - 1], 0, 0)]
    ppermute x0 -> x6, waiting for transfers between devices: none -> 1.25 us  [crossings(): lax.ppermute(value, ROWS[:2], [(i, i ^ change) for i in range(4)])]
    pallas_call x5 -> x6, Pallas kernels: 9.72 us -> 10.7 us  [local(): pl.pallas_call(body, out_shape=outs, in_specs=smem + [VMEM] * (len(args)...]
  transfers between devices with their start and end apart: 0 -> 7, of which waited for: 0 -> 2; matrix products, arithmetic and copies ran while one was open for 0% -> 0% of each run, Pallas kernels for 0% -> 4%
where the time goes in v4:
time: 97.4 us; the launch traced here: 97 us
  blocking collectives  58.5 us (60%)
  starting transfers between devices  11.2 us (11%)
  Pallas kernels  10.7 us (11%)
  local copies, waits for them, and re-layouts  9.87 us (10%)
  waiting for transfers between devices  5.24 us (5%)
    all_to_all x3, blocking collectives, shards(): received.append(lax.all_to_all(copies, GROUP[step], 0, 0))  45.2 us
    all_to_all x1, blocking collectives, shards(): sums = jnp.sum(lax.all_to_all(sums, MEM, 0, 0), axis=0)  13.4 us
    pallas_call x6, Pallas kernels, local(): pl.pallas_call(body, out_shape=outs, in_specs=smem + [VMEM] * (len(args)...  10.7 us
    unnamed x16, local copies, waits for them, and re-layouts  9.87 us
    ppermute x6, starting transfers between devices, crossings(): lax.ppermute(value, ROWS[:2], [(i, i ^ change) for i in range(4)])  7.8 us
    all_to_all x1, waiting for transfers between devices, shards(): received = lax.all_to_all(copies, GROUP[STEPS - 1], 0, 0)  3.99 us
    all_to_all x1, starting transfers between devices, shards(): received = lax.all_to_all(copies, GROUP[STEPS - 1], 0, 0)  3.37 us
  transfers between devices with their start and end apart: 7, of which 2 were waited for; matrix products, arithmetic and copies ran while one was open for 0% of the time, Pallas kernels for 4%

profile of v4, /device:TPU:1, one launch (start us, length us, event | category | flops | bytes accessed | tf_op | source)
XLA Modules:
  0.0 97.0 jit_solution(2182416167398637062)
XLA Ops:
  0.7 0.1 pad_add_fusion.refs_0_.count_ref
  0.7 0.0 copy-start.6
  0.7 0.9 copy-done.6
  1.6 0.0 copy-start
  1.6 0.0 copy-start.3
  1.7 18.9 %all_to_all.25.refs_1_ = f32[16,32,128]{2,1,0:T(8,128)S(1)} all-to-all(f32[16,32,128]{2,1,0:T(8,128)S(1)} %get-tuple-element.27), channel_id=1, replica_groups=mesh['xh'=2,'xl'=2,'zh'=2,'zl'=4,'y'=4,'core'=2] {'xl','zh','zl'}, dimensions={0} | all-to-all | bytes 524288 | tf_op jit(solution)/shard_map/all_to_all | solution.py:169
  20.5 0.0 copy-done
  20.5 0.0 copy-done.3
  20.6 1.2 %shard_map.59 = (f32[16,32,128]{2,1,0:T(8,128)S(1)}, f32[32,128]{1,0:T(8,128)S(1)}) custom-call(s32[2]{0:T(128)S(1)} %pad_add_fusion.refs_0_.count_ref, f32[16,32,128]{2,1,0:T(8,128)S(1)} %all_to_all.25.refs_1_, f32[32,128]{1,0:T(8,128)S(1)} %get-tuple-element.28.refs_2_, f32[8,128,2048]{2,1,0:T(8,128)S(1)} %bitcast.13, f32[4,512,512]{2,1,0:T(8,128)S(1)} %copy-done.3), custom_call_target="tpu_custom_call" | custom-call | flops 268435456 | bytes 2097152 | tf_op jit(solution)/shard_map/pallas_call | solution.py:144
  21.8 13.1 %all_to_all.26.refs_1_.refs_2_ = f32[16,32,128]{2,1,0:T(8,128)S(1)} all-to-all(f32[16,32,128]{2,1,0:T(8,128)S(1)} %get-tuple-element.29), channel_id=1, replica_groups=mesh['xh'=2,'xl'=2,'zh'=2,'zl'=4,'y'=4,'core'=2] {'xl','zh','zl'}, dimensions={0} | all-to-all | bytes 524288 | tf_op jit(solution)/shard_map/all_to_all | solution.py:169
  34.9 1.2 %shard_map.60 = (f32[8,32,128]{2,1,0:T(8,128)S(1)}, f32[32,128]{1,0:T(8,128)S(1)}) custom-call(s32[2]{0:T(128)S(1)} %pad_add_fusion.refs_0_.count_ref, f32[16,32,128]{2,1,0:T(8,128)S(1)} %all_to_all.26.refs_1_.refs_2_, f32[32,128]{1,0:T(8,128)S(1)} %get-tuple-element.30.refs_2_, f32[8,128,2048]{2,1,0:T(8,128)S(1)} %bitcast.14, f32[4,512,512]{2,1,0:T(8,128)S(1)} %copy-done.3), custom_call_target="tpu_custom_call" | custom-call | flops 268435456 | bytes 2097152 | tf_op jit(solution)/shard_map/pallas_call | solution.py:144
  36.2 0.0 copy-start.7
  36.2 13.2 %all_to_all.27.refs_3_ = f32[8,32,128]{2,1,0:T(8,128)S(1)} all-to-all(f32[8,32,128]{2,1,0:T(8,128)S(1)} %get-tuple-element.31), channel_id=1, replica_groups=mesh['xh'=2,'xl'=2,'zh'=2,'zl'=4,'y'=4,'core'=2] {'zh','zl'}, dimensions={0} | all-to-all | bytes 262144 | tf_op jit(solution)/shard_map/all_to_all | solution.py:169
  49.3 1.9 %shard_map.61 = (f32[8,32,128]{2,1,0:T(8,128)}, f32[32,128]{1,0:T(8,128)S(1)}, f32[12,32,128]{2,1,0:T(8,128)S(1)}) custom-call(s32[2]{0:T(128)S(1)} %pad_add_fusion.refs_0_.count_ref, f32[16,32,128]{2,1,0:T(8,128)S(1)} %all_to_all.25.refs_1_, f32[16,32,128]{2,1,0:T(8,128)S(1)} %all_to_all.26.refs_1_.refs_2_, f32[8,32,128]{2,1,0:T(8,128)S(1)} %all_to_all.27.refs_3_, ...), custom_call_target="tpu_custom_call" | custom-call | flops 268435456 | bytes 2097152 | tf_op jit(solution)/shard_map/pallas_call | solution.py:144
  51.2 3.4 %all-to-all-start.3 = ((f32[8,32,128]{2,1,0:T(8,128)}), f32[8,32,128]{2,1,0:T(8,128)S(1)}, u32[]{:S(2)}, u32[]{:S(2)}) async-start(f32[8,32,128]{2,1,0:T(8,128)} %get-tuple-element.34), calls=%async_computation.3 | async-start | bytes 262144 | tf_op jit(solution)/shard_map/all_to_all | solution.py:180
  54.6 1.3 %collective-permute-start = (f32[12,32,128]{2,1,0:T(8,128)S(1)}, f32[12,32,128]{2,1,0:T(8,128)S(1)}, u32[]{:S(2)}, u32[]{:S(2)}) collective-permute-start(f32[12,32,128]{2,1,0:T(8,128)S(1)} %get-tuple-element.38.refs_0_), channel_id=1, source_target_pairs={{0,64},{64,0},{128,192},{192,128},{1,65},{65,1},{129,193},{193,129... | collective-permute-start | bytes 589832 | tf_op jit(solution)/shard_map/ppermute | solution.py:35
  55.9 2.5 %collective-permute-start.1 = (f32[12,32,128]{2,1,0:T(8,128)S(1)}, f32[12,32,128]{2,1,0:T(8,128)S(1)}, u32[]{:S(2)}, u32[]{:S(2)}) collective-permute-start(f32[12,32,128]{2,1,0:T(8,128)S(1)} %get-tuple-element.38.refs_0_), channel_id=1, source_target_pairs={{0,128},{64,192},{128,0},{192,64},{1,129},{65,193},{129,1},{193,65... | collective-permute-start | bytes 589832 | tf_op jit(solution)/shard_map/ppermute | solution.py:35
  58.3 0.2 collective-permute-start.2
  58.6 4.0 %all-to-all-done.3 = f32[8,32,128]{2,1,0:T(8,128)S(1)} async-done(((f32[8,32,128]{2,1,0:T(8,128)}), f32[8,32,128]{2,1,0:T(8,128)S(1)}, u32[]{:S(2)}, u32[]{:S(2)}) %all-to-all-start.3) | async-done | bytes 131104 | tf_op jit(solution)/shard_map/all_to_all | solution.py:180
  62.5 1.2 %collective-permute-start.3 = (f32[4,32,128]{2,1,0:T(8,128)S(1)}, f32[4,32,128]{2,1,0:T(8,128)S(1)}, u32[]{:S(2)}, u32[]{:S(2)}) collective-permute-start(f32[4,32,128]{2,1,0:T(8,128)S(1)} %slice.12.refs_0_), channel_id=1, source_target_pairs={{0,64},{64,0},{128,192},{192,128},{1,65},{65,1},{129,193},{193,129... | collective-permute-start | bytes 196616 | tf_op jit(solution)/shard_map/ppermute | solution.py:35
  63.7 2.5 %collective-permute-start.4 = (f32[4,32,128]{2,1,0:T(8,128)S(1)}, f32[4,32,128]{2,1,0:T(8,128)S(1)}, u32[]{:S(2)}, u32[]{:S(2)}) collective-permute-start(f32[4,32,128]{2,1,0:T(8,128)S(1)} %slice.12.refs_0_), channel_id=1, source_target_pairs={{0,128},{64,192},{128,0},{192,64},{1,129},{65,193},{129,1},{193,65... | collective-permute-start | bytes 196616 | tf_op jit(solution)/shard_map/ppermute | solution.py:35
  66.2 0.0 collective-permute-done.refs_1_
  66.2 0.2 collective-permute-start.5
  66.4 0.0 collective-permute-done.1.refs_2_
  66.4 1.2 %collective-permute-done.2.refs_3_ = f32[12,32,128]{2,1,0:T(8,128)S(1)} collective-permute-done((f32[12,32,128]{2,1,0:T(8,128)S(1)}, f32[12,32,128]{2,1,0:T(8,128)S(1)}, u32[]{:S(2)}, u32[]{:S(2)}) %collective-permute-start.2) | collective-permute-done | bytes 196640 | tf_op jit(solution)/shard_map/ppermute | solution.py:35
  67.6 0.0 copy-done.7
  67.6 0.0 copy-start.1
  67.7 3.4 %copy-done.1 = f32[8,1,128,2048]{3,2,1,0:T(8,128)S(1)} copy-done((f32[8,1,128,2048]{3,2,1,0:T(8,128)S(1)}, f32[8,1,128,2048]{3,2,1,0:T(8,128)}, u32[]{:S(2)}) %copy-start.1) | copy-done | bytes 8388632
  71.0 0.0 copy-start.4
  71.0 2.2 %copy-done.4 = f32[4,512,512]{2,1,0:T(8,128)S(1)} copy-done((f32[4,512,512]{2,1,0:T(8,128)S(1)}, f32[4,512,512]{2,1,0:T(8,128)}, u32[]{:S(2)}) %copy-start.4) | copy-done | bytes 4194328
  73.2 0.0 copy-start.5
  73.2 3.9 %shard_map.62 = (f32[32,1536]{1,0:T(8,128)S(1)}, f32[8,32,128]{2,1,0:T(8,128)S(1)}) custom-call(s32[2]{0:T(128)S(1)} %pad_add_fusion.refs_0_.count_ref, f32[12,32,128]{2,1,0:T(8,128)S(1)} %get-tuple-element.38.refs_0_, f32[12,32,128]{2,1,0:T(8,128)S(1)} %collective-permute-done.refs_1_, f32[12,32,128]{2,1,0:T(8,128)S(1)} %collective-permute-done.1.refs_2_, ...), custom_call_target="tpu_custom_call" | custom-call | flops 1073741824 | bytes 12582912 | tf_op jit(solution)/shard_map/pallas_call | solution.py:144
  77.1 0.0 collective-permute-done.3.refs_1_
  77.1 0.0 collective-permute-done.4.refs_2_
  77.1 0.0 collective-permute-done.5.refs_3_
  77.2 0.0 copy-done.5
  77.2 0.0 copy-start.2
  77.2 3.4 %copy-done.2 = f32[8,1,128,2048]{3,2,1,0:T(8,128)S(1)} copy-done((f32[8,1,128,2048]{3,2,1,0:T(8,128)S(1)}, f32[8,1,128,2048]{3,2,1,0:T(8,128)}, u32[]{:S(2)}) %copy-start.2) | copy-done | bytes 8388632
  80.5 2.4 %shard_map.63 = (f32[32,2048]{1,0:T(8,128)}, f32[8,32,128]{2,1,0:T(8,128)}, f32[8,2,8,128]{3,2,1,0:T(8,128)S(1)}) custom-call(s32[2]{0:T(128)S(1)} %pad_add_fusion.refs_0_.count_ref, f32[4,32,128]{2,1,0:T(8,128)S(1)} %slice.12.refs_0_, f32[4,32,128]{2,1,0:T(8,128)S(1)} %collective-permute-done.3.refs_1_, f32[4,32,128]{2,1,0:T(8,128)S(1)} %collective-permute-done.4.refs_2_, ...), custom_call_target="tpu_custom_call" | custom-call | flops 268435456 | bytes 4194304 | tf_op jit(solution)/shard_map/pallas_call | solution.py:144
  83.0 13.4 %all_to_all.28 = f32[8,2,8,128]{3,2,1,0:T(8,128)S(1)} all-to-all(f32[8,2,8,128]{3,2,1,0:T(8,128)S(1)} %get-tuple-element.46), channel_id=1, replica_groups=mesh['xh'=2,'xl'=2,'zh'=2,'zl'=4,'y'=4,'core'=2] {'y','core'}, dimensions={0} | all-to-all | bytes 131072 | tf_op jit(solution)/shard_map/all_to_all | solution.py:194
  96.4 0.6 fusion.1
  (3 shorter events, 0.0 us)
Async XLA Ops:
  0.7 0.9 copy-start.6
  1.6 18.9 %copy-start = (f32[8,1,128,2048]{3,2,1,0:T(8,128)S(1)}, f32[8,1,128,2048]{3,2,1,0:T(8,128)}, u32[]{:S(2)}) copy-start(f32[8,1,128,2048]{3,2,1,0:T(8,128)} %param.3) | copy-start | bytes 25165828
  1.6 18.9 %copy-start.3 = (f32[4,512,512]{2,1,0:T(8,128)S(1)}, f32[4,512,512]{2,1,0:T(8,128)}, u32[]{:S(2)}) copy-start(f32[4,512,512]{2,1,0:T(8,128)} %refs_8_.1) | copy-start | bytes 12582916
  36.2 31.5 %copy-start.7 = (f32[8,1,128,32]{2,3,1,0:T(8,128)S(1)}, f32[8,1,128,32]{2,3,1,0:T(8,128)}, u32[]{:S(2)}) copy-start(f32[8,1,128,32]{2,3,1,0:T(8,128)} %param.4) | copy-start | bytes 393220
  51.2 11.3 %all-to-all-start.3 = ((f32[8,32,128]{2,1,0:T(8,128)}), f32[8,32,128]{2,1,0:T(8,128)S(1)}, u32[]{:S(2)}, u32[]{:S(2)}) async-start(f32[8,32,128]{2,1,0:T(8,128)} %get-tuple-element.34), calls=%async_computation.3 | async-start | bytes 262144 | tf_op jit(solution)/shard_map/all_to_all | solution.py:180
  54.6 11.6 %collective-permute-start = (f32[12,32,128]{2,1,0:T(8,128)S(1)}, f32[12,32,128]{2,1,0:T(8,128)S(1)}, u32[]{:S(2)}, u32[]{:S(2)}) collective-permute-start(f32[12,32,128]{2,1,0:T(8,128)S(1)} %get-tuple-element.38.refs_0_), channel_id=1, source_target_pairs={{0,64},{64,0},{128,192},{192,128},{1,65},{65,1},{129,193},{193,129... | collective-permute-start | bytes 589832 | tf_op jit(solution)/shard_map/ppermute | solution.py:35
  55.9 10.5 %collective-permute-start.1 = (f32[12,32,128]{2,1,0:T(8,128)S(1)}, f32[12,32,128]{2,1,0:T(8,128)S(1)}, u32[]{:S(2)}, u32[]{:S(2)}) collective-permute-start(f32[12,32,128]{2,1,0:T(8,128)S(1)} %get-tuple-element.38.refs_0_), channel_id=1, source_target_pairs={{0,128},{64,192},{128,0},{192,64},{1,129},{65,193},{129,1},{193,65... | collective-permute-start | bytes 589832 | tf_op jit(solution)/shard_map/ppermute | solution.py:35
  58.3 9.3 %collective-permute-start.2 = (f32[12,32,128]{2,1,0:T(8,128)S(1)}, f32[12,32,128]{2,1,0:T(8,128)S(1)}, u32[]{:S(2)}, u32[]{:S(2)}) collective-permute-start(f32[12,32,128]{2,1,0:T(8,128)S(1)} %get-tuple-element.38.refs_0_), channel_id=1, source_target_pairs={{0,192},{64,128},{128,64},{192,0},{1,193},{65,129},{129,65},{193,1... | collective-permute-start | bytes 589832 | tf_op jit(solution)/shard_map/ppermute | solution.py:35
  62.5 14.6 %collective-permute-start.3 = (f32[4,32,128]{2,1,0:T(8,128)S(1)}, f32[4,32,128]{2,1,0:T(8,128)S(1)}, u32[]{:S(2)}, u32[]{:S(2)}) collective-permute-start(f32[4,32,128]{2,1,0:T(8,128)S(1)} %slice.12.refs_0_), channel_id=1, source_target_pairs={{0,64},{64,0},{128,192},{192,128},{1,65},{65,1},{129,193},{193,129... | collective-permute-start | bytes 196616 | tf_op jit(solution)/shard_map/ppermute | solution.py:35
  63.7 13.4 %collective-permute-start.4 = (f32[4,32,128]{2,1,0:T(8,128)S(1)}, f32[4,32,128]{2,1,0:T(8,128)S(1)}, u32[]{:S(2)}, u32[]{:S(2)}) collective-permute-start(f32[4,32,128]{2,1,0:T(8,128)S(1)} %slice.12.refs_0_), channel_id=1, source_target_pairs={{0,128},{64,192},{128,0},{192,64},{1,129},{65,193},{129,1},{193,65... | collective-permute-start | bytes 196616 | tf_op jit(solution)/shard_map/ppermute | solution.py:35
  66.2 11.0 %collective-permute-start.5 = (f32[4,32,128]{2,1,0:T(8,128)S(1)}, f32[4,32,128]{2,1,0:T(8,128)S(1)}, u32[]{:S(2)}, u32[]{:S(2)}) collective-permute-start(f32[4,32,128]{2,1,0:T(8,128)S(1)} %slice.12.refs_0_), channel_id=1, source_target_pairs={{0,192},{64,128},{128,64},{192,0},{1,193},{65,129},{129,65},{193,1... | collective-permute-start | bytes 196616 | tf_op jit(solution)/shard_map/ppermute | solution.py:35
  67.6 3.4 %copy-start.1 = (f32[8,1,128,2048]{3,2,1,0:T(8,128)S(1)}, f32[8,1,128,2048]{3,2,1,0:T(8,128)}, u32[]{:S(2)}) copy-start(f32[8,1,128,2048]{3,2,1,0:T(8,128)} %param.3) | copy-start | bytes 25165828
  71.0 2.2 %copy-start.4 = (f32[4,512,512]{2,1,0:T(8,128)S(1)}, f32[4,512,512]{2,1,0:T(8,128)}, u32[]{:S(2)}) copy-start(f32[4,512,512]{2,1,0:T(8,128)} %refs_8_.1) | copy-start | bytes 12582916
  73.2 3.9 %copy-start.5 = (f32[4,512,512]{2,1,0:T(8,128)S(1)}, f32[4,512,512]{2,1,0:T(8,128)}, u32[]{:S(2)}) copy-start(f32[4,512,512]{2,1,0:T(8,128)} %refs_8_.1) | copy-start | bytes 12582916
  77.2 3.4 %copy-start.2 = (f32[8,1,128,2048]{3,2,1,0:T(8,128)S(1)}, f32[8,1,128,2048]{3,2,1,0:T(8,128)}, u32[]{:S(2)}) copy-start(f32[8,1,128,2048]{3,2,1,0:T(8,128)} %param.3) | copy-start | bytes 25165828

commit v5 on v4

--- a/solution.py
+++ b/solution.py
@@ -16,10 +16,10 @@
 STEPS = 4
 WIDTH = 512
 NT = (((1,), (1,)), ((), ()))
-SOURCES = 4
-GROUP = (OWNERS, OWNERS, ROWS[2:], ROWS[2:])
-NUMBER = (16, 16, 8, 8)
-FIRST = (0, 4, 0, 4)
+SOURCES = 2
+GROUP = (OWNERS,) * STEPS
+NUMBER = (16,) * STEPS
+FIRST = (0, 4, 8, 12)
 
 
 def FINAL(step):
@@ -27,14 +27,11 @@
 
 
 def line_of():
-    return jnp.bitwise_xor(lax.axis_index(ROWS[:2]), 1)
+    return lax.axis_index("xh")
 
 
 def crossings(value):
-    return [
-        lax.ppermute(value, ROWS[:2], [(i, i ^ change) for i in range(4)])
-        for change in (1, 2, 3)
-    ]
+    return [lax.ppermute(value, "xh", [(0, 1), (1, 0)])]
 
 
 def split(value):

time: 97.4 us -> 97.6 us (level)
    ppermute x6 -> x2, starting transfers between devices: 7.8 us -> 4.99 us  [crossings(): return [lax.ppermute(value, 'xh', [(0, 1), (1, 0)])]]
    all_to_all x1, starting transfers between devices: 3.37 us -> 6.08 us  [shards(): received = lax.all_to_all(copies, GROUP[STEPS - 1], 0, 0)]
    all_to_all x1, waiting for transfers between devices: 3.99 us -> 5.36 us  [shards(): received = lax.all_to_all(copies, GROUP[STEPS - 1], 0, 0)]
    ppermute x6 -> x2, waiting for transfers between devices: 1.25 us -> 0.02 us  [crossings(): return [lax.ppermute(value, 'xh', [(0, 1), (1, 0)])]]
  transfers between devices with their start and end apart: 7 -> 3, of which waited for: 2 -> 1; matrix products, arithmetic and copies ran while one was open for 0% -> 0% of each run, Pallas kernels for 4% -> 4%
where the time goes in v5:
time: 97.6 us; the launch traced here: 97.1 us
  blocking collectives  58.7 us (60%)
  starting transfers between devices  11.1 us (11%)
  Pallas kernels  10.8 us (11%)
  local copies, waits for them, and re-layouts  9.87 us (10%)
  waiting for transfers between devices  5.38 us (6%)
    all_to_all x3, blocking collectives, shards(): received.append(lax.all_to_all(copies, GROUP[step], 0, 0))  46.1 us
    all_to_all x1, blocking collectives, shards(): sums = jnp.sum(lax.all_to_all(sums, MEM, 0, 0), axis=0)  12.6 us
    pallas_call x6, Pallas kernels, local(): pl.pallas_call(body, out_shape=outs, in_specs=smem + [VMEM] * (len(args)...  10.8 us
    unnamed x16, local copies, waits for them, and re-layouts  9.87 us
    all_to_all x1, starting transfers between devices, shards(): received = lax.all_to_all(copies, GROUP[STEPS - 1], 0, 0)  6.08 us
    all_to_all x1, waiting for transfers between devices, shards(): received = lax.all_to_all(copies, GROUP[STEPS - 1], 0, 0)  5.36 us
    ppermute x2, starting transfers between devices, crossings(): return [lax.ppermute(value, 'xh', [(0, 1), (1, 0)])]  4.99 us
  transfers between devices with their start and end apart: 3, of which 1 were waited for; matrix products, arithmetic and copies ran while one was open for 0% of the time, Pallas kernels for 4%

profile of v5, /device:TPU:1, one launch (start us, length us, event | category | flops | bytes accessed | tf_op | source)
XLA Modules:
  0.0 97.1 jit_solution(9621362103539748568)
XLA Ops:
  0.7 0.1 pad_add_fusion.refs_0_.count_ref
  0.7 0.0 copy-start.6
  0.7 0.9 copy-done.6
  1.6 0.0 copy-start
  1.6 0.0 copy-start.3
  1.7 18.9 %all_to_all.25.refs_1_ = f32[16,32,128]{2,1,0:T(8,128)S(1)} all-to-all(f32[16,32,128]{2,1,0:T(8,128)S(1)} %get-tuple-element.25), channel_id=1, replica_groups=mesh['xh'=2,'xl'=2,'zh'=2,'zl'=4,'y'=4,'core'=2] {'xl','zh','zl'}, dimensions={0} | all-to-all | bytes 524288 | tf_op jit(solution)/shard_map/all_to_all | solution.py:166
  20.5 0.0 copy-done
  20.5 0.0 copy-done.3
  20.6 1.2 %shard_map.59 = (f32[16,32,128]{2,1,0:T(8,128)S(1)}, f32[32,128]{1,0:T(8,128)S(1)}) custom-call(s32[2]{0:T(128)S(1)} %pad_add_fusion.refs_0_.count_ref, f32[16,32,128]{2,1,0:T(8,128)S(1)} %all_to_all.25.refs_1_, f32[32,128]{1,0:T(8,128)S(1)} %get-tuple-element.26.refs_2_, f32[8,128,2048]{2,1,0:T(8,128)S(1)} %bitcast.13, f32[4,512,512]{2,1,0:T(8,128)S(1)} %copy-done.3), custom_call_target="tpu_custom_call" | custom-call | flops 268435456 | bytes 2097152 | tf_op jit(solution)/shard_map/pallas_call | solution.py:141
  21.8 13.1 %all_to_all.26.refs_1_.refs_2_ = f32[16,32,128]{2,1,0:T(8,128)S(1)} all-to-all(f32[16,32,128]{2,1,0:T(8,128)S(1)} %get-tuple-element.27), channel_id=1, replica_groups=mesh['xh'=2,'xl'=2,'zh'=2,'zl'=4,'y'=4,'core'=2] {'xl','zh','zl'}, dimensions={0} | all-to-all | bytes 524288 | tf_op jit(solution)/shard_map/all_to_all | solution.py:166
  34.9 1.2 %shard_map.60 = (f32[16,32,128]{2,1,0:T(8,128)S(1)}, f32[32,128]{1,0:T(8,128)S(1)}) custom-call(s32[2]{0:T(128)S(1)} %pad_add_fusion.refs_0_.count_ref, f32[16,32,128]{2,1,0:T(8,128)S(1)} %all_to_all.26.refs_1_.refs_2_, f32[32,128]{1,0:T(8,128)S(1)} %get-tuple-element.28.refs_2_, f32[8,128,2048]{2,1,0:T(8,128)S(1)} %bitcast.14, f32[4,512,512]{2,1,0:T(8,128)S(1)} %copy-done.3), custom_call_target="tpu_custom_call" | custom-call | flops 268435456 | bytes 2097152 | tf_op jit(solution)/shard_map/pallas_call | solution.py:141
  36.2 0.0 copy-start.7
  36.2 14.1 %all_to_all.27.refs_3_ = f32[16,32,128]{2,1,0:T(8,128)S(1)} all-to-all(f32[16,32,128]{2,1,0:T(8,128)S(1)} %get-tuple-element.29), channel_id=1, replica_groups=mesh['xh'=2,'xl'=2,'zh'=2,'zl'=4,'y'=4,'core'=2] {'xl','zh','zl'}, dimensions={0} | all-to-all | bytes 524288 | tf_op jit(solution)/shard_map/all_to_all | solution.py:166
  50.2 2.0 %shard_map.61 = (f32[16,32,128]{2,1,0:T(8,128)}, f32[32,128]{1,0:T(8,128)S(1)}, f32[12,32,128]{2,1,0:T(8,128)S(1)}) custom-call(s32[2]{0:T(128)S(1)} %pad_add_fusion.refs_0_.count_ref, f32[16,32,128]{2,1,0:T(8,128)S(1)} %all_to_all.25.refs_1_, f32[16,32,128]{2,1,0:T(8,128)S(1)} %all_to_all.26.refs_1_.refs_2_, f32[16,32,128]{2,1,0:T(8,128)S(1)} %all_to_all.27.refs_3_, ...), custom_call_target="tpu_custom_call" | custom-call | flops 268435456 | bytes 2097152 | tf_op jit(solution)/shard_map/pallas_call | solution.py:141
  52.2 6.1 %all-to-all-start.3 = ((f32[16,32,128]{2,1,0:T(8,128)}), f32[16,32,128]{2,1,0:T(8,128)S(1)}, u32[]{:S(2)}, u32[]{:S(2)}) async-start(f32[16,32,128]{2,1,0:T(8,128)} %get-tuple-element.32), calls=%async_computation.3 | async-start | bytes 524288 | tf_op jit(solution)/shard_map/all_to_all | solution.py:177
  58.3 2.5 %collective-permute-start = (f32[12,32,128]{2,1,0:T(8,128)S(1)}, f32[12,32,128]{2,1,0:T(8,128)S(1)}, u32[]{:S(2)}, u32[]{:S(2)}) collective-permute-start(f32[12,32,128]{2,1,0:T(8,128)S(1)} %get-tuple-element.36.refs_0_), channel_id=1, source_target_pairs={{0,128},{128,0},{1,129},{129,1},{2,130},{130,2},{3,131},{131,3},{4... | collective-permute-start | bytes 589832 | tf_op jit(solution)/shard_map/ppermute | solution.py:34
  60.8 5.4 %all-to-all-done.3 = f32[16,32,128]{2,1,0:T(8,128)S(1)} async-done(((f32[16,32,128]{2,1,0:T(8,128)}), f32[16,32,128]{2,1,0:T(8,128)S(1)}, u32[]{:S(2)}, u32[]{:S(2)}) %all-to-all-start.3) | async-done | bytes 262176 | tf_op jit(solution)/shard_map/all_to_all | solution.py:177
  66.2 2.5 %collective-permute-start.1 = (f32[4,32,128]{2,1,0:T(8,128)S(1)}, f32[4,32,128]{2,1,0:T(8,128)S(1)}, u32[]{:S(2)}, u32[]{:S(2)}) collective-permute-start(f32[4,32,128]{2,1,0:T(8,128)S(1)} %slice.12.refs_0_), channel_id=1, source_target_pairs={{0,128},{128,0},{1,129},{129,1},{2,130},{130,2},{3,131},{131,3},{4... | collective-permute-start | bytes 196616 | tf_op jit(solution)/shard_map/ppermute | solution.py:34
  68.6 0.0 collective-permute-done.refs_1_
  68.6 0.0 copy-done.7
  68.6 0.0 copy-start.1
  68.7 3.4 %copy-done.1 = f32[8,1,128,2048]{3,2,1,0:T(8,128)S(1)} copy-done((f32[8,1,128,2048]{3,2,1,0:T(8,128)S(1)}, f32[8,1,128,2048]{3,2,1,0:T(8,128)}, u32[]{:S(2)}) %copy-start.1) | copy-done | bytes 8388632
  72.0 0.0 copy-start.4
  72.0 2.2 %copy-done.4 = f32[4,512,512]{2,1,0:T(8,128)S(1)} copy-done((f32[4,512,512]{2,1,0:T(8,128)S(1)}, f32[4,512,512]{2,1,0:T(8,128)}, u32[]{:S(2)}) %copy-start.4) | copy-done | bytes 4194328
  74.2 0.0 copy-start.5
  74.2 3.9 %shard_map.62 = (f32[32,1536]{1,0:T(8,128)S(1)}, f32[8,32,128]{2,1,0:T(8,128)S(1)}) custom-call(s32[2]{0:T(128)S(1)} %pad_add_fusion.refs_0_.count_ref, f32[12,32,128]{2,1,0:T(8,128)S(1)} %get-tuple-element.36.refs_0_, f32[12,32,128]{2,1,0:T(8,128)S(1)} %collective-permute-done.refs_1_, f32[8,32,128]{2,1,0:T(8,128)S(1)} %bitcast.19, ...), custom_call_target="tpu_custom_call" | custom-call | flops 1073741824 | bytes 12582912 | tf_op jit(solution)/shard_map/pallas_call | solution.py:141
  78.1 0.0 collective-permute-done.1.refs_1_
  78.1 0.0 copy-done.5
  78.1 0.0 copy-start.2
  78.1 3.4 %copy-done.2 = f32[8,1,128,2048]{3,2,1,0:T(8,128)S(1)} copy-done((f32[8,1,128,2048]{3,2,1,0:T(8,128)S(1)}, f32[8,1,128,2048]{3,2,1,0:T(8,128)}, u32[]{:S(2)}) %copy-start.2) | copy-done | bytes 8388632
  81.5 2.4 %shard_map.63 = (f32[32,2048]{1,0:T(8,128)}, f32[8,32,128]{2,1,0:T(8,128)}, f32[8,2,8,128]{3,2,1,0:T(8,128)S(1)}) custom-call(s32[2]{0:T(128)S(1)} %pad_add_fusion.refs_0_.count_ref, f32[4,32,128]{2,1,0:T(8,128)S(1)} %slice.12.refs_0_, f32[4,32,128]{2,1,0:T(8,128)S(1)} %collective-permute-done.1.refs_1_, f32[32,128]{1,0:T(8,128)S(1)} %get-tuple-element.35.refs_2_, ...), custom_call_target="tpu_custom_call" | custom-call | flops 268435456 | bytes 4194304 | tf_op jit(solution)/shard_map/pallas_call | solution.py:141
  83.9 12.6 %all_to_all.28 = f32[8,2,8,128]{3,2,1,0:T(8,128)S(1)} all-to-all(f32[8,2,8,128]{3,2,1,0:T(8,128)S(1)} %get-tuple-element.42), channel_id=1, replica_groups=mesh['xh'=2,'xl'=2,'zh'=2,'zl'=4,'y'=4,'core'=2] {'y','core'}, dimensions={0} | all-to-all | bytes 131072 | tf_op jit(solution)/shard_map/all_to_all | solution.py:191
  96.5 0.6 fusion.1
  (3 shorter events, 0.0 us)
Async XLA Ops:
  0.7 0.9 copy-start.6
  1.6 18.9 %copy-start = (f32[8,1,128,2048]{3,2,1,0:T(8,128)S(1)}, f32[8,1,128,2048]{3,2,1,0:T(8,128)}, u32[]{:S(2)}) copy-start(f32[8,1,128,2048]{3,2,1,0:T(8,128)} %param.3) | copy-start | bytes 25165828
  1.6 18.9 %copy-start.3 = (f32[4,512,512]{2,1,0:T(8,128)S(1)}, f32[4,512,512]{2,1,0:T(8,128)}, u32[]{:S(2)}) copy-start(f32[4,512,512]{2,1,0:T(8,128)} %refs_6_.3) | copy-start | bytes 12582916
  36.2 32.5 %copy-start.7 = (f32[8,1,128,32]{2,3,1,0:T(8,128)S(1)}, f32[8,1,128,32]{2,3,1,0:T(8,128)}, u32[]{:S(2)}) copy-start(f32[8,1,128,32]{2,3,1,0:T(8,128)} %param.4) | copy-start | bytes 393220
  52.2 14.0 %all-to-all-start.3 = ((f32[16,32,128]{2,1,0:T(8,128)}), f32[16,32,128]{2,1,0:T(8,128)S(1)}, u32[]{:S(2)}, u32[]{:S(2)}) async-start(f32[16,32,128]{2,1,0:T(8,128)} %get-tuple-element.32), calls=%async_computation.3 | async-start | bytes 524288 | tf_op jit(solution)/shard_map/all_to_all | solution.py:177
  58.3 10.4 %collective-permute-start = (f32[12,32,128]{2,1,0:T(8,128)S(1)}, f32[12,32,128]{2,1,0:T(8,128)S(1)}, u32[]{:S(2)}, u32[]{:S(2)}) collective-permute-start(f32[12,32,128]{2,1,0:T(8,128)S(1)} %get-tuple-element.36.refs_0_), channel_id=1, source_target_pairs={{0,128},{128,0},{1,129},{129,1},{2,130},{130,2},{3,131},{131,3},{4... | collective-permute-start | bytes 589832 | tf_op jit(solution)/shard_map/ppermute | solution.py:34
  66.2 11.9 %collective-permute-start.1 = (f32[4,32,128]{2,1,0:T(8,128)S(1)}, f32[4,32,128]{2,1,0:T(8,128)S(1)}, u32[]{:S(2)}, u32[]{:S(2)}) collective-permute-start(f32[4,32,128]{2,1,0:T(8,128)S(1)} %slice.12.refs_0_), channel_id=1, source_target_pairs={{0,128},{128,0},{1,129},{129,1},{2,130},{130,2},{3,131},{131,3},{4... | collective-permute-start | bytes 196616 | tf_op jit(solution)/shard_map/ppermute | solution.py:34
  68.6 3.4 %copy-start.1 = (f32[8,1,128,2048]{3,2,1,0:T(8,128)S(1)}, f32[8,1,128,2048]{3,2,1,0:T(8,128)}, u32[]{:S(2)}) copy-start(f32[8,1,128,2048]{3,2,1,0:T(8,128)} %param.3) | copy-start | bytes 25165828
  72.0 2.2 %copy-start.4 = (f32[4,512,512]{2,1,0:T(8,128)S(1)}, f32[4,512,512]{2,1,0:T(8,128)}, u32[]{:S(2)}) copy-start(f32[4,512,512]{2,1,0:T(8,128)} %refs_6_.3) | copy-start | bytes 12582916
  74.2 3.9 %copy-start.5 = (f32[4,512,512]{2,1,0:T(8,128)S(1)}, f32[4,512,512]{2,1,0:T(8,128)}, u32[]{:S(2)}) copy-start(f32[4,512,512]{2,1,0:T(8,128)} %refs_6_.3) | copy-start | bytes 12582916
  78.1 3.4 %copy-start.2 = (f32[8,1,128,2048]{3,2,1,0:T(8,128)S(1)}, f32[8,1,128,2048]{3,2,1,0:T(8,128)}, u32[]{:S(2)}) copy-start(f32[8,1,128,2048]{3,2,1,0:T(8,128)} %param.3) | copy-start | bytes 25165828

commit v6 on v5

--- a/solution.py
+++ b/solution.py
@@ -16,14 +16,9 @@
 STEPS = 4
 WIDTH = 512
 NT = (((1,), (1,)), ((), ()))
+NN = (((1,), (0,)), ((), ()))
 SOURCES = 2
-GROUP = (OWNERS,) * STEPS
-NUMBER = (16,) * STEPS
-FIRST = (0, 4, 8, 12)
-
-
-def FINAL(step):
-    return step == STEPS - 2
+GROUP = 16
 
 
 def line_of():
@@ -62,26 +57,59 @@
     return value
 
 
-def begin_body(right_ref, copies_ref, own_ref):
-    own = right_ref[0]
-    own_ref[...] = own
-    for i in range(copies_ref.shape[0]):
+def begin_body(right_ref, own_ref):
+    own_ref[...] = right_ref[0]
+
+
+def prepare_body(panel_ref, inverses_ref, factor_ref):
+    for step in range(STEPS - 1):
+        part = panel_ref[0, :, step * WIDTH:(step + 1) * WIDTH]
+        factor_ref[:, step * WIDTH:(step + 1) * WIDTH] = lax.dot_general(
+            part, inverses_ref[step], NN, precision=lax.Precision.HIGHEST,
+            preferred_element_type=f32,
+        )
+
+
+def arrived(lane, refs, at):
+    tiles = []
+    for tile in range(TILES):
+        wanted = jnp.bitwise_xor(lane, tile)
+        value = refs[0][at]
+        for change in range(1, TILES):
+            value = jnp.where(wanted == change, refs[change][at], value)
+        tiles.append(value)
+    return tiles
+
+
+def advanced(count_ref, own_ref, factor_ref, tiles):
+    steps = len(tiles) // TILES
+    change = times_split(jnp.concatenate(tiles, axis=1), factor_ref[:, :steps * WIDTH])
+    return jnp.where(count_ref[0] == steps, own_ref[...] - change, own_ref[...])
+
+
+def first_body(count_ref, r0, r1, r2, r3, own_ref, factor_ref, own_out_ref):
+    own = advanced(count_ref, own_ref, factor_ref, arrived(count_ref[2], (r0, r1, r2, r3), 0))
+    own_out_ref[0] = own
+    own_out_ref[1] = r0[0]
+
+
+def second_body(count_ref, r0, r1, r2, r3, own_ref, factor_ref, copies_ref, own_out_ref):
+    refs = (r0, r1, r2, r3)
+    tiles = arrived(count_ref[2], refs, 1) + arrived(count_ref[2], refs, 0)
+    own = advanced(count_ref, own_ref.at[0], factor_ref, tiles)
+    own_out_ref[...] = own
+    for i in range(GROUP):
         copies_ref[i] = own
 
 
-def advance_body(step, count_ref, *refs):
-    outs = refs[-3:] if FINAL(step) else refs[-2:]
-    *tiles, own_ref, panel_ref, inverses_ref = refs[:-len(outs)]
-    solved = times_split(joined(tiles[-1], FIRST[step]), inverses_ref[step])
-    change = times_split(solved, panel_ref[0, :, step * WIDTH:(step + 1) * WIDTH])
-    own = jnp.where(count_ref[0] > step, own_ref[...] - change, own_ref[...])
-    outs[1][...] = own
-    for i in range(outs[0].shape[0]):
-        outs[0][i] = own
-    if FINAL(step):
-        for at, ref in enumerate(tiles):
-            for i in range(TILES):
-                outs[2][at * TILES + i] = ref[FIRST[at] + i]
+def third_body(count_ref, tiles_ref, own_ref, factor_ref, copies_ref, own_out_ref, packed_ref):
+    tiles = [tiles_ref[i] for i in range((STEPS - 1) * TILES)]
+    own = advanced(count_ref, own_ref, factor_ref, tiles)
+    own_out_ref[...] = own
+    for i in range(GROUP):
+        copies_ref[i] = own
+    for i, value in enumerate(tiles):
+        packed_ref[i] = value
 
 
 def middle_body(count_ref, *refs):
@@ -148,36 +176,51 @@
     )(*args)
 
 
+def forward(value, step):
+    ahead = (step + 1) * TILES
+    return [
+        lax.ppermute(
+            value, ROWS, [(ahead - TILES + i, ahead + (i ^ change)) for i in range(TILES)]
+        )
+        for change in range(TILES)
+    ]
+
+
 def shards(factor_panel, right_side, inverses):
     blocks, _, rows, columns = factor_panel.shape
     members = right_side.shape[3]
     panel = factor_panel.reshape(blocks, rows, columns)
     right = right_side.reshape(blocks, rows, members).transpose(0, 2, 1)
     step_of = lax.axis_index(ROWS) // TILES
-    count = jnp.stack([jnp.where(step_of < STEPS, step_of, -1), line_of()]).astype(jnp.int32)
+    lane = lax.axis_index("zl")
+    count = jnp.stack([jnp.where(step_of < STEPS, step_of, -1), line_of(), lane])
+    count = count.astype(jnp.int32)
     tile = shape(members, rows)
+    group = shape(GROUP, members, rows)
     right, count = lax.optimization_barrier((right, count))
 
-    copies, own = local(
-        begin_body, 8, [shape(NUMBER[0], members, rows), tile], 1 << 34, 1 << 20, right
-    )
-    received = []
-    for step in range(STEPS - 1):
-        received.append(lax.all_to_all(copies, GROUP[step], 0, 0))
-        outs = [shape(NUMBER[step + 1], members, rows), tile]
-        tiles = received[-1:]
-        if FINAL(step):
-            tiles = received
-            outs.append(shape(3 * TILES, members, rows))
-        copies, own, *packed = local(
-            lambda *refs, step=step: advance_body(step, *refs), 8, outs,
-            1 << 28, 2 << 20, count, *tiles, own, panel, inverses,
-        )
-    early = crossings(packed[0])
-    received = lax.all_to_all(copies, GROUP[STEPS - 1], 0, 0)
-    ends = received[FIRST[STEPS - 1]:FIRST[STEPS - 1] + TILES]
+    own, = local(begin_body, 8, [tile], 1 << 34, 1 << 20, right)
+    tiles = forward(own[None], 0)
+    factor, = local(
+        prepare_body, 16, [shape(rows, (STEPS - 1) * WIDTH)], 1 << 30, 4 << 20,
+        panel, inverses,
+    )
+    own, = local(
+        first_body, 8, [shape(2, members, rows)], 1 << 26, 1 << 20,
+        count, *tiles, own, factor,
+    )
+    tiles = forward(own, 1)
+    copies, own = local(second_body, 8, [group, tile], 1 << 27, 1 << 20, count, *tiles, own, factor)
+    tiles = lax.all_to_all(copies, OWNERS, 0, 0)
+    copies, own, packed = local(
+        third_body, 8, [group, tile, shape(3 * TILES, members, rows)],
+        1 << 27, 2 << 20, count, tiles, own, factor,
+    )
+    early = crossings(packed)
+    received = lax.all_to_all(copies, OWNERS, 0, 0)
+    ends = received[(STEPS - 1) * TILES:]
     late = crossings(ends)
-    own, ends, *early = lax.optimization_barrier((own, ends, packed[0], *early))
+    own, ends, *early = lax.optimization_barrier((own, ends, packed, *early))
     before, partly = local(
         middle_body, 16,
         [shape(members, (STEPS - 1) * WIDTH), shape(blocks, members, rows)],

time: 97.6 us -> 86.8 us (0.89)
  blocking collectives: 58.7 us -> 34.4 us
  starting transfers between devices: 11.1 us -> 21.2 us
  waiting for transfers between devices: 5.38 us -> 7.7 us
    all_to_all x3 -> x1, blocking collectives: 46.1 us -> 20 us  [shards(): tiles = lax.all_to_all(copies, OWNERS, 0, 0)]
    ppermute x0 -> x8, starting transfers between devices: none -> 16.8 us  [forward(): lax.ppermute(value, ROWS, [(ahead - TILES + i, ahead + (i ^ change)) for...]
    ppermute x2, starting transfers between devices: 4.99 us -> 0.1 us  [crossings(): return [lax.ppermute(value, 'xh', [(0, 1), (1, 0)])]]
    all_to_all x1, waiting for transfers between devices: 5.36 us -> 7.66 us  [shards(): received = lax.all_to_all(copies, OWNERS, 0, 0)]
    all_to_all x1, blocking collectives: 12.6 us -> 14.4 us  [shards(): sums = jnp.sum(lax.all_to_all(sums, MEM, 0, 0), axis=0)]
    all_to_all x1, starting transfers between devices: 6.08 us -> 4.31 us  [shards(): received = lax.all_to_all(copies, OWNERS, 0, 0)]
    pallas_call x6 -> x7, Pallas kernels: 10.8 us -> 11 us  [local(): pl.pallas_call(body, out_shape=outs, in_specs=smem + [VMEM] * (len(args)...]
  transfers between devices with their start and end apart: 3 -> 11, of which waited for: 1 -> 1; matrix products, arithmetic and copies ran while one was open for 0% -> 0% of each run, Pallas kernels for 4% -> 6%
where the time goes in v6:
time: 86.8 us; the launch traced here: 85.8 us
  blocking collectives  34.4 us (40%)
  starting transfers between devices  21.2 us (24%)
  Pallas kernels  11 us (13%)
  local copies, waits for them, and re-layouts  9.87 us (11%)
  waiting for transfers between devices  7.7 us (9%)
  between operations  0.92 us (1%)
    all_to_all x1, blocking collectives, shards(): tiles = lax.all_to_all(copies, OWNERS, 0, 0)  20 us
    ppermute x8, starting transfers between devices, forward(): lax.ppermute(value, ROWS, [(ahead - TILES + i, ahead + (i ^ change)) for...  16.8 us
    all_to_all x1, blocking collectives, shards(): sums = jnp.sum(lax.all_to_all(sums, MEM, 0, 0), axis=0)  14.4 us
    pallas_call x7, Pallas kernels, local(): pl.pallas_call(body, out_shape=outs, in_specs=smem + [VMEM] * (len(args)...  11 us
    unnamed x16, local copies, waits for them, and re-layouts  9.86 us
    all_to_all x1, waiting for transfers between devices, shards(): received = lax.all_to_all(copies, OWNERS, 0, 0)  7.66 us
    all_to_all x1, starting transfers between devices, shards(): received = lax.all_to_all(copies, OWNERS, 0, 0)  4.31 us
  transfers between devices with their start and end apart: 11, of which 1 were waited for; matrix products, arithmetic and copies ran while one was open for 0% of the time, Pallas kernels for 6%

profile of v6, /device:TPU:1, one launch (start us, length us, event | category | flops | bytes accessed | tf_op | source)
XLA Modules:
  0.0 85.8 jit_solution(17480823863163746251)
XLA Ops:
  0.7 0.1 pad_add_fusion.count_ref
  0.7 0.0 copy-start.6
  0.7 0.9 %copy-done.6 = f32[8,1,128,32]{2,3,1,0:T(8,128)S(1)} copy-done((f32[8,1,128,32]{2,3,1,0:T(8,128)S(1)}, f32[8,1,128,32]{2,3,1,0:T(8,128)}, u32[]{:S(2)}) %copy-start.6) | copy-done | bytes 131096
  1.6 0.0 copy-start
  1.6 0.0 copy-start.3
  1.6 8.6 %collective-permute-start.3 = (f32[1,32,128]{2,1,0:T(8,128)S(1)}, f32[1,32,128]{2,1,0:T(8,128)S(1)}, u32[]{:S(2)}, u32[]{:S(2)}) collective-permute-start(f32[1,32,128]{2,1,0:T(8,128)S(1)} %bitcast.20), channel_id=1, source_target_pairs={{0,56},{8,48},{16,40},{24,32},{1,57},{9,49},{17,41},{25,33},{2,58}... | collective-permute-start | bytes 49160 | tf_op jit(solution)/shard_map/ppermute | solution.py:182
  10.2 2.0 %collective-permute-start.2 = (f32[1,32,128]{2,1,0:T(8,128)S(1)}, f32[1,32,128]{2,1,0:T(8,128)S(1)}, u32[]{:S(2)}, u32[]{:S(2)}) collective-permute-start(f32[1,32,128]{2,1,0:T(8,128)S(1)} %bitcast.21), channel_id=1, source_target_pairs={{0,48},{8,56},{16,32},{24,40},{1,49},{9,57},{17,33},{25,41},{2,50}... | collective-permute-start | bytes 49160 | tf_op jit(solution)/shard_map/ppermute | solution.py:182
  12.2 1.9 %collective-permute-start.1 = (f32[1,32,128]{2,1,0:T(8,128)S(1)}, f32[1,32,128]{2,1,0:T(8,128)S(1)}, u32[]{:S(2)}, u32[]{:S(2)}) collective-permute-start(f32[1,32,128]{2,1,0:T(8,128)S(1)} %bitcast.22), channel_id=1, source_target_pairs={{0,40},{8,32},{16,56},{24,48},{1,41},{9,33},{17,57},{25,49},{2,42}... | collective-permute-start | bytes 49160 | tf_op jit(solution)/shard_map/ppermute | solution.py:182
  14.1 1.7 %collective-permute-start = (f32[1,32,128]{2,1,0:T(8,128)S(1)}, f32[1,32,128]{2,1,0:T(8,128)S(1)}, u32[]{:S(2)}, u32[]{:S(2)}) collective-permute-start(f32[1,32,128]{2,1,0:T(8,128)S(1)} %bitcast.23), channel_id=1, source_target_pairs={{0,32},{8,40},{16,48},{24,56},{1,33},{9,41},{17,49},{25,57},{2,34}... | collective-permute-start | bytes 49160 | tf_op jit(solution)/shard_map/ppermute | solution.py:182
  15.8 0.0 copy-done
  15.8 0.0 copy-done.3
  15.8 0.0 copy-start.7
  15.9 1.6 %shard_map.59.factor_ref = f32[128,1536]{1,0:T(8,128)S(1)} custom-call(f32[8,128,2048]{2,1,0:T(8,128)S(1)} %bitcast.15, f32[4,512,512]{2,1,0:T(8,128)S(1)} %copy-done.3), custom_call_target="tpu_custom_call" | custom-call | flops 1073741824 | bytes 4194304 | tf_op jit(solution)/shard_map/pallas_call | solution.py:169
  17.5 0.0 collective-permute-done.3.r3
  17.5 0.0 collective-permute-done.2.r2
  17.5 0.0 collective-permute-done.1.r1
  17.5 0.0 collective-permute-done.r0
  17.5 0.7 shard_map.60.own_ref
  18.3 0.7 collective-permute-start.7
  18.9 0.7 collective-permute-start.6
  19.6 0.7 collective-permute-start.5
  20.3 0.7 collective-permute-start.4
  20.9 0.0 collective-permute-done.7.r3
  21.0 0.0 collective-permute-done.6.r2
  21.0 0.0 collective-permute-done.5.r1
  21.0 0.0 collective-permute-done.4.r0
  21.0 0.8 shard_map.61
  21.8 20.0 %all_to_all.15.tiles_ref = f32[16,32,128]{2,1,0:T(8,128)S(1)} all-to-all(f32[16,32,128]{2,1,0:T(8,128)S(1)} %get-tuple-element.21), channel_id=1, replica_groups=mesh['xh'=2,'xl'=2,'zh'=2,'zl'=4,'y'=4,'core'=2] {'xl','zh','zl'}, dimensions={0} | all-to-all | bytes 524288 | tf_op jit(solution)/shard_map/all_to_all | solution.py:214
  41.9 1.6 %shard_map.62 = (f32[16,32,128]{2,1,0:T(8,128)}, f32[32,128]{1,0:T(8,128)S(1)}, f32[12,32,128]{2,1,0:T(8,128)S(1)}) custom-call(s32[3]{0:T(128)S(1)} %pad_add_fusion.count_ref, f32[16,32,128]{2,1,0:T(8,128)S(1)} %all_to_all.15.tiles_ref, f32[32,128]{1,0:T(8,128)S(1)} %get-tuple-element.22.own_ref, f32[128,1536]{1,0:T(8,128)S(1)} %shard_map.59.factor_ref), custom_call_target="tpu_custom_call" | custom-call | flops 134217728 | bytes 2097152 | tf_op jit(solution)/shard_map/pallas_call | solution.py:169
  43.5 4.3 %all-to-all-start.1 = ((f32[16,32,128]{2,1,0:T(8,128)}), f32[16,32,128]{2,1,0:T(8,128)S(1)}, u32[]{:S(2)}, u32[]{:S(2)}) async-start(f32[16,32,128]{2,1,0:T(8,128)} %get-tuple-element.24), calls=%async_computation.1 | async-start | bytes 524288 | tf_op jit(solution)/shard_map/all_to_all | solution.py:220
  47.8 0.1 collective-permute-start.8
  47.9 7.7 %all-to-all-done.1 = f32[16,32,128]{2,1,0:T(8,128)S(1)} async-done(((f32[16,32,128]{2,1,0:T(8,128)}), f32[16,32,128]{2,1,0:T(8,128)S(1)}, u32[]{:S(2)}, u32[]{:S(2)}) %all-to-all-start.1) | async-done | bytes 262176 | tf_op jit(solution)/shard_map/all_to_all | solution.py:220
  55.6 0.0 collective-permute-start.9
  55.6 0.0 collective-permute-done.8.refs_1_
  55.6 0.0 copy-done.7
  55.6 0.0 copy-start.1
  55.7 3.4 %copy-done.1 = f32[8,1,128,2048]{3,2,1,0:T(8,128)S(1)} copy-done((f32[8,1,128,2048]{3,2,1,0:T(8,128)S(1)}, f32[8,1,128,2048]{3,2,1,0:T(8,128)}, u32[]{:S(2)}) %copy-start.1) | copy-done | bytes 8388632
  59.0 0.0 copy-start.4
  59.0 2.2 %copy-done.4 = f32[4,512,512]{2,1,0:T(8,128)S(1)} copy-done((f32[4,512,512]{2,1,0:T(8,128)S(1)}, f32[4,512,512]{2,1,0:T(8,128)}, u32[]{:S(2)}) %copy-start.4) | copy-done | bytes 4194328
  61.2 0.0 copy-start.5
  61.2 3.7 %shard_map.63 = (f32[32,1536]{1,0:T(8,128)S(1)}, f32[8,32,128]{2,1,0:T(8,128)S(1)}) custom-call(s32[3]{0:T(128)S(1)} %pad_add_fusion.count_ref, f32[12,32,128]{2,1,0:T(8,128)S(1)} %get-tuple-element.28.refs_0_, f32[12,32,128]{2,1,0:T(8,128)S(1)} %collective-permute-done.8.refs_1_, f32[8,32,128]{2,1,0:T(8,128)S(1)} %bitcast.19, f32[8,128,2048]{2,1,0:T(8,128)S(1)} %bitcast.16, ...), custom_call_target="tpu_custom_call" | custom-call | flops 1073741824 | bytes 12582912 | tf_op jit(solution)/shard_map/pallas_call | solution.py:169
  65.0 0.0 collective-permute-done.9.refs_1_
  65.0 0.0 copy-done.5
  65.0 0.0 copy-start.2
  65.0 3.4 %copy-done.2 = f32[8,1,128,2048]{3,2,1,0:T(8,128)S(1)} copy-done((f32[8,1,128,2048]{3,2,1,0:T(8,128)S(1)}, f32[8,1,128,2048]{3,2,1,0:T(8,128)}, u32[]{:S(2)}) %copy-start.2) | copy-done | bytes 8388632
  68.4 2.4 %shard_map.64 = (f32[32,2048]{1,0:T(8,128)}, f32[8,32,128]{2,1,0:T(8,128)}, f32[8,2,8,128]{3,2,1,0:T(8,128)S(1)}) custom-call(s32[3]{0:T(128)S(1)} %pad_add_fusion.count_ref, f32[4,32,128]{2,1,0:T(8,128)S(1)} %slice.12.refs_0_, f32[4,32,128]{2,1,0:T(8,128)S(1)} %collective-permute-done.9.refs_1_, f32[32,128]{1,0:T(8,128)S(1)} %get-tuple-element.27.refs_2_, ...), custom_call_target="tpu_custom_call" | custom-call | flops 268435456 | bytes 4194304 | tf_op jit(solution)/shard_map/pallas_call | solution.py:169
  70.8 14.4 %all_to_all.16 = f32[8,2,8,128]{3,2,1,0:T(8,128)S(1)} all-to-all(f32[8,2,8,128]{3,2,1,0:T(8,128)S(1)} %get-tuple-element.34), channel_id=1, replica_groups=mesh['xh'=2,'xl'=2,'zh'=2,'zl'=4,'y'=4,'core'=2] {'y','core'}, dimensions={0} | all-to-all | bytes 131072 | tf_op jit(solution)/shard_map/all_to_all | solution.py:234
  85.2 0.6 fusion.1
  (3 shorter events, 0.0 us)
Async XLA Ops:
  0.7 0.9 %copy-start.6 = (f32[8,1,128,32]{2,3,1,0:T(8,128)S(1)}, f32[8,1,128,32]{2,3,1,0:T(8,128)}, u32[]{:S(2)}) copy-start(f32[8,1,128,32]{2,3,1,0:T(8,128)} %param.4) | copy-start | bytes 393220
  1.6 14.2 %copy-start = (f32[8,1,128,2048]{3,2,1,0:T(8,128)S(1)}, f32[8,1,128,2048]{3,2,1,0:T(8,128)}, u32[]{:S(2)}) copy-start(f32[8,1,128,2048]{3,2,1,0:T(8,128)} %param.3) | copy-start | bytes 25165828
  1.6 14.2 %copy-start.3 = (f32[4,512,512]{2,1,0:T(8,128)S(1)}, f32[4,512,512]{2,1,0:T(8,128)}, u32[]{:S(2)}) copy-start(f32[4,512,512]{2,1,0:T(8,128)} %refs_6_.1) | copy-start | bytes 12582916
  1.6 15.8 %collective-permute-start.3 = (f32[1,32,128]{2,1,0:T(8,128)S(1)}, f32[1,32,128]{2,1,0:T(8,128)S(1)}, u32[]{:S(2)}, u32[]{:S(2)}) collective-permute-start(f32[1,32,128]{2,1,0:T(8,128)S(1)} %bitcast.20), channel_id=1, source_target_pairs={{0,56},{8,48},{16,40},{24,32},{1,57},{9,49},{17,41},{25,33},{2,58}... | collective-permute-start | bytes 49160 | tf_op jit(solution)/shard_map/ppermute | solution.py:182
  10.2 7.3 %collective-permute-start.2 = (f32[1,32,128]{2,1,0:T(8,128)S(1)}, f32[1,32,128]{2,1,0:T(8,128)S(1)}, u32[]{:S(2)}, u32[]{:S(2)}) collective-permute-start(f32[1,32,128]{2,1,0:T(8,128)S(1)} %bitcast.21), channel_id=1, source_target_pairs={{0,48},{8,56},{16,32},{24,40},{1,49},{9,57},{17,33},{25,41},{2,50}... | collective-permute-start | bytes 49160 | tf_op jit(solution)/shard_map/ppermute | solution.py:182
  12.2 5.3 %collective-permute-start.1 = (f32[1,32,128]{2,1,0:T(8,128)S(1)}, f32[1,32,128]{2,1,0:T(8,128)S(1)}, u32[]{:S(2)}, u32[]{:S(2)}) collective-permute-start(f32[1,32,128]{2,1,0:T(8,128)S(1)} %bitcast.22), channel_id=1, source_target_pairs={{0,40},{8,32},{16,56},{24,48},{1,41},{9,33},{17,57},{25,49},{2,42}... | collective-permute-start | bytes 49160 | tf_op jit(solution)/shard_map/ppermute | solution.py:182
  14.1 3.4 %collective-permute-start = (f32[1,32,128]{2,1,0:T(8,128)S(1)}, f32[1,32,128]{2,1,0:T(8,128)S(1)}, u32[]{:S(2)}, u32[]{:S(2)}) collective-permute-start(f32[1,32,128]{2,1,0:T(8,128)S(1)} %bitcast.23), channel_id=1, source_target_pairs={{0,32},{8,40},{16,48},{24,56},{1,33},{9,41},{17,49},{25,57},{2,34}... | collective-permute-start | bytes 49160 | tf_op jit(solution)/shard_map/ppermute | solution.py:182
  15.8 39.8 %copy-start.7 = (f32[8,1,128,32]{2,3,1,0:T(8,128)S(1)}, f32[8,1,128,32]{2,3,1,0:T(8,128)}, u32[]{:S(2)}) copy-start(f32[8,1,128,32]{2,3,1,0:T(8,128)} %param.4) | copy-start | bytes 393220
  18.3 2.7 %collective-permute-start.7 = (f32[2,32,128]{2,1,0:T(8,128)S(1)}, f32[2,32,128]{2,1,0:T(8,128)S(1)}, u32[]{:S(2)}, u32[]{:S(2)}) collective-permute-start(f32[2,32,128]{2,1,0:T(8,128)S(1)} %shard_map.60.own_ref), channel_id=1, source_target_pairs={{32,88},{40,80},{48,72},{56,64},{33,89},{41,81},{49,73},{57,65},{3... | collective-permute-start | bytes 98312 | tf_op jit(solution)/shard_map/ppermute | solution.py:182
  18.9 2.0 %collective-permute-start.6 = (f32[2,32,128]{2,1,0:T(8,128)S(1)}, f32[2,32,128]{2,1,0:T(8,128)S(1)}, u32[]{:S(2)}, u32[]{:S(2)}) collective-permute-start(f32[2,32,128]{2,1,0:T(8,128)S(1)} %shard_map.60.own_ref), channel_id=1, source_target_pairs={{32,80},{40,88},{48,64},{56,72},{33,81},{41,89},{49,65},{57,73},{3... | collective-permute-start | bytes 98312 | tf_op jit(solution)/shard_map/ppermute | solution.py:182
  19.6 1.4 %collective-permute-start.5 = (f32[2,32,128]{2,1,0:T(8,128)S(1)}, f32[2,32,128]{2,1,0:T(8,128)S(1)}, u32[]{:S(2)}, u32[]{:S(2)}) collective-permute-start(f32[2,32,128]{2,1,0:T(8,128)S(1)} %shard_map.60.own_ref), channel_id=1, source_target_pairs={{32,72},{40,64},{48,88},{56,80},{33,73},{41,65},{49,89},{57,81},{3... | collective-permute-start | bytes 98312 | tf_op jit(solution)/shard_map/ppermute | solution.py:182
  20.3 0.7 collective-permute-start.4
  43.5 12.1 %all-to-all-start.1 = ((f32[16,32,128]{2,1,0:T(8,128)}), f32[16,32,128]{2,1,0:T(8,128)S(1)}, u32[]{:S(2)}, u32[]{:S(2)}) async-start(f32[16,32,128]{2,1,0:T(8,128)} %get-tuple-element.24), calls=%async_computation.1 | async-start | bytes 524288 | tf_op jit(solution)/shard_map/all_to_all | solution.py:220
  47.8 7.8 %collective-permute-start.8 = (f32[12,32,128]{2,1,0:T(8,128)S(1)}, f32[12,32,128]{2,1,0:T(8,128)S(1)}, u32[]{:S(2)}, u32[]{:S(2)}) collective-permute-start(f32[12,32,128]{2,1,0:T(8,128)S(1)} %get-tuple-element.28.refs_0_), channel_id=1, source_target_pairs={{0,128},{128,0},{1,129},{129,1},{2,130},{130,2},{3,131},{131,3},{4... | collective-permute-start | bytes 589832 | tf_op jit(solution)/shard_map/ppermute | solution.py:29
  55.6 9.4 %collective-permute-start.9 = (f32[4,32,128]{2,1,0:T(8,128)S(1)}, f32[4,32,128]{2,1,0:T(8,128)S(1)}, u32[]{:S(2)}, u32[]{:S(2)}) collective-permute-start(f32[4,32,128]{2,1,0:T(8,128)S(1)} %slice.12.refs_0_), channel_id=1, source_target_pairs={{0,128},{128,0},{1,129},{129,1},{2,130},{130,2},{3,131},{131,3},{4... | collective-permute-start | bytes 196616 | tf_op jit(solution)/shard_map/ppermute | solution.py:29
  55.6 3.4 %copy-start.1 = (f32[8,1,128,2048]{3,2,1,0:T(8,128)S(1)}, f32[8,1,128,2048]{3,2,1,0:T(8,128)}, u32[]{:S(2)}) copy-start(f32[8,1,128,2048]{3,2,1,0:T(8,128)} %param.3) | copy-start | bytes 25165828
  59.0 2.2 %copy-start.4 = (f32[4,512,512]{2,1,0:T(8,128)S(1)}, f32[4,512,512]{2,1,0:T(8,128)}, u32[]{:S(2)}) copy-start(f32[4,512,512]{2,1,0:T(8,128)} %refs_6_.1) | copy-start | bytes 12582916
  61.2 3.8 %copy-start.5 = (f32[4,512,512]{2,1,0:T(8,128)S(1)}, f32[4,512,512]{2,1,0:T(8,128)}, u32[]{:S(2)}) copy-start(f32[4,512,512]{2,1,0:T(8,128)} %refs_6_.1) | copy-start | bytes 12582916
  65.0 3.4 %copy-start.2 = (f32[8,1,128,2048]{3,2,1,0:T(8,128)S(1)}, f32[8,1,128,2048]{3,2,1,0:T(8,128)}, u32[]{:S(2)}) copy-start(f32[8,1,128,2048]{3,2,1,0:T(8,128)} %param.3) | copy-start | bytes 25165828

commit v7 on v6

--- a/solution.py
+++ b/solution.py
@@ -19,6 +19,7 @@
 NN = (((1,), (0,)), ((), ()))
 SOURCES = 2
 GROUP = 16
+ORDER = (2, 3, 1, 0)
 
 
 def line_of():
@@ -26,7 +27,7 @@
 
 
 def crossings(value):
-    return [lax.ppermute(value, "xh", [(0, 1), (1, 0)])]
+    return [lax.ppermute(value, "xh", [(0, 1)])]
 
 
 def split(value):
@@ -43,9 +44,12 @@
 
 
 def times_split(value, right):
+    return times_halves(value, *split(right))
+
+
+def times_halves(value, right_high, right_low):
     rows = value.shape[0]
     high, low = split(value)
-    right_high, right_low = split(right)
     wide = dot16(jnp.concatenate([high, low], axis=0), right_high, NT)
     return wide[:rows] + wide[rows:] + dot16(high, right_low, NT)
 
@@ -61,13 +65,50 @@
     own_ref[...] = right_ref[0]
 
 
-def prepare_body(panel_ref, inverses_ref, factor_ref):
+def prepare_body(panel_ref, inverses_ref, high_ref, low_ref, part_ref, inverse_ref, sems):
+    copies = []
     for step in range(STEPS - 1):
-        part = panel_ref[0, :, step * WIDTH:(step + 1) * WIDTH]
-        factor_ref[:, step * WIDTH:(step + 1) * WIDTH] = lax.dot_general(
-            part, inverses_ref[step], NN, precision=lax.Precision.HIGHEST,
+        columns = pl.ds(step * WIDTH, WIDTH)
+        copies.append((
+            pltpu.make_async_copy(
+                panel_ref.at[0, :, columns], part_ref.at[step], sems.at[0, step]
+            ),
+            pltpu.make_async_copy(
+                inverses_ref.at[step], inverse_ref.at[step], sems.at[1, step]
+            ),
+        ))
+    for pair in copies:
+        for copy in pair:
+            copy.start()
+    for step, pair in enumerate(copies):
+        for copy in pair:
+            copy.wait()
+        factor = lax.dot_general(
+            part_ref[step], inverse_ref[step], NN, precision=lax.Precision.HIGHEST,
             preferred_element_type=f32,
         )
+        columns = slice(step * WIDTH, (step + 1) * WIDTH)
+        high_ref[:, columns], low_ref[:, columns] = split(factor)
+
+
+def prepare(panel, inverses):
+    rows = panel.shape[1]
+    number = STEPS - 1
+    half = jax.ShapeDtypeStruct((rows, number * WIDTH), bf16)
+    return pl.pallas_call(
+        prepare_body,
+        out_shape=[half, half],
+        in_specs=[pl.BlockSpec(memory_space=pl.ANY)] * 2,
+        out_specs=[VMEM] * 2,
+        scratch_shapes=[
+            pltpu.VMEM((number, rows, WIDTH), f32),
+            pltpu.VMEM((number, WIDTH, WIDTH), f32),
+            pltpu.SemaphoreType.DMA((2, number)),
+        ],
+        compiler_params=params(16),
+        cost_estimate=cost(1 << 30, 4 << 20),
+        name="prepare",
+    )(panel, inverses)
 
 
 def arrived(lane, refs, at):
@@ -81,30 +122,32 @@
     return tiles
 
 
-def advanced(count_ref, own_ref, factor_ref, tiles):
+def advanced(count_ref, own_ref, high_ref, low_ref, tiles):
     steps = len(tiles) // TILES
-    change = times_split(jnp.concatenate(tiles, axis=1), factor_ref[:, :steps * WIDTH])
+    change = times_halves(
+        jnp.concatenate(tiles, axis=1), high_ref[:, :steps * WIDTH], low_ref[:, :steps * WIDTH]
+    )
     return jnp.where(count_ref[0] == steps, own_ref[...] - change, own_ref[...])
 
 
-def first_body(count_ref, r0, r1, r2, r3, own_ref, factor_ref, own_out_ref):
-    own = advanced(count_ref, own_ref, factor_ref, arrived(count_ref[2], (r0, r1, r2, r3), 0))
+def first_body(count_ref, r0, r1, r2, r3, own_ref, high_ref, low_ref, own_out_ref):
+    own = advanced(count_ref, own_ref, high_ref, low_ref, arrived(count_ref[2], (r0, r1, r2, r3), 0))
     own_out_ref[0] = own
     own_out_ref[1] = r0[0]
 
 
-def second_body(count_ref, r0, r1, r2, r3, own_ref, factor_ref, copies_ref, own_out_ref):
+def second_body(count_ref, r0, r1, r2, r3, own_ref, high_ref, low_ref, copies_ref, own_out_ref):
     refs = (r0, r1, r2, r3)
     tiles = arrived(count_ref[2], refs, 1) + arrived(count_ref[2], refs, 0)
-    own = advanced(count_ref, own_ref.at[0], factor_ref, tiles)
+    own = advanced(count_ref, own_ref.at[0], high_ref, low_ref, tiles)
     own_out_ref[...] = own
     for i in range(GROUP):
         copies_ref[i] = own
 
 
-def third_body(count_ref, tiles_ref, own_ref, factor_ref, copies_ref, own_out_ref, packed_ref):
+def third_body(count_ref, tiles_ref, own_ref, high_ref, low_ref, copies_ref, own_out_ref, packed_ref):
     tiles = [tiles_ref[i] for i in range((STEPS - 1) * TILES)]
-    own = advanced(count_ref, own_ref, factor_ref, tiles)
+    own = advanced(count_ref, own_ref, high_ref, low_ref, tiles)
     own_out_ref[...] = own
     for i in range(GROUP):
         copies_ref[i] = own
@@ -178,12 +221,13 @@
 
 def forward(value, step):
     ahead = (step + 1) * TILES
-    return [
-        lax.ppermute(
+    pieces = {
+        change: lax.ppermute(
             value, ROWS, [(ahead - TILES + i, ahead + (i ^ change)) for i in range(TILES)]
         )
-        for change in range(TILES)
-    ]
+        for change in ORDER
+    }
+    return [pieces[change] for change in range(TILES)]
 
 
 def shards(factor_panel, right_side, inverses):
@@ -199,22 +243,21 @@
     group = shape(GROUP, members, rows)
     right, count = lax.optimization_barrier((right, count))
 
-    own, = local(begin_body, 8, [tile], 1 << 34, 1 << 20, right)
+    own, = local(begin_body, 8, [tile], 1 << 20, 1 << 20, right)
     tiles = forward(own[None], 0)
-    factor, = local(
-        prepare_body, 16, [shape(rows, (STEPS - 1) * WIDTH)], 1 << 30, 4 << 20,
-        panel, inverses,
-    )
+    factor = prepare(panel, inverses)
     own, = local(
-        first_body, 8, [shape(2, members, rows)], 1 << 26, 1 << 20,
-        count, *tiles, own, factor,
+        first_body, 8, [shape(2, members, rows)], 1 << 34, 1 << 20,
+        count, *tiles, own, *factor,
     )
     tiles = forward(own, 1)
-    copies, own = local(second_body, 8, [group, tile], 1 << 27, 1 << 20, count, *tiles, own, factor)
+    copies, own = local(
+        second_body, 8, [group, tile], 1 << 27, 1 << 20, count, *tiles, own, *factor,
+    )
     tiles = lax.all_to_all(copies, OWNERS, 0, 0)
     copies, own, packed = local(
         third_body, 8, [group, tile, shape(3 * TILES, members, rows)],
-        1 << 27, 2 << 20, count, tiles, own, factor,
+        1 << 27, 2 << 20, count, tiles, own, *factor,
     )
     early = crossings(packed)
     received = lax.all_to_all(copies, OWNERS, 0, 0)

time: 86.8 us -> 87.7 us (1.010)
  blocking collectives: 34.4 us -> 28 us
  local copies, waits for them, and re-layouts: 9.87 us -> 15.4 us
  starting transfers between devices: 21.2 us -> 23.7 us
  waiting for transfers between devices: 7.7 us -> 6.69 us
    unnamed x16, local copies, waits for them, and re-layouts: 9.86 us -> 15.4 us
    all_to_all x1, blocking collectives: 20 us -> 14.8 us  [shards(): tiles = lax.all_to_all(copies, OWNERS, 0, 0)]
    ppermute x2, starting transfers between devices: 0.1 us -> 2.58 us  [crossings(): return [lax.ppermute(value, 'xh', [(0, 1)])]]
    pallas_call x0 -> x1, Pallas kernels: none -> 2.31 us  [prepare(): pl.pallas_call(prepare_body, out_shape=[half, half], in_specs=[pl.BlockSp...]
    pallas_call x7 -> x6, Pallas kernels: 11 us -> 9.37 us  [local(): pl.pallas_call(body, out_shape=outs, in_specs=smem + [VMEM] * (len(args)...]
    all_to_all x1, blocking collectives: 14.4 us -> 13.1 us  [shards(): sums = jnp.sum(lax.all_to_all(sums, MEM, 0, 0), axis=0)]
    all_to_all x1, waiting for transfers between devices: 7.66 us -> 6.65 us  [shards(): received = lax.all_to_all(copies, OWNERS, 0, 0)]
  transfers between devices with their start and end apart: 11 -> 11, of which waited for: 1 -> 1; matrix products, arithmetic and copies ran while one was open for 0% -> 0% of each run, Pallas kernels for 6% -> 7%
where the time goes in v7:
time: 87.7 us; the launch traced here: 87.1 us
  blocking collectives  28 us (32%)
  starting transfers between devices  23.7 us (27%)
  local copies, waits for them, and re-layouts  15.4 us (18%)
  Pallas kernels  11.7 us (13%)
  waiting for transfers between devices  6.69 us (8%)
  between operations  0.9 us (1%)
    ppermute x8, starting transfers between devices, forward(): lax.ppermute(value, ROWS, [(ahead - TILES + i, ahead + (i ^ change)) for...  16.2 us
    unnamed x16, local copies, waits for them, and re-layouts  15.4 us
    all_to_all x1, blocking collectives, shards(): tiles = lax.all_to_all(copies, OWNERS, 0, 0)  14.8 us
    all_to_all x1, blocking collectives, shards(): sums = jnp.sum(lax.all_to_all(sums, MEM, 0, 0), axis=0)  13.1 us
    pallas_call x6, Pallas kernels, local(): pl.pallas_call(body, out_shape=outs, in_specs=smem + [VMEM] * (len(args)...  9.37 us
    all_to_all x1, waiting for transfers between devices, shards(): received = lax.all_to_all(copies, OWNERS, 0, 0)  6.65 us
    all_to_all x1, starting transfers between devices, shards(): received = lax.all_to_all(copies, OWNERS, 0, 0)  4.99 us
    ppermute x2, starting transfers between devices, crossings(): return [lax.ppermute(value, 'xh', [(0, 1)])]  2.58 us
  transfers between devices with their start and end apart: 11, of which 1 were waited for; matrix products, arithmetic and copies ran while one was open for 0% of the time, Pallas kernels for 7%

profile of v7, /device:TPU:1, one launch (start us, length us, event | category | flops | bytes accessed | tf_op | source)
XLA Modules:
  0.0 87.1 jit_solution(17662768582948546236)
XLA Ops:
  0.7 0.1 pad_add_fusion.count_ref
  0.7 0.0 copy-start.6
  0.7 0.9 %copy-done.6 = f32[8,1,128,32]{2,3,1,0:T(8,128)S(1)} copy-done((f32[8,1,128,32]{2,3,1,0:T(8,128)S(1)}, f32[8,1,128,32]{2,3,1,0:T(8,128)}, u32[]{:S(2)}) %copy-start.6) | copy-done | bytes 131096
  1.6 8.3 %collective-permute-start.3 = (f32[1,32,128]{2,1,0:T(8,128)S(1)}, f32[1,32,128]{2,1,0:T(8,128)S(1)}, u32[]{:S(2)}, u32[]{:S(2)}) collective-permute-start(f32[1,32,128]{2,1,0:T(8,128)S(1)} %bitcast.20), channel_id=1, source_target_pairs={{0,56},{8,48},{16,40},{24,32},{1,57},{9,49},{17,41},{25,33},{2,58}... | collective-permute-start | bytes 49160 | tf_op jit(solution)/shard_map/ppermute | solution.py:225
  9.9 1.7 %collective-permute-start.2 = (f32[1,32,128]{2,1,0:T(8,128)S(1)}, f32[1,32,128]{2,1,0:T(8,128)S(1)}, u32[]{:S(2)}, u32[]{:S(2)}) collective-permute-start(f32[1,32,128]{2,1,0:T(8,128)S(1)} %bitcast.21), channel_id=1, source_target_pairs={{0,48},{8,56},{16,32},{24,40},{1,49},{9,57},{17,33},{25,41},{2,50}... | collective-permute-start | bytes 49160 | tf_op jit(solution)/shard_map/ppermute | solution.py:225
  11.7 1.7 %collective-permute-start.1 = (f32[1,32,128]{2,1,0:T(8,128)S(1)}, f32[1,32,128]{2,1,0:T(8,128)S(1)}, u32[]{:S(2)}, u32[]{:S(2)}) collective-permute-start(f32[1,32,128]{2,1,0:T(8,128)S(1)} %bitcast.22), channel_id=1, source_target_pairs={{0,40},{8,32},{16,56},{24,48},{1,41},{9,33},{17,57},{25,49},{2,42}... | collective-permute-start | bytes 49160 | tf_op jit(solution)/shard_map/ppermute | solution.py:225
  13.4 1.7 %collective-permute-start = (f32[1,32,128]{2,1,0:T(8,128)S(1)}, f32[1,32,128]{2,1,0:T(8,128)S(1)}, u32[]{:S(2)}, u32[]{:S(2)}) collective-permute-start(f32[1,32,128]{2,1,0:T(8,128)S(1)} %bitcast.23), channel_id=1, source_target_pairs={{0,32},{8,40},{16,48},{24,56},{1,33},{9,41},{17,49},{25,57},{2,34}... | collective-permute-start | bytes 49160 | tf_op jit(solution)/shard_map/ppermute | solution.py:225
  15.2 0.0 copy-start
  15.2 3.4 %copy-done = f32[8,1,128,2048]{3,2,1,0:T(8,128)S(1)} copy-done((f32[8,1,128,2048]{3,2,1,0:T(8,128)S(1)}, f32[8,1,128,2048]{3,2,1,0:T(8,128)}, u32[]{:S(2)}) %copy-start) | copy-done | bytes 8388632
  18.6 0.0 copy-start.3
  18.6 2.2 %copy-done.3 = f32[4,512,512]{2,1,0:T(8,128)S(1)} copy-done((f32[4,512,512]{2,1,0:T(8,128)S(1)}, f32[4,512,512]{2,1,0:T(8,128)}, u32[]{:S(2)}) %copy-start.3) | copy-done | bytes 4194328
  20.7 2.3 %prepare.1 = (bf16[128,1536]{1,0:T(8,128)(2,1)S(1)}, bf16[128,1536]{1,0:T(8,128)(2,1)S(1)}) custom-call(f32[8,128,2048]{2,1,0:T(8,128)S(1)} %bitcast.15, f32[4,512,512]{2,1,0:T(8,128)S(1)} %copy-done.3), custom_call_target="tpu_custom_call" | custom-call | flops 1073741824 | bytes 4194304 | tf_op jit(solution)/shard_map/prepare/pallas_call | solution.py:98
  23.1 0.0 collective-permute-done.3.r3
  23.1 0.0 collective-permute-done.2.r2
  23.1 0.0 collective-permute-done.1.r1
  23.1 0.0 collective-permute-done.r0
  23.1 0.0 copy-start.7
  23.1 0.7 shard_map.59.own_ref
  23.8 0.7 collective-permute-start.7
  24.5 0.7 collective-permute-start.6
  25.2 0.7 collective-permute-start.5
  25.9 0.7 collective-permute-start.4
  26.5 0.0 collective-permute-done.7.r3
  26.5 0.0 collective-permute-done.6.r2
  26.6 0.0 collective-permute-done.5.r1
  26.6 0.0 collective-permute-done.4.r0
  26.6 0.8 shard_map.60
  27.4 14.8 %all_to_all.15.tiles_ref = f32[16,32,128]{2,1,0:T(8,128)S(1)} all-to-all(f32[16,32,128]{2,1,0:T(8,128)S(1)} %get-tuple-element.25), channel_id=1, replica_groups=mesh['xh'=2,'xl'=2,'zh'=2,'zl'=4,'y'=4,'core'=2] {'xl','zh','zl'}, dimensions={0} | all-to-all | bytes 524288 | tf_op jit(solution)/shard_map/all_to_all | solution.py:257
  42.3 1.6 %shard_map.61 = (f32[16,32,128]{2,1,0:T(8,128)}, f32[32,128]{1,0:T(8,128)S(1)}, f32[12,32,128]{2,1,0:T(8,128)S(1)}) custom-call(s32[3]{0:T(128)S(1)} %pad_add_fusion.count_ref, f32[16,32,128]{2,1,0:T(8,128)S(1)} %all_to_all.15.tiles_ref, f32[32,128]{1,0:T(8,128)S(1)} %get-tuple-element.26.own_ref, bf16[128,1536]{1,0:T(8,128)(2,1)S(1)} %get-tuple-element.23.high_ref, ...), custom_call_target="tpu_custom_call" | custom-call | flops 134217728 | bytes 2097152 | tf_op jit(solution)/shard_map/pallas_call | solution.py:212
  43.9 5.0 %all-to-all-start.1 = ((f32[16,32,128]{2,1,0:T(8,128)}), f32[16,32,128]{2,1,0:T(8,128)S(1)}, u32[]{:S(2)}, u32[]{:S(2)}) async-start(f32[16,32,128]{2,1,0:T(8,128)} %get-tuple-element.28), calls=%async_computation.1 | async-start | bytes 524288 | tf_op jit(solution)/shard_map/all_to_all | solution.py:263
  48.9 1.3 %collective-permute-start.8 = (f32[12,32,128]{2,1,0:T(8,128)S(1)}, f32[12,32,128]{2,1,0:T(8,128)S(1)}, u32[]{:S(2)}, u32[]{:S(2)}) collective-permute-start(f32[12,32,128]{2,1,0:T(8,128)S(1)} %get-tuple-element.32.refs_0_), channel_id=1, source_target_pairs={{0,128},{1,129},{2,130},{3,131},{4,132},{5,133},{6,134},{7,135},{8... | collective-permute-start | bytes 589832 | tf_op jit(solution)/shard_map/ppermute | solution.py:30
  50.2 6.7 %all-to-all-done.1 = f32[16,32,128]{2,1,0:T(8,128)S(1)} async-done(((f32[16,32,128]{2,1,0:T(8,128)}), f32[16,32,128]{2,1,0:T(8,128)S(1)}, u32[]{:S(2)}, u32[]{:S(2)}) %all-to-all-start.1) | async-done | bytes 262176 | tf_op jit(solution)/shard_map/all_to_all | solution.py:263
  56.9 1.3 %collective-permute-start.9 = (f32[4,32,128]{2,1,0:T(8,128)S(1)}, f32[4,32,128]{2,1,0:T(8,128)S(1)}, u32[]{:S(2)}, u32[]{:S(2)}) collective-permute-start(f32[4,32,128]{2,1,0:T(8,128)S(1)} %slice.12.refs_0_), channel_id=1, source_target_pairs={{0,128},{1,129},{2,130},{3,131},{4,132},{5,133},{6,134},{7,135},{8... | collective-permute-start | bytes 196616 | tf_op jit(solution)/shard_map/ppermute | solution.py:30
  58.1 0.0 collective-permute-done.8.refs_1_
  58.2 0.0 copy-done.7
  58.2 0.0 copy-start.1
  58.2 3.4 %copy-done.1 = f32[8,1,128,2048]{3,2,1,0:T(8,128)S(1)} copy-done((f32[8,1,128,2048]{3,2,1,0:T(8,128)S(1)}, f32[8,1,128,2048]{3,2,1,0:T(8,128)}, u32[]{:S(2)}) %copy-start.1) | copy-done | bytes 8388632
  61.6 0.0 copy-start.4
  61.6 2.2 %copy-done.4 = f32[4,512,512]{2,1,0:T(8,128)S(1)} copy-done((f32[4,512,512]{2,1,0:T(8,128)S(1)}, f32[4,512,512]{2,1,0:T(8,128)}, u32[]{:S(2)}) %copy-start.4) | copy-done | bytes 4194328
  63.7 0.0 copy-start.5
  63.7 3.7 %shard_map.62 = (f32[32,1536]{1,0:T(8,128)S(1)}, f32[8,32,128]{2,1,0:T(8,128)S(1)}) custom-call(s32[3]{0:T(128)S(1)} %pad_add_fusion.count_ref, f32[12,32,128]{2,1,0:T(8,128)S(1)} %get-tuple-element.32.refs_0_, f32[12,32,128]{2,1,0:T(8,128)S(1)} %collective-permute-done.8.refs_1_, f32[8,32,128]{2,1,0:T(8,128)S(1)} %bitcast.19, f32[8,128,2048]{2,1,0:T(8,128)S(1)} %bitcast.16, ...), custom_call_target="tpu_custom_call" | custom-call | flops 1073741824 | bytes 12582912 | tf_op jit(solution)/shard_map/pallas_call | solution.py:212
  67.5 0.0 collective-permute-done.9.refs_1_
  67.5 0.0 copy-done.5
  67.5 0.0 copy-start.2
  67.5 3.4 %copy-done.2 = f32[8,1,128,2048]{3,2,1,0:T(8,128)S(1)} copy-done((f32[8,1,128,2048]{3,2,1,0:T(8,128)S(1)}, f32[8,1,128,2048]{3,2,1,0:T(8,128)}, u32[]{:S(2)}) %copy-start.2) | copy-done | bytes 8388632
  70.9 2.4 %shard_map.63 = (f32[32,2048]{1,0:T(8,128)}, f32[8,32,128]{2,1,0:T(8,128)}, f32[8,2,8,128]{3,2,1,0:T(8,128)S(1)}) custom-call(s32[3]{0:T(128)S(1)} %pad_add_fusion.count_ref, f32[4,32,128]{2,1,0:T(8,128)S(1)} %slice.12.refs_0_, f32[4,32,128]{2,1,0:T(8,128)S(1)} %collective-permute-done.9.refs_1_, f32[32,128]{1,0:T(8,128)S(1)} %get-tuple-element.31.refs_2_, ...), custom_call_target="tpu_custom_call" | custom-call | flops 268435456 | bytes 4194304 | tf_op jit(solution)/shard_map/pallas_call | solution.py:212
  73.3 13.1 %all_to_all.16 = f32[8,2,8,128]{3,2,1,0:T(8,128)S(1)} all-to-all(f32[8,2,8,128]{3,2,1,0:T(8,128)S(1)} %get-tuple-element.38), channel_id=1, replica_groups=mesh['xh'=2,'xl'=2,'zh'=2,'zl'=4,'y'=4,'core'=2] {'y','core'}, dimensions={0} | all-to-all | bytes 131072 | tf_op jit(solution)/shard_map/all_to_all | solution.py:277
  86.5 0.6 fusion.1
  (3 shorter events, 0.0 us)
Async XLA Ops:
  0.7 0.9 %copy-start.6 = (f32[8,1,128,32]{2,3,1,0:T(8,128)S(1)}, f32[8,1,128,32]{2,3,1,0:T(8,128)}, u32[]{:S(2)}) copy-start(f32[8,1,128,32]{2,3,1,0:T(8,128)} %param.4) | copy-start | bytes 393220
  1.6 21.4 %collective-permute-start.3 = (f32[1,32,128]{2,1,0:T(8,128)S(1)}, f32[1,32,128]{2,1,0:T(8,128)S(1)}, u32[]{:S(2)}, u32[]{:S(2)}) collective-permute-start(f32[1,32,128]{2,1,0:T(8,128)S(1)} %bitcast.20), channel_id=1, source_target_pairs={{0,56},{8,48},{16,40},{24,32},{1,57},{9,49},{17,41},{25,33},{2,58}... | collective-permute-start | bytes 49160 | tf_op jit(solution)/shard_map/ppermute | solution.py:225
  9.9 13.1 %collective-permute-start.2 = (f32[1,32,128]{2,1,0:T(8,128)S(1)}, f32[1,32,128]{2,1,0:T(8,128)S(1)}, u32[]{:S(2)}, u32[]{:S(2)}) collective-permute-start(f32[1,32,128]{2,1,0:T(8,128)S(1)} %bitcast.21), channel_id=1, source_target_pairs={{0,48},{8,56},{16,32},{24,40},{1,49},{9,57},{17,33},{25,41},{2,50}... | collective-permute-start | bytes 49160 | tf_op jit(solution)/shard_map/ppermute | solution.py:225
  11.7 11.4 %collective-permute-start.1 = (f32[1,32,128]{2,1,0:T(8,128)S(1)}, f32[1,32,128]{2,1,0:T(8,128)S(1)}, u32[]{:S(2)}, u32[]{:S(2)}) collective-permute-start(f32[1,32,128]{2,1,0:T(8,128)S(1)} %bitcast.22), channel_id=1, source_target_pairs={{0,40},{8,32},{16,56},{24,48},{1,41},{9,33},{17,57},{25,49},{2,42}... | collective-permute-start | bytes 49160 | tf_op jit(solution)/shard_map/ppermute | solution.py:225
  13.4 9.7 %collective-permute-start = (f32[1,32,128]{2,1,0:T(8,128)S(1)}, f32[1,32,128]{2,1,0:T(8,128)S(1)}, u32[]{:S(2)}, u32[]{:S(2)}) collective-permute-start(f32[1,32,128]{2,1,0:T(8,128)S(1)} %bitcast.23), channel_id=1, source_target_pairs={{0,32},{8,40},{16,48},{24,56},{1,33},{9,41},{17,49},{25,57},{2,34}... | collective-permute-start | bytes 49160 | tf_op jit(solution)/shard_map/ppermute | solution.py:225
  15.2 3.4 %copy-start = (f32[8,1,128,2048]{3,2,1,0:T(8,128)S(1)}, f32[8,1,128,2048]{3,2,1,0:T(8,128)}, u32[]{:S(2)}) copy-start(f32[8,1,128,2048]{3,2,1,0:T(8,128)} %param.3) | copy-start | bytes 25165828
  18.6 2.2 %copy-start.3 = (f32[4,512,512]{2,1,0:T(8,128)S(1)}, f32[4,512,512]{2,1,0:T(8,128)}, u32[]{:S(2)}) copy-start(f32[4,512,512]{2,1,0:T(8,128)} %refs_6_.1) | copy-start | bytes 12582916
  23.1 35.1 %copy-start.7 = (f32[8,1,128,32]{2,3,1,0:T(8,128)S(1)}, f32[8,1,128,32]{2,3,1,0:T(8,128)}, u32[]{:S(2)}) copy-start(f32[8,1,128,32]{2,3,1,0:T(8,128)} %param.4) | copy-start | bytes 393220
  23.8 2.7 %collective-permute-start.7 = (f32[2,32,128]{2,1,0:T(8,128)S(1)}, f32[2,32,128]{2,1,0:T(8,128)S(1)}, u32[]{:S(2)}, u32[]{:S(2)}) collective-permute-start(f32[2,32,128]{2,1,0:T(8,128)S(1)} %shard_map.59.own_ref), channel_id=1, source_target_pairs={{32,88},{40,80},{48,72},{56,64},{33,89},{41,81},{49,73},{57,65},{3... | collective-permute-start | bytes 98312 | tf_op jit(solution)/shard_map/ppermute | solution.py:225
  24.5 2.0 %collective-permute-start.6 = (f32[2,32,128]{2,1,0:T(8,128)S(1)}, f32[2,32,128]{2,1,0:T(8,128)S(1)}, u32[]{:S(2)}, u32[]{:S(2)}) collective-permute-start(f32[2,32,128]{2,1,0:T(8,128)S(1)} %shard_map.59.own_ref), channel_id=1, source_target_pairs={{32,80},{40,88},{48,64},{56,72},{33,81},{41,89},{49,65},{57,73},{3... | collective-permute-start | bytes 98312 | tf_op jit(solution)/shard_map/ppermute | solution.py:225
  25.2 1.4 %collective-permute-start.5 = (f32[2,32,128]{2,1,0:T(8,128)S(1)}, f32[2,32,128]{2,1,0:T(8,128)S(1)}, u32[]{:S(2)}, u32[]{:S(2)}) collective-permute-start(f32[2,32,128]{2,1,0:T(8,128)S(1)} %shard_map.59.own_ref), channel_id=1, source_target_pairs={{32,72},{40,64},{48,88},{56,80},{33,73},{41,65},{49,89},{57,81},{3... | collective-permute-start | bytes 98312 | tf_op jit(solution)/shard_map/ppermute | solution.py:225
  25.9 0.7 collective-permute-start.4
  43.9 13.0 %all-to-all-start.1 = ((f32[16,32,128]{2,1,0:T(8,128)}), f32[16,32,128]{2,1,0:T(8,128)S(1)}, u32[]{:S(2)}, u32[]{:S(2)}) async-start(f32[16,32,128]{2,1,0:T(8,128)} %get-tuple-element.28), calls=%async_computation.1 | async-start | bytes 524288 | tf_op jit(solution)/shard_map/all_to_all | solution.py:263
  48.9 9.3 %collective-permute-start.8 = (f32[12,32,128]{2,1,0:T(8,128)S(1)}, f32[12,32,128]{2,1,0:T(8,128)S(1)}, u32[]{:S(2)}, u32[]{:S(2)}) collective-permute-start(f32[12,32,128]{2,1,0:T(8,128)S(1)} %get-tuple-element.32.refs_0_), channel_id=1, source_target_pairs={{0,128},{1,129},{2,130},{3,131},{4,132},{5,133},{6,134},{7,135},{8... | collective-permute-start | bytes 589832 | tf_op jit(solution)/shard_map/ppermute | solution.py:30
  56.9 10.6 %collective-permute-start.9 = (f32[4,32,128]{2,1,0:T(8,128)S(1)}, f32[4,32,128]{2,1,0:T(8,128)S(1)}, u32[]{:S(2)}, u32[]{:S(2)}) collective-permute-start(f32[4,32,128]{2,1,0:T(8,128)S(1)} %slice.12.refs_0_), channel_id=1, source_target_pairs={{0,128},{1,129},{2,130},{3,131},{4,132},{5,133},{6,134},{7,135},{8... | collective-permute-start | bytes 196616 | tf_op jit(solution)/shard_map/ppermute | solution.py:30
  58.2 3.4 %copy-start.1 = (f32[8,1,128,2048]{3,2,1,0:T(8,128)S(1)}, f32[8,1,128,2048]{3,2,1,0:T(8,128)}, u32[]{:S(2)}) copy-start(f32[8,1,128,2048]{3,2,1,0:T(8,128)} %param.3) | copy-start | bytes 25165828
  61.6 2.2 %copy-start.4 = (f32[4,512,512]{2,1,0:T(8,128)S(1)}, f32[4,512,512]{2,1,0:T(8,128)}, u32[]{:S(2)}) copy-start(f32[4,512,512]{2,1,0:T(8,128)} %refs_6_.1) | copy-start | bytes 12582916
  63.7 3.8 %copy-start.5 = (f32[4,512,512]{2,1,0:T(8,128)S(1)}, f32[4,512,512]{2,1,0:T(8,128)}, u32[]{:S(2)}) copy-start(f32[4,512,512]{2,1,0:T(8,128)} %refs_6_.1) | copy-start | bytes 12582916
  67.5 3.4 %copy-start.2 = (f32[8,1,128,2048]{3,2,1,0:T(8,128)S(1)}, f32[8,1,128,2048]{3,2,1,0:T(8,128)}, u32[]{:S(2)}) copy-start(f32[8,1,128,2048]{3,2,1,0:T(8,128)} %param.3) | copy-start | bytes 25165828

commit v8 on v7

--- a/solution.py
+++ b/solution.py
@@ -27,7 +27,7 @@
 
 
 def crossings(value):
-    return [lax.ppermute(value, "xh", [(0, 1)])]
+    return [lax.ppermute(value, ROWS[:2], [(0, 3), (1, 2)])]
 
 
 def split(value):
@@ -83,10 +83,11 @@
     for step, pair in enumerate(copies):
         for copy in pair:
             copy.wait()
-        factor = lax.dot_general(
-            part_ref[step], inverse_ref[step], NN, precision=lax.Precision.HIGHEST,
-            preferred_element_type=f32,
-        )
+        high, low = split(part_ref[step])
+        inverse_high, inverse_low = split(inverse_ref[step])
+        wide = dot16(jnp.concatenate([high, low], axis=0), inverse_high, NN)
+        rows = high.shape[0]
+        factor = wide[:rows] + wide[rows:] + dot16(high, inverse_low, NN)
         columns = slice(step * WIDTH, (step + 1) * WIDTH)
         high_ref[:, columns], low_ref[:, columns] = split(factor)
 
@@ -116,8 +117,8 @@
     for tile in range(TILES):
         wanted = jnp.bitwise_xor(lane, tile)
         value = refs[0][at]
-        for change in range(1, TILES):
-            value = jnp.where(wanted == change, refs[change][at], value)
+        for change, ref in zip(ORDER[1:], refs[1:]):
+            value = jnp.where(wanted == change, ref[at], value)
         tiles.append(value)
     return tiles
 
@@ -133,7 +134,7 @@
 def first_body(count_ref, r0, r1, r2, r3, own_ref, high_ref, low_ref, own_out_ref):
     own = advanced(count_ref, own_ref, high_ref, low_ref, arrived(count_ref[2], (r0, r1, r2, r3), 0))
     own_out_ref[0] = own
-    own_out_ref[1] = r0[0]
+    own_out_ref[1] = r3[0]
 
 
 def second_body(count_ref, r0, r1, r2, r3, own_ref, high_ref, low_ref, copies_ref, own_out_ref):
@@ -221,13 +222,12 @@
 
 def forward(value, step):
     ahead = (step + 1) * TILES
-    pieces = {
-        change: lax.ppermute(
+    return [
+        lax.ppermute(
             value, ROWS, [(ahead - TILES + i, ahead + (i ^ change)) for i in range(TILES)]
         )
         for change in ORDER
-    }
-    return [pieces[change] for change in range(TILES)]
+    ]
 
 
 def shards(factor_panel, right_side, inverses):

time: 87.7 us -> 88.2 us (level)
  blocking collectives: 28 us -> 28.9 us
    all_to_all x1, blocking collectives: 14.8 us -> 16.5 us  [shards(): tiles = lax.all_to_all(copies, OWNERS, 0, 0)]
  transfers between devices with their start and end apart: 11 -> 11, of which waited for: 1 -> 1; matrix products, arithmetic and copies ran while one was open for 0% -> 0% of each run, Pallas kernels for 7% -> 6%
where the time goes in v8:
time: 88.2 us; the launch traced here: 87.6 us
  blocking collectives  28.9 us (33%)
  starting transfers between devices  24.2 us (27%)
  local copies, waits for them, and re-layouts  15.4 us (17%)
  Pallas kernels  10.9 us (12%)
  waiting for transfers between devices  6.64 us (8%)
  between operations  0.9 us (1%)
    all_to_all x1, blocking collectives, shards(): tiles = lax.all_to_all(copies, OWNERS, 0, 0)  16.5 us
    ppermute x8, starting transfers between devices, forward(): lax.ppermute(value, ROWS, [(ahead - TILES + i, ahead + (i ^ change)) for...  16.2 us
    unnamed x16, local copies, waits for them, and re-layouts  15.4 us
    all_to_all x1, blocking collectives, shards(): sums = jnp.sum(lax.all_to_all(sums, MEM, 0, 0), axis=0)  12.3 us
    pallas_call x6, Pallas kernels, local(): pl.pallas_call(body, out_shape=outs, in_specs=smem + [VMEM] * (len(args)...  9.38 us
    all_to_all x1, waiting for transfers between devices, shards(): received = lax.all_to_all(copies, OWNERS, 0, 0)  6.6 us
    all_to_all x1, starting transfers between devices, shards(): received = lax.all_to_all(copies, OWNERS, 0, 0)  5.46 us
    ppermute x2, starting transfers between devices, crossings(): return [lax.ppermute(value, ROWS[:2], [(0, 3), (1, 2)])]  2.58 us
  transfers between devices with their start and end apart: 11, of which 1 were waited for; matrix products, arithmetic and copies ran while one was open for 0% of the time, Pallas kernels for 6%

profile of v8, /device:TPU:1, one launch (start us, length us, event | category | flops | bytes accessed | tf_op | source)
XLA Modules:
  0.0 87.6 jit_solution(12555455096076506154)
XLA Ops:
  0.7 0.1 pad_add_fusion.count_ref
  0.7 0.0 copy-start.6
  0.7 0.9 %copy-done.6 = f32[8,1,128,32]{2,3,1,0:T(8,128)S(1)} copy-done((f32[8,1,128,32]{2,3,1,0:T(8,128)S(1)}, f32[8,1,128,32]{2,3,1,0:T(8,128)}, u32[]{:S(2)}) %copy-start.6) | copy-done | bytes 131096
  1.6 9.6 %collective-permute-start.3 = (f32[1,32,128]{2,1,0:T(8,128)S(1)}, f32[1,32,128]{2,1,0:T(8,128)S(1)}, u32[]{:S(2)}, u32[]{:S(2)}) collective-permute-start(f32[1,32,128]{2,1,0:T(8,128)S(1)} %bitcast.20), channel_id=1, source_target_pairs={{0,32},{8,40},{16,48},{24,56},{1,33},{9,41},{17,49},{25,57},{2,34}... | collective-permute-start | bytes 49160 | tf_op jit(solution)/shard_map/ppermute | solution.py:226
  11.3 1.3 %collective-permute-start.2 = (f32[1,32,128]{2,1,0:T(8,128)S(1)}, f32[1,32,128]{2,1,0:T(8,128)S(1)}, u32[]{:S(2)}, u32[]{:S(2)}) collective-permute-start(f32[1,32,128]{2,1,0:T(8,128)S(1)} %bitcast.21), channel_id=1, source_target_pairs={{0,40},{8,32},{16,56},{24,48},{1,41},{9,33},{17,57},{25,49},{2,42}... | collective-permute-start | bytes 49160 | tf_op jit(solution)/shard_map/ppermute | solution.py:226
  12.6 1.3 %collective-permute-start.1 = (f32[1,32,128]{2,1,0:T(8,128)S(1)}, f32[1,32,128]{2,1,0:T(8,128)S(1)}, u32[]{:S(2)}, u32[]{:S(2)}) collective-permute-start(f32[1,32,128]{2,1,0:T(8,128)S(1)} %bitcast.22), channel_id=1, source_target_pairs={{0,56},{8,48},{16,40},{24,32},{1,57},{9,49},{17,41},{25,33},{2,58}... | collective-permute-start | bytes 49160 | tf_op jit(solution)/shard_map/ppermute | solution.py:226
  13.9 1.3 %collective-permute-start = (f32[1,32,128]{2,1,0:T(8,128)S(1)}, f32[1,32,128]{2,1,0:T(8,128)S(1)}, u32[]{:S(2)}, u32[]{:S(2)}) collective-permute-start(f32[1,32,128]{2,1,0:T(8,128)S(1)} %bitcast.23), channel_id=1, source_target_pairs={{0,48},{8,56},{16,32},{24,40},{1,49},{9,57},{17,33},{25,41},{2,50}... | collective-permute-start | bytes 49160 | tf_op jit(solution)/shard_map/ppermute | solution.py:226
  15.2 0.0 copy-start
  15.2 3.4 %copy-done = f32[8,1,128,2048]{3,2,1,0:T(8,128)S(1)} copy-done((f32[8,1,128,2048]{3,2,1,0:T(8,128)S(1)}, f32[8,1,128,2048]{3,2,1,0:T(8,128)}, u32[]{:S(2)}) %copy-start) | copy-done | bytes 8388632
  18.5 0.0 copy-start.3
  18.6 2.2 %copy-done.3 = f32[4,512,512]{2,1,0:T(8,128)S(1)} copy-done((f32[4,512,512]{2,1,0:T(8,128)S(1)}, f32[4,512,512]{2,1,0:T(8,128)}, u32[]{:S(2)}) %copy-start.3) | copy-done | bytes 4194328
  20.7 1.5 %prepare.1 = (bf16[128,1536]{1,0:T(8,128)(2,1)S(1)}, bf16[128,1536]{1,0:T(8,128)(2,1)S(1)}) custom-call(f32[8,128,2048]{2,1,0:T(8,128)S(1)} %bitcast.15, f32[4,512,512]{2,1,0:T(8,128)S(1)} %copy-done.3), custom_call_target="tpu_custom_call" | custom-call | flops 1073741824 | bytes 4194304 | tf_op jit(solution)/shard_map/prepare/pallas_call | solution.py:99
  22.2 0.0 collective-permute-done.3.r3
  22.2 0.0 collective-permute-done.2.r2
  22.2 0.0 collective-permute-done.1.r1
  22.3 0.0 collective-permute-done.r0
  22.3 0.0 copy-start.7
  22.3 0.7 shard_map.59.own_ref
  23.0 0.7 collective-permute-start.7
  23.7 0.7 collective-permute-start.6
  24.4 0.7 collective-permute-start.5
  25.0 0.7 collective-permute-start.4
  25.7 0.0 collective-permute-done.7.r3
  25.7 0.0 collective-permute-done.6.r2
  25.7 0.0 collective-permute-done.5.r1
  25.7 0.0 collective-permute-done.4.r0
  25.7 0.8 shard_map.60
  26.6 16.5 %all_to_all.15.tiles_ref = f32[16,32,128]{2,1,0:T(8,128)S(1)} all-to-all(f32[16,32,128]{2,1,0:T(8,128)S(1)} %get-tuple-element.25), channel_id=1, replica_groups=mesh['xh'=2,'xl'=2,'zh'=2,'zl'=4,'y'=4,'core'=2] {'xl','zh','zl'}, dimensions={0} | all-to-all | bytes 524288 | tf_op jit(solution)/shard_map/all_to_all | solution.py:257
  43.1 1.6 %shard_map.61 = (f32[16,32,128]{2,1,0:T(8,128)}, f32[32,128]{1,0:T(8,128)S(1)}, f32[12,32,128]{2,1,0:T(8,128)S(1)}) custom-call(s32[3]{0:T(128)S(1)} %pad_add_fusion.count_ref, f32[16,32,128]{2,1,0:T(8,128)S(1)} %all_to_all.15.tiles_ref, f32[32,128]{1,0:T(8,128)S(1)} %get-tuple-element.26.own_ref, bf16[128,1536]{1,0:T(8,128)(2,1)S(1)} %get-tuple-element.23.high_ref, ...), custom_call_target="tpu_custom_call" | custom-call | flops 134217728 | bytes 2097152 | tf_op jit(solution)/shard_map/pallas_call | solution.py:213
  44.7 5.5 %all-to-all-start.1 = ((f32[16,32,128]{2,1,0:T(8,128)}), f32[16,32,128]{2,1,0:T(8,128)S(1)}, u32[]{:S(2)}, u32[]{:S(2)}) async-start(f32[16,32,128]{2,1,0:T(8,128)} %get-tuple-element.28), calls=%async_computation.1 | async-start | bytes 524288 | tf_op jit(solution)/shard_map/all_to_all | solution.py:263
  50.2 1.3 %collective-permute-start.8 = (f32[12,32,128]{2,1,0:T(8,128)S(1)}, f32[12,32,128]{2,1,0:T(8,128)S(1)}, u32[]{:S(2)}, u32[]{:S(2)}) collective-permute-start(f32[12,32,128]{2,1,0:T(8,128)S(1)} %get-tuple-element.32.refs_0_), channel_id=1, source_target_pairs={{0,192},{64,128},{1,193},{65,129},{2,194},{66,130},{3,195},{67,131... | collective-permute-start | bytes 589832 | tf_op jit(solution)/shard_map/ppermute | solution.py:30
  51.5 6.6 %all-to-all-done.1 = f32[16,32,128]{2,1,0:T(8,128)S(1)} async-done(((f32[16,32,128]{2,1,0:T(8,128)}), f32[16,32,128]{2,1,0:T(8,128)S(1)}, u32[]{:S(2)}, u32[]{:S(2)}) %all-to-all-start.1) | async-done | bytes 262176 | tf_op jit(solution)/shard_map/all_to_all | solution.py:263
  58.1 1.3 %collective-permute-start.9 = (f32[4,32,128]{2,1,0:T(8,128)S(1)}, f32[4,32,128]{2,1,0:T(8,128)S(1)}, u32[]{:S(2)}, u32[]{:S(2)}) collective-permute-start(f32[4,32,128]{2,1,0:T(8,128)S(1)} %slice.12.refs_0_), channel_id=1, source_target_pairs={{0,192},{64,128},{1,193},{65,129},{2,194},{66,130},{3,195},{67,131... | collective-permute-start | bytes 196616 | tf_op jit(solution)/shard_map/ppermute | solution.py:30
  59.4 0.0 collective-permute-done.8.refs_1_
  59.4 0.0 copy-done.7
  59.4 0.0 copy-start.1
  59.5 3.4 %copy-done.1 = f32[8,1,128,2048]{3,2,1,0:T(8,128)S(1)} copy-done((f32[8,1,128,2048]{3,2,1,0:T(8,128)S(1)}, f32[8,1,128,2048]{3,2,1,0:T(8,128)}, u32[]{:S(2)}) %copy-start.1) | copy-done | bytes 8388632
  62.8 0.0 copy-start.4
  62.8 2.2 %copy-done.4 = f32[4,512,512]{2,1,0:T(8,128)S(1)} copy-done((f32[4,512,512]{2,1,0:T(8,128)S(1)}, f32[4,512,512]{2,1,0:T(8,128)}, u32[]{:S(2)}) %copy-start.4) | copy-done | bytes 4194328
  65.0 0.0 copy-start.5
  65.0 3.7 %shard_map.62 = (f32[32,1536]{1,0:T(8,128)S(1)}, f32[8,32,128]{2,1,0:T(8,128)S(1)}) custom-call(s32[3]{0:T(128)S(1)} %pad_add_fusion.count_ref, f32[12,32,128]{2,1,0:T(8,128)S(1)} %get-tuple-element.32.refs_0_, f32[12,32,128]{2,1,0:T(8,128)S(1)} %collective-permute-done.8.refs_1_, f32[8,32,128]{2,1,0:T(8,128)S(1)} %bitcast.19, f32[8,128,2048]{2,1,0:T(8,128)S(1)} %bitcast.16, ...), custom_call_target="tpu_custom_call" | custom-call | flops 1073741824 | bytes 12582912 | tf_op jit(solution)/shard_map/pallas_call | solution.py:213
  68.8 0.0 collective-permute-done.9.refs_1_
  68.8 0.0 copy-done.5
  68.8 0.0 copy-start.2
  68.8 3.4 %copy-done.2 = f32[8,1,128,2048]{3,2,1,0:T(8,128)S(1)} copy-done((f32[8,1,128,2048]{3,2,1,0:T(8,128)S(1)}, f32[8,1,128,2048]{3,2,1,0:T(8,128)}, u32[]{:S(2)}) %copy-start.2) | copy-done | bytes 8388632
  72.2 2.4 %shard_map.63 = (f32[32,2048]{1,0:T(8,128)}, f32[8,32,128]{2,1,0:T(8,128)}, f32[8,2,8,128]{3,2,1,0:T(8,128)S(1)}) custom-call(s32[3]{0:T(128)S(1)} %pad_add_fusion.count_ref, f32[4,32,128]{2,1,0:T(8,128)S(1)} %slice.12.refs_0_, f32[4,32,128]{2,1,0:T(8,128)S(1)} %collective-permute-done.9.refs_1_, f32[32,128]{1,0:T(8,128)S(1)} %get-tuple-element.31.refs_2_, ...), custom_call_target="tpu_custom_call" | custom-call | flops 268435456 | bytes 4194304 | tf_op jit(solution)/shard_map/pallas_call | solution.py:213
  74.6 12.3 %all_to_all.16 = f32[8,2,8,128]{3,2,1,0:T(8,128)S(1)} all-to-all(f32[8,2,8,128]{3,2,1,0:T(8,128)S(1)} %get-tuple-element.38), channel_id=1, replica_groups=mesh['xh'=2,'xl'=2,'zh'=2,'zl'=4,'y'=4,'core'=2] {'y','core'}, dimensions={0} | all-to-all | bytes 131072 | tf_op jit(solution)/shard_map/all_to_all | solution.py:277
  87.0 0.6 fusion.1
  (3 shorter events, 0.0 us)
Async XLA Ops:
  0.7 0.9 %copy-start.6 = (f32[8,1,128,32]{2,3,1,0:T(8,128)S(1)}, f32[8,1,128,32]{2,3,1,0:T(8,128)}, u32[]{:S(2)}) copy-start(f32[8,1,128,32]{2,3,1,0:T(8,128)} %param.4) | copy-start | bytes 393220
  1.6 20.6 %collective-permute-start.3 = (f32[1,32,128]{2,1,0:T(8,128)S(1)}, f32[1,32,128]{2,1,0:T(8,128)S(1)}, u32[]{:S(2)}, u32[]{:S(2)}) collective-permute-start(f32[1,32,128]{2,1,0:T(8,128)S(1)} %bitcast.20), channel_id=1, source_target_pairs={{0,32},{8,40},{16,48},{24,56},{1,33},{9,41},{17,49},{25,57},{2,34}... | collective-permute-start | bytes 49160 | tf_op jit(solution)/shard_map/ppermute | solution.py:226
  11.3 11.0 %collective-permute-start.2 = (f32[1,32,128]{2,1,0:T(8,128)S(1)}, f32[1,32,128]{2,1,0:T(8,128)S(1)}, u32[]{:S(2)}, u32[]{:S(2)}) collective-permute-start(f32[1,32,128]{2,1,0:T(8,128)S(1)} %bitcast.21), channel_id=1, source_target_pairs={{0,40},{8,32},{16,56},{24,48},{1,41},{9,33},{17,57},{25,49},{2,42}... | collective-permute-start | bytes 49160 | tf_op jit(solution)/shard_map/ppermute | solution.py:226
  12.6 9.7 %collective-permute-start.1 = (f32[1,32,128]{2,1,0:T(8,128)S(1)}, f32[1,32,128]{2,1,0:T(8,128)S(1)}, u32[]{:S(2)}, u32[]{:S(2)}) collective-permute-start(f32[1,32,128]{2,1,0:T(8,128)S(1)} %bitcast.22), channel_id=1, source_target_pairs={{0,56},{8,48},{16,40},{24,32},{1,57},{9,49},{17,41},{25,33},{2,58}... | collective-permute-start | bytes 49160 | tf_op jit(solution)/shard_map/ppermute | solution.py:226
  13.9 8.4 %collective-permute-start = (f32[1,32,128]{2,1,0:T(8,128)S(1)}, f32[1,32,128]{2,1,0:T(8,128)S(1)}, u32[]{:S(2)}, u32[]{:S(2)}) collective-permute-start(f32[1,32,128]{2,1,0:T(8,128)S(1)} %bitcast.23), channel_id=1, source_target_pairs={{0,48},{8,56},{16,32},{24,40},{1,49},{9,57},{17,33},{25,41},{2,50}... | collective-permute-start | bytes 49160 | tf_op jit(solution)/shard_map/ppermute | solution.py:226
  15.2 3.4 %copy-start = (f32[8,1,128,2048]{3,2,1,0:T(8,128)S(1)}, f32[8,1,128,2048]{3,2,1,0:T(8,128)}, u32[]{:S(2)}) copy-start(f32[8,1,128,2048]{3,2,1,0:T(8,128)} %param.3) | copy-start | bytes 25165828
  18.5 2.2 %copy-start.3 = (f32[4,512,512]{2,1,0:T(8,128)S(1)}, f32[4,512,512]{2,1,0:T(8,128)}, u32[]{:S(2)}) copy-start(f32[4,512,512]{2,1,0:T(8,128)} %refs_6_.1) | copy-start | bytes 12582916
  22.3 37.2 %copy-start.7 = (f32[8,1,128,32]{2,3,1,0:T(8,128)S(1)}, f32[8,1,128,32]{2,3,1,0:T(8,128)}, u32[]{:S(2)}) copy-start(f32[8,1,128,32]{2,3,1,0:T(8,128)} %param.4) | copy-start | bytes 393220
  23.0 2.7 %collective-permute-start.7 = (f32[2,32,128]{2,1,0:T(8,128)S(1)}, f32[2,32,128]{2,1,0:T(8,128)S(1)}, u32[]{:S(2)}, u32[]{:S(2)}) collective-permute-start(f32[2,32,128]{2,1,0:T(8,128)S(1)} %shard_map.59.own_ref), channel_id=1, source_target_pairs={{32,64},{40,72},{48,80},{56,88},{33,65},{41,73},{49,81},{57,89},{3... | collective-permute-start | bytes 98312 | tf_op jit(solution)/shard_map/ppermute | solution.py:226
  23.7 2.0 %collective-permute-start.6 = (f32[2,32,128]{2,1,0:T(8,128)S(1)}, f32[2,32,128]{2,1,0:T(8,128)S(1)}, u32[]{:S(2)}, u32[]{:S(2)}) collective-permute-start(f32[2,32,128]{2,1,0:T(8,128)S(1)} %shard_map.59.own_ref), channel_id=1, source_target_pairs={{32,72},{40,64},{48,88},{56,80},{33,73},{41,65},{49,89},{57,81},{3... | collective-permute-start | bytes 98312 | tf_op jit(solution)/shard_map/ppermute | solution.py:226
  24.4 1.4 %collective-permute-start.5 = (f32[2,32,128]{2,1,0:T(8,128)S(1)}, f32[2,32,128]{2,1,0:T(8,128)S(1)}, u32[]{:S(2)}, u32[]{:S(2)}) collective-permute-start(f32[2,32,128]{2,1,0:T(8,128)S(1)} %shard_map.59.own_ref), channel_id=1, source_target_pairs={{32,88},{40,80},{48,72},{56,64},{33,89},{41,81},{49,73},{57,65},{3... | collective-permute-start | bytes 98312 | tf_op jit(solution)/shard_map/ppermute | solution.py:226
  25.0 0.7 collective-permute-start.4
  44.7 13.4 %all-to-all-start.1 = ((f32[16,32,128]{2,1,0:T(8,128)}), f32[16,32,128]{2,1,0:T(8,128)S(1)}, u32[]{:S(2)}, u32[]{:S(2)}) async-start(f32[16,32,128]{2,1,0:T(8,128)} %get-tuple-element.28), calls=%async_computation.1 | async-start | bytes 524288 | tf_op jit(solution)/shard_map/all_to_all | solution.py:263
  50.2 9.2 %collective-permute-start.8 = (f32[12,32,128]{2,1,0:T(8,128)S(1)}, f32[12,32,128]{2,1,0:T(8,128)S(1)}, u32[]{:S(2)}, u32[]{:S(2)}) collective-permute-start(f32[12,32,128]{2,1,0:T(8,128)S(1)} %get-tuple-element.32.refs_0_), channel_id=1, source_target_pairs={{0,192},{64,128},{1,193},{65,129},{2,194},{66,130},{3,195},{67,131... | collective-permute-start | bytes 589832 | tf_op jit(solution)/shard_map/ppermute | solution.py:30
  58.1 10.6 %collective-permute-start.9 = (f32[4,32,128]{2,1,0:T(8,128)S(1)}, f32[4,32,128]{2,1,0:T(8,128)S(1)}, u32[]{:S(2)}, u32[]{:S(2)}) collective-permute-start(f32[4,32,128]{2,1,0:T(8,128)S(1)} %slice.12.refs_0_), channel_id=1, source_target_pairs={{0,192},{64,128},{1,193},{65,129},{2,194},{66,130},{3,195},{67,131... | collective-permute-start | bytes 196616 | tf_op jit(solution)/shard_map/ppermute | solution.py:30
  59.4 3.4 %copy-start.1 = (f32[8,1,128,2048]{3,2,1,0:T(8,128)S(1)}, f32[8,1,128,2048]{3,2,1,0:T(8,128)}, u32[]{:S(2)}) copy-start(f32[8,1,128,2048]{3,2,1,0:T(8,128)} %param.3) | copy-start | bytes 25165828
  62.8 2.2 %copy-start.4 = (f32[4,512,512]{2,1,0:T(8,128)S(1)}, f32[4,512,512]{2,1,0:T(8,128)}, u32[]{:S(2)}) copy-start(f32[4,512,512]{2,1,0:T(8,128)} %refs_6_.1) | copy-start | bytes 12582916
  65.0 3.8 %copy-start.5 = (f32[4,512,512]{2,1,0:T(8,128)S(1)}, f32[4,512,512]{2,1,0:T(8,128)}, u32[]{:S(2)}) copy-start(f32[4,512,512]{2,1,0:T(8,128)} %refs_6_.1) | copy-start | bytes 12582916
  68.8 3.4 %copy-start.2 = (f32[8,1,128,2048]{3,2,1,0:T(8,128)S(1)}, f32[8,1,128,2048]{3,2,1,0:T(8,128)}, u32[]{:S(2)}) copy-start(f32[8,1,128,2048]{3,2,1,0:T(8,128)} %param.3) | copy-start | bytes 25165828

commit v9 on v8

--- a/solution.py
+++ b/solution.py
@@ -26,8 +26,12 @@
     return lax.axis_index("xh")
 
 
-def crossings(value):
-    return [lax.ppermute(value, ROWS[:2], [(0, 3), (1, 2)])]
+EARLY = [(0, 2), (1, 3)]
+LATE = [(0, 3), (1, 2)]
+
+
+def crossings(value, pairs):
+    return [lax.ppermute(value, ROWS[:2], pairs)]
 
 
 def split(value):
@@ -173,23 +177,20 @@
 
 def finish_body(count_ref, *refs):
     sources = refs[:SOURCES]
-    own_ref, partly_ref, before_ref, panel_ref, inverses_ref = refs[SOURCES:SOURCES + 5]
-    solved_ref, left_ref, sums_ref = refs[-3:]
+    own_ref, partly_ref, panel_ref, inverses_ref = refs[SOURCES:SOURCES + 4]
+    solved_ref, low_ref, high_ref, sums_ref = refs[-4:]
     step = STEPS - 1
     solved = times_split(chosen(count_ref[1], sources, 0), inverses_ref[step])
-    solved_ref[:, :step * WIDTH] = before_ref[...]
-    solved_ref[:, step * WIDTH:] = solved
+    solved_ref[...] = solved
     for block in range(partly_ref.shape[0]):
         product = times_split(solved, panel_ref[block, :, step * WIDTH:])
         left = partly_ref[block] - product
         if block == 0:
             left = jnp.where(count_ref[0] >= 0, own_ref[...], left)
-        left_ref[block] = left
-        total = jnp.sum(left, axis=0, keepdims=True)
-        square = jnp.sum(left * left, axis=0, keepdims=True)
-        for i in range(8):
-            sums_ref[i, 0, block:block + 1] = total
-            sums_ref[i, 1, block:block + 1] = square
+        half = low_ref if 2 * block < partly_ref.shape[0] else high_ref
+        half[block % half.shape[0]] = left
+        sums_ref[0, block:block + 1] = jnp.sum(left, axis=0, keepdims=True)
+        sums_ref[1, block:block + 1] = jnp.sum(left * left, axis=0, keepdims=True)
 
 
 VMEM = pl.BlockSpec(memory_space=pltpu.VMEM)
@@ -222,12 +223,12 @@
 
 def forward(value, step):
     ahead = (step + 1) * TILES
-    return [
-        lax.ppermute(
+    pieces = []
+    for change in ORDER:
+        pieces.append(lax.ppermute(
             value, ROWS, [(ahead - TILES + i, ahead + (i ^ change)) for i in range(TILES)]
-        )
-        for change in ORDER
-    ]
+        ))
+    return pieces
 
 
 def shards(factor_panel, right_side, inverses):
@@ -259,22 +260,28 @@
         third_body, 8, [group, tile, shape(3 * TILES, members, rows)],
         1 << 27, 2 << 20, count, tiles, own, *factor,
     )
-    early = crossings(packed)
+    early = crossings(packed, EARLY)
     received = lax.all_to_all(copies, OWNERS, 0, 0)
     ends = received[(STEPS - 1) * TILES:]
-    late = crossings(ends)
+    late = crossings(ends, LATE)
     own, ends, *early = lax.optimization_barrier((own, ends, packed, *early))
     before, partly = local(
         middle_body, 16,
         [shape(members, (STEPS - 1) * WIDTH), shape(blocks, members, rows)],
         1 << 30, 12 << 20, count, *early, right, panel, inverses,
     )
-    solved, left, sums = local(
+    last, low, high, sums = local(
         finish_body, 16,
-        [shape(members, STEPS * WIDTH), shape(blocks, members, rows), shape(8, 2, blocks, rows)],
-        1 << 28, 4 << 20, count, ends, *late, own, partly, before, panel, inverses,
-    )
-    sums = jnp.sum(lax.all_to_all(sums, MEM, 0, 0), axis=0)
+        [shape(members, WIDTH)] + [shape(blocks // 2, members, rows)] * 2 + [shape(2, blocks, rows)],
+        1 << 28, 4 << 20, count, ends, *late, own, partly, panel, inverses,
+    )
+    sums = sums + lax.ppermute(sums, "core", [(0, 1), (1, 0)])
+    others = [
+        lax.ppermute(sums, "y", [(i, i ^ change) for i in range(4)]) for change in (1, 2, 3)
+    ]
+    sums = sums + others[0] + (others[1] + others[2])
+    solved = jnp.concatenate([before, last], axis=1)
+    left = jnp.concatenate([low, high], axis=0)
     size = members * 8
     mean = sums[0] / size
     spread = sums[1] / size - mean * mean

time: 88.2 us -> 86.4 us (0.980)
  blocking collectives: 28.9 us -> 16.5 us
  starting transfers between devices: 24.2 us -> 30.8 us
  waiting for transfers between devices: 6.64 us -> 9.51 us
  other arithmetic: 0.68 us -> 2.07 us
    all_to_all x1 -> x0, blocking collectives: 12.3 us -> none  [shards(): sums = jnp.sum(lax.all_to_all(sums, MEM, 0, 0), axis=0)]
    ppermute x2 -> x6, starting transfers between devices: 2.58 us -> 9.22 us  [the longest x1 3.32 us: shards(): sums = sums + lax.ppermute(sums, 'core', [(0, 1), (1, 0)])]
    ppermute x2 -> x6, waiting for transfers between devices: 0.02 us -> 2.89 us  [the longest x3 2.76 us: shards(): lax.ppermute(sums, 'y', [(i, i ^ change) for i in range(4)])]
  transfers between devices with their start and end apart: 11 -> 15, of which waited for: 1 -> 3; matrix products, arithmetic and copies ran while one was open for 0% -> 2% of each run, Pallas kernels for 6% -> 6%
where the time goes in v9:
time: 86.4 us; the launch traced here: 85.5 us
  starting transfers between devices  30.8 us (36%)
  blocking collectives  16.5 us (19%)
  local copies, waits for them, and re-layouts  15.4 us (18%)
  Pallas kernels  10.2 us (12%)
  waiting for transfers between devices  9.51 us (11%)
  other arithmetic  2.07 us (2%)
  between operations  0.92 us (1%)
    all_to_all x1, blocking collectives, shards(): tiles = lax.all_to_all(copies, OWNERS, 0, 0)  16.5 us
    ppermute x8, starting transfers between devices, forward(): lax.ppermute(value, ROWS, [(ahead - TILES + i, ahead + (i ^ change)) for...  16.2 us
    unnamed x16, local copies, waits for them, and re-layouts  15.4 us
    pallas_call x6, Pallas kernels, local(): pl.pallas_call(body, out_shape=outs, in_specs=smem + [VMEM] * (len(args)...  8.73 us
    all_to_all x1, waiting for transfers between devices, shards(): received = lax.all_to_all(copies, OWNERS, 0, 0)  6.6 us
    all_to_all x1, starting transfers between devices, shards(): received = lax.all_to_all(copies, OWNERS, 0, 0)  5.46 us
    ppermute x1, starting transfers between devices, shards(): sums = sums + lax.ppermute(sums, 'core', [(0, 1), (1, 0)])  3.32 us
    ppermute x3, starting transfers between devices, shards(): lax.ppermute(sums, 'y', [(i, i ^ change) for i in range(4)])  3.32 us
  transfers between devices with their start and end apart: 15, of which 3 were waited for; matrix products, arithmetic and copies ran while one was open for 2% of the time, Pallas kernels for 6%

profile of v9, /device:TPU:1, one launch (start us, length us, event | category | flops | bytes accessed | tf_op | source)
XLA Modules:
  0.0 85.5 jit_solution(12518961668577321090)
XLA Ops:
  0.7 0.1 pad_add_fusion.count_ref
  0.7 0.0 copy-start.6
  0.7 0.9 %copy-done.6 = f32[8,1,128,32]{2,3,1,0:T(8,128)S(1)} copy-done((f32[8,1,128,32]{2,3,1,0:T(8,128)S(1)}, f32[8,1,128,32]{2,3,1,0:T(8,128)}, u32[]{:S(2)}) %copy-start.6) | copy-done | bytes 131096
  1.6 9.6 %collective-permute-start.3 = (f32[1,32,128]{2,1,0:T(8,128)S(1)}, f32[1,32,128]{2,1,0:T(8,128)S(1)}, u32[]{:S(2)}, u32[]{:S(2)}) collective-permute-start(f32[1,32,128]{2,1,0:T(8,128)S(1)} %bitcast.24), channel_id=1, source_target_pairs={{0,32},{8,40},{16,48},{24,56},{1,33},{9,41},{17,49},{25,57},{2,34}... | collective-permute-start | bytes 49160 | tf_op jit(solution)/shard_map/ppermute | solution.py:228
  11.3 1.3 %collective-permute-start.2 = (f32[1,32,128]{2,1,0:T(8,128)S(1)}, f32[1,32,128]{2,1,0:T(8,128)S(1)}, u32[]{:S(2)}, u32[]{:S(2)}) collective-permute-start(f32[1,32,128]{2,1,0:T(8,128)S(1)} %bitcast.25), channel_id=1, source_target_pairs={{0,40},{8,32},{16,56},{24,48},{1,41},{9,33},{17,57},{25,49},{2,42}... | collective-permute-start | bytes 49160 | tf_op jit(solution)/shard_map/ppermute | solution.py:228
  12.6 1.3 %collective-permute-start.1 = (f32[1,32,128]{2,1,0:T(8,128)S(1)}, f32[1,32,128]{2,1,0:T(8,128)S(1)}, u32[]{:S(2)}, u32[]{:S(2)}) collective-permute-start(f32[1,32,128]{2,1,0:T(8,128)S(1)} %bitcast.26), channel_id=1, source_target_pairs={{0,56},{8,48},{16,40},{24,32},{1,57},{9,49},{17,41},{25,33},{2,58}... | collective-permute-start | bytes 49160 | tf_op jit(solution)/shard_map/ppermute | solution.py:228
  13.9 1.3 %collective-permute-start = (f32[1,32,128]{2,1,0:T(8,128)S(1)}, f32[1,32,128]{2,1,0:T(8,128)S(1)}, u32[]{:S(2)}, u32[]{:S(2)}) collective-permute-start(f32[1,32,128]{2,1,0:T(8,128)S(1)} %bitcast.27), channel_id=1, source_target_pairs={{0,48},{8,56},{16,32},{24,40},{1,49},{9,57},{17,33},{25,41},{2,50}... | collective-permute-start | bytes 49160 | tf_op jit(solution)/shard_map/ppermute | solution.py:228
  15.2 0.0 copy-start
  15.2 3.4 %copy-done = f32[8,1,128,2048]{3,2,1,0:T(8,128)S(1)} copy-done((f32[8,1,128,2048]{3,2,1,0:T(8,128)S(1)}, f32[8,1,128,2048]{3,2,1,0:T(8,128)}, u32[]{:S(2)}) %copy-start) | copy-done | bytes 8388632
  18.5 0.0 copy-start.3
  18.6 2.2 %copy-done.3 = f32[4,512,512]{2,1,0:T(8,128)S(1)} copy-done((f32[4,512,512]{2,1,0:T(8,128)S(1)}, f32[4,512,512]{2,1,0:T(8,128)}, u32[]{:S(2)}) %copy-start.3) | copy-done | bytes 4194328
  20.7 1.5 %prepare.1 = (bf16[128,1536]{1,0:T(8,128)(2,1)S(1)}, bf16[128,1536]{1,0:T(8,128)(2,1)S(1)}) custom-call(f32[8,128,2048]{2,1,0:T(8,128)S(1)} %bitcast.19, f32[4,512,512]{2,1,0:T(8,128)S(1)} %copy-done.3), custom_call_target="tpu_custom_call" | custom-call | flops 1073741824 | bytes 4194304 | tf_op jit(solution)/shard_map/prepare/pallas_call | solution.py:103
  22.2 0.0 collective-permute-done.3.r3
  22.2 0.0 collective-permute-done.2.r2
  22.2 0.0 collective-permute-done.1.r1
  22.3 0.0 collective-permute-done.r0
  22.3 0.0 copy-start.7
  22.3 0.7 shard_map.59.own_ref
  23.0 0.7 collective-permute-start.7
  23.7 0.7 collective-permute-start.6
  24.4 0.7 collective-permute-start.5
  25.0 0.7 collective-permute-start.4
  25.7 0.0 collective-permute-done.7.r3
  25.7 0.0 collective-permute-done.6.r2
  25.7 0.0 collective-permute-done.5.r1
  25.7 0.0 collective-permute-done.4.r0
  25.7 0.8 shard_map.60
  26.6 16.5 %all_to_all.10.tiles_ref = f32[16,32,128]{2,1,0:T(8,128)S(1)} all-to-all(f32[16,32,128]{2,1,0:T(8,128)S(1)} %get-tuple-element.26), channel_id=1, replica_groups=mesh['xh'=2,'xl'=2,'zh'=2,'zl'=4,'y'=4,'core'=2] {'xl','zh','zl'}, dimensions={0} | all-to-all | bytes 524288 | tf_op jit(solution)/shard_map/all_to_all | solution.py:258
  43.1 1.6 %shard_map.61 = (f32[16,32,128]{2,1,0:T(8,128)}, f32[32,128]{1,0:T(8,128)S(1)}, f32[12,32,128]{2,1,0:T(8,128)S(1)}) custom-call(s32[3]{0:T(128)S(1)} %pad_add_fusion.count_ref, f32[16,32,128]{2,1,0:T(8,128)S(1)} %all_to_all.10.tiles_ref, f32[32,128]{1,0:T(8,128)S(1)} %get-tuple-element.27.own_ref, bf16[128,1536]{1,0:T(8,128)(2,1)S(1)} %get-tuple-element.24.high_ref, ...), custom_call_target="tpu_custom_call" | custom-call | flops 134217728 | bytes 2097152 | tf_op jit(solution)/shard_map/pallas_call | solution.py:214
  44.7 5.5 %all-to-all-start.1 = ((f32[16,32,128]{2,1,0:T(8,128)}), f32[16,32,128]{2,1,0:T(8,128)S(1)}, u32[]{:S(2)}, u32[]{:S(2)}) async-start(f32[16,32,128]{2,1,0:T(8,128)} %get-tuple-element.29), calls=%async_computation.1 | async-start | bytes 524288 | tf_op jit(solution)/shard_map/all_to_all | solution.py:264
  50.2 1.3 %collective-permute-start.8 = (f32[12,32,128]{2,1,0:T(8,128)S(1)}, f32[12,32,128]{2,1,0:T(8,128)S(1)}, u32[]{:S(2)}, u32[]{:S(2)}) collective-permute-start(f32[12,32,128]{2,1,0:T(8,128)S(1)} %get-tuple-element.31.refs_0_), channel_id=1, source_target_pairs={{0,128},{64,192},{1,129},{65,193},{2,130},{66,194},{3,131},{67,195... | collective-permute-start | bytes 589832 | tf_op jit(solution)/shard_map/ppermute | solution.py:34
  51.5 6.6 %all-to-all-done.1 = f32[16,32,128]{2,1,0:T(8,128)S(1)} async-done(((f32[16,32,128]{2,1,0:T(8,128)}), f32[16,32,128]{2,1,0:T(8,128)S(1)}, u32[]{:S(2)}, u32[]{:S(2)}) %all-to-all-start.1) | async-done | bytes 262176 | tf_op jit(solution)/shard_map/all_to_all | solution.py:264
  58.1 1.3 %collective-permute-start.9 = (f32[4,32,128]{2,1,0:T(8,128)S(1)}, f32[4,32,128]{2,1,0:T(8,128)S(1)}, u32[]{:S(2)}, u32[]{:S(2)}) collective-permute-start(f32[4,32,128]{2,1,0:T(8,128)S(1)} %slice.12.refs_0_), channel_id=1, source_target_pairs={{0,192},{64,128},{1,193},{65,129},{2,194},{66,130},{3,195},{67,131... | collective-permute-start | bytes 196616 | tf_op jit(solution)/shard_map/ppermute | solution.py:34
  59.4 0.0 collective-permute-done.8.refs_1_
  59.4 0.0 copy-done.7
  59.4 0.0 copy-start.1
  59.5 3.4 %copy-done.1 = f32[8,1,128,2048]{3,2,1,0:T(8,128)S(1)} copy-done((f32[8,1,128,2048]{3,2,1,0:T(8,128)S(1)}, f32[8,1,128,2048]{3,2,1,0:T(8,128)}, u32[]{:S(2)}) %copy-start.1) | copy-done | bytes 8388632
  62.8 0.0 copy-start.4
  62.8 2.2 %copy-done.4 = f32[4,512,512]{2,1,0:T(8,128)S(1)} copy-done((f32[4,512,512]{2,1,0:T(8,128)S(1)}, f32[4,512,512]{2,1,0:T(8,128)}, u32[]{:S(2)}) %copy-start.4) | copy-done | bytes 4194328
  65.0 0.0 copy-start.5
  65.0 3.7 %shard_map.62 = (f32[32,1536]{1,0:T(8,128)S(1)}, f32[8,32,128]{2,1,0:T(8,128)S(1)}) custom-call(s32[3]{0:T(128)S(1)} %pad_add_fusion.count_ref, f32[12,32,128]{2,1,0:T(8,128)S(1)} %get-tuple-element.31.refs_0_, f32[12,32,128]{2,1,0:T(8,128)S(1)} %collective-permute-done.8.refs_1_, f32[8,32,128]{2,1,0:T(8,128)S(1)} %bitcast.23, f32[8,128,2048]{2,1,0:T(8,128)S(1)} %bitcast.20, ...), custom_call_target="tpu_custom_call" | custom-call | flops 1073741824 | bytes 12582912 | tf_op jit(solution)/shard_map/pallas_call | solution.py:214
  68.8 0.0 collective-permute-done.9.refs_1_
  68.8 0.0 copy-done.5
  68.8 0.0 copy-start.2
  68.8 3.4 %copy-done.2 = f32[8,1,128,2048]{3,2,1,0:T(8,128)S(1)} copy-done((f32[8,1,128,2048]{3,2,1,0:T(8,128)S(1)}, f32[8,1,128,2048]{3,2,1,0:T(8,128)}, u32[]{:S(2)}) %copy-start.2) | copy-done | bytes 8388632
  72.2 1.8 %shard_map.63 = (f32[32,512]{1,0:T(8,128)S(1)}, f32[4,32,128]{2,1,0:T(8,128)S(1)}, f32[4,32,128]{2,1,0:T(8,128)S(1)}, f32[2,8,128]{2,1,0:T(8,128)S(1)}) custom-call(s32[3]{0:T(128)S(1)} %pad_add_fusion.count_ref, f32[4,32,128]{2,1,0:T(8,128)S(1)} %slice.12.refs_0_, f32[4,32,128]{2,1,0:T(8,128)S(1)} %collective-permute-done.9.refs_1_, ...), custom_call_target="tpu_custom_call" | custom-call | flops 268435456 | bytes 4194304 | tf_op jit(solution)/shard_map/pallas_call | solution.py:214
  74.0 3.3 %collective-permute-start.10 = (f32[2,8,128]{2,1,0:T(8,128)S(1)}, f32[2,8,128]{2,1,0:T(8,128)S(1)}, u32[]{:S(2)}, u32[]{:S(2)}) collective-permute-start(f32[2,8,128]{2,1,0:T(8,128)S(1)} %get-tuple-element.40), channel_id=1, source_target_pairs={{0,1},{1,0},{2,3},{3,2},{4,5},{5,4},{6,7},{7,6},{8,9},{9,8},{10,11... | collective-permute-start | bytes 24584 | tf_op jit(solution)/shard_map/ppermute | solution.py:278
  77.3 0.7 maximum_bitcast_fusion
  78.0 0.1 collective-permute-done.10
  78.1 2.7 %collective-permute-start.13 = (f32[2,8,128]{2,1,0:T(8,128)S(1)}, f32[2,8,128]{2,1,0:T(8,128)S(1)}, u32[]{:S(2)}, u32[]{:S(2)}) collective-permute-start(f32[2,8,128]{2,1,0:T(8,128)S(1)} %add.25), channel_id=1, source_target_pairs={{0,6},{2,4},{4,2},{6,0},{1,7},{3,5},{5,3},{7,1},{8,14},{10,12},{12... | collective-permute-start | bytes 24584 | tf_op jit(solution)/shard_map/ppermute | solution.py:280
  80.9 0.3 collective-permute-start.12
  81.2 0.2 collective-permute-start.11
  81.4 0.7 maximum_bitcast_fusion.1
  82.1 0.0 collective-permute-done.13
  82.1 2.8 %collective-permute-done.12 = f32[2,8,128]{2,1,0:T(8,128)S(1)} collective-permute-done((f32[2,8,128]{2,1,0:T(8,128)S(1)}, f32[2,8,128]{2,1,0:T(8,128)S(1)}, u32[]{:S(2)}, u32[]{:S(2)}) %collective-permute-start.12) | collective-permute-done | bytes 8224 | tf_op jit(solution)/shard_map/ppermute | solution.py:280
  84.9 0.0 collective-permute-done.11
  84.9 0.6 fusion.1
  (4 shorter events, 0.0 us)
Async XLA Ops:
  0.7 0.9 %copy-start.6 = (f32[8,1,128,32]{2,3,1,0:T(8,128)S(1)}, f32[8,1,128,32]{2,3,1,0:T(8,128)}, u32[]{:S(2)}) copy-start(f32[8,1,128,32]{2,3,1,0:T(8,128)} %param.4) | copy-start | bytes 393220
  1.6 20.6 %collective-permute-start.3 = (f32[1,32,128]{2,1,0:T(8,128)S(1)}, f32[1,32,128]{2,1,0:T(8,128)S(1)}, u32[]{:S(2)}, u32[]{:S(2)}) collective-permute-start(f32[1,32,128]{2,1,0:T(8,128)S(1)} %bitcast.24), channel_id=1, source_target_pairs={{0,32},{8,40},{16,48},{24,56},{1,33},{9,41},{17,49},{25,57},{2,34}... | collective-permute-start | bytes 49160 | tf_op jit(solution)/shard_map/ppermute | solution.py:228
  11.3 11.0 %collective-permute-start.2 = (f32[1,32,128]{2,1,0:T(8,128)S(1)}, f32[1,32,128]{2,1,0:T(8,128)S(1)}, u32[]{:S(2)}, u32[]{:S(2)}) collective-permute-start(f32[1,32,128]{2,1,0:T(8,128)S(1)} %bitcast.25), channel_id=1, source_target_pairs={{0,40},{8,32},{16,56},{24,48},{1,41},{9,33},{17,57},{25,49},{2,42}... | collective-permute-start | bytes 49160 | tf_op jit(solution)/shard_map/ppermute | solution.py:228
  12.6 9.7 %collective-permute-start.1 = (f32[1,32,128]{2,1,0:T(8,128)S(1)}, f32[1,32,128]{2,1,0:T(8,128)S(1)}, u32[]{:S(2)}, u32[]{:S(2)}) collective-permute-start(f32[1,32,128]{2,1,0:T(8,128)S(1)} %bitcast.26), channel_id=1, source_target_pairs={{0,56},{8,48},{16,40},{24,32},{1,57},{9,49},{17,41},{25,33},{2,58}... | collective-permute-start | bytes 49160 | tf_op jit(solution)/shard_map/ppermute | solution.py:228
  13.9 8.4 %collective-permute-start = (f32[1,32,128]{2,1,0:T(8,128)S(1)}, f32[1,32,128]{2,1,0:T(8,128)S(1)}, u32[]{:S(2)}, u32[]{:S(2)}) collective-permute-start(f32[1,32,128]{2,1,0:T(8,128)S(1)} %bitcast.27), channel_id=1, source_target_pairs={{0,48},{8,56},{16,32},{24,40},{1,49},{9,57},{17,33},{25,41},{2,50}... | collective-permute-start | bytes 49160 | tf_op jit(solution)/shard_map/ppermute | solution.py:228
  15.2 3.4 %copy-start = (f32[8,1,128,2048]{3,2,1,0:T(8,128)S(1)}, f32[8,1,128,2048]{3,2,1,0:T(8,128)}, u32[]{:S(2)}) copy-start(f32[8,1,128,2048]{3,2,1,0:T(8,128)} %param.3) | copy-start | bytes 25165828
  18.5 2.2 %copy-start.3 = (f32[4,512,512]{2,1,0:T(8,128)S(1)}, f32[4,512,512]{2,1,0:T(8,128)}, u32[]{:S(2)}) copy-start(f32[4,512,512]{2,1,0:T(8,128)} %refs_5_.1) | copy-start | bytes 12582916
  22.3 37.2 %copy-start.7 = (f32[8,1,128,32]{2,3,1,0:T(8,128)S(1)}, f32[8,1,128,32]{2,3,1,0:T(8,128)}, u32[]{:S(2)}) copy-start(f32[8,1,128,32]{2,3,1,0:T(8,128)} %param.4) | copy-start | bytes 393220
  23.0 2.7 %collective-permute-start.7 = (f32[2,32,128]{2,1,0:T(8,128)S(1)}, f32[2,32,128]{2,1,0:T(8,128)S(1)}, u32[]{:S(2)}, u32[]{:S(2)}) collective-permute-start(f32[2,32,128]{2,1,0:T(8,128)S(1)} %shard_map.59.own_ref), channel_id=1, source_target_pairs={{32,64},{40,72},{48,80},{56,88},{33,65},{41,73},{49,81},{57,89},{3... | collective-permute-start | bytes 98312 | tf_op jit(solution)/shard_map/ppermute | solution.py:228
  23.7 2.0 %collective-permute-start.6 = (f32[2,32,128]{2,1,0:T(8,128)S(1)}, f32[2,32,128]{2,1,0:T(8,128)S(1)}, u32[]{:S(2)}, u32[]{:S(2)}) collective-permute-start(f32[2,32,128]{2,1,0:T(8,128)S(1)} %shard_map.59.own_ref), channel_id=1, source_target_pairs={{32,72},{40,64},{48,88},{56,80},{33,73},{41,65},{49,89},{57,81},{3... | collective-permute-start | bytes 98312 | tf_op jit(solution)/shard_map/ppermute | solution.py:228
  24.4 1.4 %collective-permute-start.5 = (f32[2,32,128]{2,1,0:T(8,128)S(1)}, f32[2,32,128]{2,1,0:T(8,128)S(1)}, u32[]{:S(2)}, u32[]{:S(2)}) collective-permute-start(f32[2,32,128]{2,1,0:T(8,128)S(1)} %shard_map.59.own_ref), channel_id=1, source_target_pairs={{32,88},{40,80},{48,72},{56,64},{33,89},{41,81},{49,73},{57,65},{3... | collective-permute-start | bytes 98312 | tf_op jit(solution)/shard_map/ppermute | solution.py:228
  25.0 0.7 collective-permute-start.4
  44.7 13.4 %all-to-all-start.1 = ((f32[16,32,128]{2,1,0:T(8,128)}), f32[16,32,128]{2,1,0:T(8,128)S(1)}, u32[]{:S(2)}, u32[]{:S(2)}) async-start(f32[16,32,128]{2,1,0:T(8,128)} %get-tuple-element.29), calls=%async_computation.1 | async-start | bytes 524288 | tf_op jit(solution)/shard_map/all_to_all | solution.py:264
  50.2 9.2 %collective-permute-start.8 = (f32[12,32,128]{2,1,0:T(8,128)S(1)}, f32[12,32,128]{2,1,0:T(8,128)S(1)}, u32[]{:S(2)}, u32[]{:S(2)}) collective-permute-start(f32[12,32,128]{2,1,0:T(8,128)S(1)} %get-tuple-element.31.refs_0_), channel_id=1, source_target_pairs={{0,128},{64,192},{1,129},{65,193},{2,130},{66,194},{3,131},{67,195... | collective-permute-start | bytes 589832 | tf_op jit(solution)/shard_map/ppermute | solution.py:34
  58.1 10.6 %collective-permute-start.9 = (f32[4,32,128]{2,1,0:T(8,128)S(1)}, f32[4,32,128]{2,1,0:T(8,128)S(1)}, u32[]{:S(2)}, u32[]{:S(2)}) collective-permute-start(f32[4,32,128]{2,1,0:T(8,128)S(1)} %slice.12.refs_0_), channel_id=1, source_target_pairs={{0,192},{64,128},{1,193},{65,129},{2,194},{66,130},{3,195},{67,131... | collective-permute-start | bytes 196616 | tf_op jit(solution)/shard_map/ppermute | solution.py:34
  59.4 3.4 %copy-start.1 = (f32[8,1,128,2048]{3,2,1,0:T(8,128)S(1)}, f32[8,1,128,2048]{3,2,1,0:T(8,128)}, u32[]{:S(2)}) copy-start(f32[8,1,128,2048]{3,2,1,0:T(8,128)} %param.3) | copy-start | bytes 25165828
  62.8 2.2 %copy-start.4 = (f32[4,512,512]{2,1,0:T(8,128)S(1)}, f32[4,512,512]{2,1,0:T(8,128)}, u32[]{:S(2)}) copy-start(f32[4,512,512]{2,1,0:T(8,128)} %refs_5_.1) | copy-start | bytes 12582916
  65.0 3.8 %copy-start.5 = (f32[4,512,512]{2,1,0:T(8,128)S(1)}, f32[4,512,512]{2,1,0:T(8,128)}, u32[]{:S(2)}) copy-start(f32[4,512,512]{2,1,0:T(8,128)} %refs_5_.1) | copy-start | bytes 12582916
  68.8 3.4 %copy-start.2 = (f32[8,1,128,2048]{3,2,1,0:T(8,128)S(1)}, f32[8,1,128,2048]{3,2,1,0:T(8,128)}, u32[]{:S(2)}) copy-start(f32[8,1,128,2048]{3,2,1,0:T(8,128)} %param.3) | copy-start | bytes 25165828
  74.0 4.1 %collective-permute-start.10 = (f32[2,8,128]{2,1,0:T(8,128)S(1)}, f32[2,8,128]{2,1,0:T(8,128)S(1)}, u32[]{:S(2)}, u32[]{:S(2)}) collective-permute-start(f32[2,8,128]{2,1,0:T(8,128)S(1)} %get-tuple-element.40), channel_id=1, source_target_pairs={{0,1},{1,0},{2,3},{3,2},{4,5},{5,4},{6,7},{7,6},{8,9},{9,8},{10,11... | collective-permute-start | bytes 24584 | tf_op jit(solution)/shard_map/ppermute | solution.py:278
  78.1 4.0 %collective-permute-start.13 = (f32[2,8,128]{2,1,0:T(8,128)S(1)}, f32[2,8,128]{2,1,0:T(8,128)S(1)}, u32[]{:S(2)}, u32[]{:S(2)}) collective-permute-start(f32[2,8,128]{2,1,0:T(8,128)S(1)} %add.25), channel_id=1, source_target_pairs={{0,6},{2,4},{4,2},{6,0},{1,7},{3,5},{5,3},{7,1},{8,14},{10,12},{12... | collective-permute-start | bytes 24584 | tf_op jit(solution)/shard_map/ppermute | solution.py:280
  80.9 4.0 %collective-permute-start.12 = (f32[2,8,128]{2,1,0:T(8,128)S(1)}, f32[2,8,128]{2,1,0:T(8,128)S(1)}, u32[]{:S(2)}, u32[]{:S(2)}) collective-permute-start(f32[2,8,128]{2,1,0:T(8,128)S(1)} %add.25), channel_id=1, source_target_pairs={{0,4},{2,6},{4,0},{6,2},{1,5},{3,7},{5,1},{7,3},{8,12},{10,14},{12... | collective-permute-start | bytes 24584 | tf_op jit(solution)/shard_map/ppermute | solution.py:280
  81.2 3.7 %collective-permute-start.11 = (f32[2,8,128]{2,1,0:T(8,128)S(1)}, f32[2,8,128]{2,1,0:T(8,128)S(1)}, u32[]{:S(2)}, u32[]{:S(2)}) collective-permute-start(f32[2,8,128]{2,1,0:T(8,128)S(1)} %add.25), channel_id=1, source_target_pairs={{0,2},{2,0},{4,6},{6,4},{1,3},{3,1},{5,7},{7,5},{8,10},{10,8},{12,... | collective-permute-start | bytes 24584 | tf_op jit(solution)/shard_map/ppermute | solution.py:280

commit v10 on v9

--- a/solution.py
+++ b/solution.py
@@ -24,6 +24,10 @@
 
 def line_of():
     return lax.axis_index("xh")
+
+
+def step_of():
+    return lax.axis_index("xh") * 4 + lax.axis_index("xl") * 2 + lax.axis_index("zh")
 
 
 EARLY = [(0, 2), (1, 3)]
@@ -127,32 +131,32 @@
     return tiles
 
 
-def advanced(count_ref, own_ref, high_ref, low_ref, tiles):
+def advanced(own_ref, high_ref, low_ref, tiles):
     steps = len(tiles) // TILES
     change = times_halves(
         jnp.concatenate(tiles, axis=1), high_ref[:, :steps * WIDTH], low_ref[:, :steps * WIDTH]
     )
-    return jnp.where(count_ref[0] == steps, own_ref[...] - change, own_ref[...])
-
-
-def first_body(count_ref, r0, r1, r2, r3, own_ref, high_ref, low_ref, own_out_ref):
-    own = advanced(count_ref, own_ref, high_ref, low_ref, arrived(count_ref[2], (r0, r1, r2, r3), 0))
+    return jnp.where(step_of() == steps, own_ref[...] - change, own_ref[...])
+
+
+def first_body(r0, r1, r2, r3, own_ref, high_ref, low_ref, own_out_ref):
+    own = advanced(own_ref, high_ref, low_ref, arrived(lax.axis_index("zl"), (r0, r1, r2, r3), 0))
     own_out_ref[0] = own
     own_out_ref[1] = r3[0]
 
 
-def second_body(count_ref, r0, r1, r2, r3, own_ref, high_ref, low_ref, copies_ref, own_out_ref):
+def second_body(r0, r1, r2, r3, own_ref, high_ref, low_ref, copies_ref, own_out_ref):
     refs = (r0, r1, r2, r3)
-    tiles = arrived(count_ref[2], refs, 1) + arrived(count_ref[2], refs, 0)
-    own = advanced(count_ref, own_ref.at[0], high_ref, low_ref, tiles)
+    tiles = arrived(lax.axis_index("zl"), refs, 1) + arrived(lax.axis_index("zl"), refs, 0)
+    own = advanced(own_ref.at[0], high_ref, low_ref, tiles)
     own_out_ref[...] = own
     for i in range(GROUP):
         copies_ref[i] = own
 
 
-def third_body(count_ref, tiles_ref, own_ref, high_ref, low_ref, copies_ref, own_out_ref, packed_ref):
+def third_body(tiles_ref, own_ref, high_ref, low_ref, copies_ref, own_out_ref, packed_ref):
     tiles = [tiles_ref[i] for i in range((STEPS - 1) * TILES)]
-    own = advanced(count_ref, own_ref, high_ref, low_ref, tiles)
+    own = advanced(own_ref, high_ref, low_ref, tiles)
     own_out_ref[...] = own
     for i in range(GROUP):
         copies_ref[i] = own
@@ -160,13 +164,13 @@
         packed_ref[i] = value
 
 
-def middle_body(count_ref, *refs):
+def middle_body(*refs):
     sources = refs[:SOURCES]
     right_ref, panel_ref, inverses_ref = refs[SOURCES:SOURCES + 3]
     solved_ref, left_ref = refs[-2:]
     parts = []
     for step in range(STEPS - 1):
-        solved = times_split(chosen(count_ref[1], sources, step * TILES), inverses_ref[step])
+        solved = times_split(chosen(line_of(), sources, step * TILES), inverses_ref[step])
         solved_ref[:, step * WIDTH:(step + 1) * WIDTH] = solved
         parts.append(solved)
     solved = jnp.concatenate(parts, axis=1)
@@ -175,18 +179,18 @@
         left_ref[block] = right_ref[block] - product
 
 
-def finish_body(count_ref, *refs):
+def finish_body(*refs):
     sources = refs[:SOURCES]
     own_ref, partly_ref, panel_ref, inverses_ref = refs[SOURCES:SOURCES + 4]
     solved_ref, low_ref, high_ref, sums_ref = refs[-4:]
     step = STEPS - 1
-    solved = times_split(chosen(count_ref[1], sources, 0), inverses_ref[step])
+    solved = times_split(chosen(line_of(), sources, 0), inverses_ref[step])
     solved_ref[...] = solved
     for block in range(partly_ref.shape[0]):
         product = times_split(solved, panel_ref[block, :, step * WIDTH:])
         left = partly_ref[block] - product
         if block == 0:
-            left = jnp.where(count_ref[0] >= 0, own_ref[...], left)
+            left = jnp.where(step_of() < STEPS, own_ref[...], left)
         half = low_ref if 2 * block < partly_ref.shape[0] else high_ref
         half[block % half.shape[0]] = left
         sums_ref[0, block:block + 1] = jnp.sum(left, axis=0, keepdims=True)
@@ -194,7 +198,6 @@
 
 
 VMEM = pl.BlockSpec(memory_space=pltpu.VMEM)
-SMEM = pl.BlockSpec(memory_space=pltpu.SMEM)
 
 
 def shape(*dims):
@@ -210,11 +213,10 @@
 
 
 def local(body, limit, outs, flops, size, *args):
-    smem = [SMEM] if args[0].ndim == 1 else []
     return pl.pallas_call(
         body,
         out_shape=outs,
-        in_specs=smem + [VMEM] * (len(args) - len(smem)),
+        in_specs=[VMEM] * len(args),
         out_specs=[VMEM] * len(outs),
         compiler_params=params(limit),
         cost_estimate=cost(flops, size),
@@ -236,29 +238,22 @@
     members = right_side.shape[3]
     panel = factor_panel.reshape(blocks, rows, columns)
     right = right_side.reshape(blocks, rows, members).transpose(0, 2, 1)
-    step_of = lax.axis_index(ROWS) // TILES
-    lane = lax.axis_index("zl")
-    count = jnp.stack([jnp.where(step_of < STEPS, step_of, -1), line_of(), lane])
-    count = count.astype(jnp.int32)
     tile = shape(members, rows)
     group = shape(GROUP, members, rows)
-    right, count = lax.optimization_barrier((right, count))
 
     own, = local(begin_body, 8, [tile], 1 << 20, 1 << 20, right)
     tiles = forward(own[None], 0)
     factor = prepare(panel, inverses)
     own, = local(
         first_body, 8, [shape(2, members, rows)], 1 << 34, 1 << 20,
-        count, *tiles, own, *factor,
+        *tiles, own, *factor,
     )
     tiles = forward(own, 1)
-    copies, own = local(
-        second_body, 8, [group, tile], 1 << 27, 1 << 20, count, *tiles, own, *factor,
-    )
+    copies, own = local(second_body, 8, [group, tile], 1 << 27, 1 << 20, *tiles, own, *factor)
     tiles = lax.all_to_all(copies, OWNERS, 0, 0)
     copies, own, packed = local(
         third_body, 8, [group, tile, shape(3 * TILES, members, rows)],
-        1 << 27, 2 << 20, count, tiles, own, *factor,
+        1 << 27, 2 << 20, tiles, own, *factor,
     )
     early = crossings(packed, EARLY)
     received = lax.all_to_all(copies, OWNERS, 0, 0)
@@ -268,17 +263,17 @@
     before, partly = local(
         middle_body, 16,
         [shape(members, (STEPS - 1) * WIDTH), shape(blocks, members, rows)],
-        1 << 30, 12 << 20, count, *early, right, panel, inverses,
+        1 << 30, 12 << 20, *early, right, panel, inverses,
     )
     last, low, high, sums = local(
         finish_body, 16,
         [shape(members, WIDTH)] + [shape(blocks // 2, members, rows)] * 2 + [shape(2, blocks, rows)],
-        1 << 28, 4 << 20, count, ends, *late, own, partly, panel, inverses,
+        1 << 28, 4 << 20, ends, *late, own, partly, panel, inverses,
     )
     sums = sums + lax.ppermute(sums, "core", [(0, 1), (1, 0)])
-    others = [
-        lax.ppermute(sums, "y", [(i, i ^ change) for i in range(4)]) for change in (1, 2, 3)
-    ]
+    others = []
+    for change in (1, 2, 3):
+        others.append(lax.ppermute(sums, "y", [(i, i ^ change) for i in range(4)]))
     sums = sums + others[0] + (others[1] + others[2])
     solved = jnp.concatenate([before, last], axis=1)
     left = jnp.concatenate([low, high], axis=0)

time: 86.4 us -> 83.5 us (0.966)
  Pallas kernels: 10.2 us -> 7.47 us
    pallas_call x6, Pallas kernels: 8.73 us -> 5.99 us  [local(): pl.pallas_call(body, out_shape=outs, in_specs=[VMEM] * len(args), out_spe...]
where the time goes in v10:
time: 83.5 us; the launch traced here: 82.6 us
  starting transfers between devices  30.8 us (37%)
  blocking collectives  16.5 us (20%)
  local copies, waits for them, and re-layouts  15.4 us (18%)
  waiting for transfers between devices  9.51 us (11%)
  Pallas kernels  7.47 us (9%)
  other arithmetic  1.99 us (2%)
  between operations  0.9 us (1%)
    all_to_all x1, blocking collectives, shards(): tiles = lax.all_to_all(copies, OWNERS, 0, 0)  16.5 us
    ppermute x8, starting transfers between devices, forward(): lax.ppermute(value, ROWS, [(ahead - TILES + i, ahead + (i ^ change)) for...  16.2 us
    unnamed x16, local copies, waits for them, and re-layouts  15.4 us
    all_to_all x1, waiting for transfers between devices, shards(): received = lax.all_to_all(copies, OWNERS, 0, 0)  6.6 us
    pallas_call x6, Pallas kernels, local(): pl.pallas_call(body, out_shape=outs, in_specs=[VMEM] * len(args), out_spe...  5.99 us
    all_to_all x1, starting transfers between devices, shards(): received = lax.all_to_all(copies, OWNERS, 0, 0)  5.48 us
    ppermute x3, starting transfers between devices, shards(): others.append(lax.ppermute(sums, 'y', [(i, i ^ change) for i in range(4)]))  3.32 us
    ppermute x1, starting transfers between devices, shards(): sums = sums + lax.ppermute(sums, 'core', [(0, 1), (1, 0)])  3.31 us
  transfers between devices with their start and end apart: 15, of which 3 were waited for; matrix products, arithmetic and copies ran while one was open for 2% of the time, Pallas kernels for 6%

profile of v10, /device:TPU:1, one launch (start us, length us, event | category | flops | bytes accessed | tf_op | source)
XLA Modules:
  0.0 82.6 jit_solution(8990142307178675474)
XLA Ops:
  0.6 0.0 copy-start.6
  0.6 0.9 %copy-done.6 = f32[8,1,128,32]{2,3,1,0:T(8,128)S(1)} copy-done((f32[8,1,128,32]{2,3,1,0:T(8,128)S(1)}, f32[8,1,128,32]{2,3,1,0:T(8,128)}, u32[]{:S(2)}) %copy-start.6) | copy-done | bytes 131096
  1.5 9.6 %collective-permute-start.3 = (f32[1,32,128]{2,1,0:T(8,128)S(1)}, f32[1,32,128]{2,1,0:T(8,128)S(1)}, u32[]{:S(2)}, u32[]{:S(2)}) collective-permute-start(f32[1,32,128]{2,1,0:T(8,128)S(1)} %bitcast.21), channel_id=1, source_target_pairs={{0,32},{8,40},{16,48},{24,56},{1,33},{9,41},{17,49},{25,57},{2,34}... | collective-permute-start | bytes 49160 | tf_op jit(solution)/shard_map/ppermute | solution.py:230
  11.2 1.3 %collective-permute-start.2 = (f32[1,32,128]{2,1,0:T(8,128)S(1)}, f32[1,32,128]{2,1,0:T(8,128)S(1)}, u32[]{:S(2)}, u32[]{:S(2)}) collective-permute-start(f32[1,32,128]{2,1,0:T(8,128)S(1)} %bitcast.22), channel_id=1, source_target_pairs={{0,40},{8,32},{16,56},{24,48},{1,41},{9,33},{17,57},{25,49},{2,42}... | collective-permute-start | bytes 49160 | tf_op jit(solution)/shard_map/ppermute | solution.py:230
  12.5 1.3 %collective-permute-start.1 = (f32[1,32,128]{2,1,0:T(8,128)S(1)}, f32[1,32,128]{2,1,0:T(8,128)S(1)}, u32[]{:S(2)}, u32[]{:S(2)}) collective-permute-start(f32[1,32,128]{2,1,0:T(8,128)S(1)} %bitcast.23), channel_id=1, source_target_pairs={{0,56},{8,48},{16,40},{24,32},{1,57},{9,49},{17,41},{25,33},{2,58}... | collective-permute-start | bytes 49160 | tf_op jit(solution)/shard_map/ppermute | solution.py:230
  13.8 1.3 %collective-permute-start = (f32[1,32,128]{2,1,0:T(8,128)S(1)}, f32[1,32,128]{2,1,0:T(8,128)S(1)}, u32[]{:S(2)}, u32[]{:S(2)}) collective-permute-start(f32[1,32,128]{2,1,0:T(8,128)S(1)} %bitcast.24), channel_id=1, source_target_pairs={{0,48},{8,56},{16,32},{24,40},{1,49},{9,57},{17,33},{25,41},{2,50}... | collective-permute-start | bytes 49160 | tf_op jit(solution)/shard_map/ppermute | solution.py:230
  15.1 0.0 copy-start
  15.1 3.4 %copy-done = f32[8,1,128,2048]{3,2,1,0:T(8,128)S(1)} copy-done((f32[8,1,128,2048]{3,2,1,0:T(8,128)S(1)}, f32[8,1,128,2048]{3,2,1,0:T(8,128)}, u32[]{:S(2)}) %copy-start) | copy-done | bytes 8388632
  18.4 0.0 copy-start.3
  18.4 2.2 %copy-done.3 = f32[4,512,512]{2,1,0:T(8,128)S(1)} copy-done((f32[4,512,512]{2,1,0:T(8,128)S(1)}, f32[4,512,512]{2,1,0:T(8,128)}, u32[]{:S(2)}) %copy-start.3) | copy-done | bytes 4194328
  20.6 1.5 %prepare.1 = (bf16[128,1536]{1,0:T(8,128)(2,1)S(1)}, bf16[128,1536]{1,0:T(8,128)(2,1)S(1)}) custom-call(f32[8,128,2048]{2,1,0:T(8,128)S(1)} %bitcast.16, f32[4,512,512]{2,1,0:T(8,128)S(1)} %copy-done.3), custom_call_target="tpu_custom_call" | custom-call | flops 1073741824 | bytes 4194304 | tf_op jit(solution)/shard_map/prepare/pallas_call | solution.py:107
  22.1 0.0 collective-permute-done.3.r3
  22.1 0.0 collective-permute-done.2.r2
  22.1 0.0 collective-permute-done.1.r1
  22.2 0.0 collective-permute-done.r0
  22.2 0.0 copy-start.7
  22.2 0.2 shard_map.59.own_ref
  22.4 0.7 collective-permute-start.7
  23.0 0.7 collective-permute-start.6
  23.7 0.7 collective-permute-start.5
  24.4 0.7 collective-permute-start.4
  25.1 0.0 collective-permute-done.7.r3
  25.1 0.0 collective-permute-done.6.r2
  25.1 0.0 collective-permute-done.5.r1
  25.1 0.0 collective-permute-done.4.r0
  25.1 0.3 shard_map.60
  25.4 16.5 %all_to_all.10.tiles_ref = f32[16,32,128]{2,1,0:T(8,128)S(1)} all-to-all(f32[16,32,128]{2,1,0:T(8,128)S(1)} %get-tuple-element.22), channel_id=1, replica_groups=mesh['xh'=2,'xl'=2,'zh'=2,'zl'=4,'y'=4,'core'=2] {'xl','zh','zl'}, dimensions={0} | all-to-all | bytes 524288 | tf_op jit(solution)/shard_map/all_to_all | solution.py:253
  41.9 1.1 %shard_map.61 = (f32[16,32,128]{2,1,0:T(8,128)}, f32[32,128]{1,0:T(8,128)S(1)}, f32[12,32,128]{2,1,0:T(8,128)S(1)}) custom-call(f32[16,32,128]{2,1,0:T(8,128)S(1)} %all_to_all.10.tiles_ref, f32[32,128]{1,0:T(8,128)S(1)} %get-tuple-element.23.own_ref, bf16[128,1536]{1,0:T(8,128)(2,1)S(1)} %get-tuple-element.20.high_ref, ...), custom_call_target="tpu_custom_call" | custom-call | flops 134217728 | bytes 2097152 | tf_op jit(solution)/shard_map/pallas_call | solution.py:216
  43.0 5.5 %all-to-all-start.1 = ((f32[16,32,128]{2,1,0:T(8,128)}), f32[16,32,128]{2,1,0:T(8,128)S(1)}, u32[]{:S(2)}, u32[]{:S(2)}) async-start(f32[16,32,128]{2,1,0:T(8,128)} %get-tuple-element.25), calls=%async_computation.1 | async-start | bytes 524288 | tf_op jit(solution)/shard_map/all_to_all | solution.py:259
  48.5 1.3 %collective-permute-start.8 = (f32[12,32,128]{2,1,0:T(8,128)S(1)}, f32[12,32,128]{2,1,0:T(8,128)S(1)}, u32[]{:S(2)}, u32[]{:S(2)}) collective-permute-start(f32[12,32,128]{2,1,0:T(8,128)S(1)} %get-tuple-element.27.refs_0_), channel_id=1, source_target_pairs={{0,128},{64,192},{1,129},{65,193},{2,130},{66,194},{3,131},{67,195... | collective-permute-start | bytes 589832 | tf_op jit(solution)/shard_map/ppermute | solution.py:38
  49.8 6.6 %all-to-all-done.1 = f32[16,32,128]{2,1,0:T(8,128)S(1)} async-done(((f32[16,32,128]{2,1,0:T(8,128)}), f32[16,32,128]{2,1,0:T(8,128)S(1)}, u32[]{:S(2)}, u32[]{:S(2)}) %all-to-all-start.1) | async-done | bytes 262176 | tf_op jit(solution)/shard_map/all_to_all | solution.py:259
  56.4 1.3 %collective-permute-start.9 = (f32[4,32,128]{2,1,0:T(8,128)S(1)}, f32[4,32,128]{2,1,0:T(8,128)S(1)}, u32[]{:S(2)}, u32[]{:S(2)}) collective-permute-start(f32[4,32,128]{2,1,0:T(8,128)S(1)} %slice.12.refs_0_), channel_id=1, source_target_pairs={{0,192},{64,128},{1,193},{65,129},{2,194},{66,130},{3,195},{67,131... | collective-permute-start | bytes 196616 | tf_op jit(solution)/shard_map/ppermute | solution.py:38
  57.7 0.0 collective-permute-done.8.refs_1_
  57.7 0.0 copy-done.7
  57.7 0.0 copy-start.1
  57.7 3.4 %copy-done.1 = f32[8,1,128,2048]{3,2,1,0:T(8,128)S(1)} copy-done((f32[8,1,128,2048]{3,2,1,0:T(8,128)S(1)}, f32[8,1,128,2048]{3,2,1,0:T(8,128)}, u32[]{:S(2)}) %copy-start.1) | copy-done | bytes 8388632
  61.1 0.0 copy-start.4
  61.1 2.2 %copy-done.4 = f32[4,512,512]{2,1,0:T(8,128)S(1)} copy-done((f32[4,512,512]{2,1,0:T(8,128)S(1)}, f32[4,512,512]{2,1,0:T(8,128)}, u32[]{:S(2)}) %copy-start.4) | copy-done | bytes 4194328
  63.3 0.0 copy-start.5
  63.3 3.2 %shard_map.62 = (f32[32,1536]{1,0:T(8,128)S(1)}, f32[8,32,128]{2,1,0:T(8,128)S(1)}) custom-call(f32[12,32,128]{2,1,0:T(8,128)S(1)} %get-tuple-element.27.refs_0_, f32[12,32,128]{2,1,0:T(8,128)S(1)} %collective-permute-done.8.refs_1_, f32[8,32,128]{2,1,0:T(8,128)S(1)} %bitcast.20, f32[8,128,2048]{2,1,0:T(8,128)S(1)} %bitcast.17, f32[4,512,512]{2,1,0:T(8,128)S(1)} %copy-done.4), custom_call_target="tpu_custom_call" | custom-call | flops 1073741824 | bytes 12582912 | tf_op jit(solution)/shard_map/pallas_call | solution.py:216
  66.5 0.0 collective-permute-done.9.refs_1_
  66.5 0.0 copy-done.5
  66.5 0.0 copy-start.2
  66.5 3.4 %copy-done.2 = f32[8,1,128,2048]{3,2,1,0:T(8,128)S(1)} copy-done((f32[8,1,128,2048]{3,2,1,0:T(8,128)S(1)}, f32[8,1,128,2048]{3,2,1,0:T(8,128)}, u32[]{:S(2)}) %copy-start.2) | copy-done | bytes 8388632
  69.9 1.2 %shard_map.63 = (f32[32,512]{1,0:T(8,128)S(1)}, f32[4,32,128]{2,1,0:T(8,128)S(1)}, f32[4,32,128]{2,1,0:T(8,128)S(1)}, f32[2,8,128]{2,1,0:T(8,128)S(1)}) custom-call(f32[4,32,128]{2,1,0:T(8,128)S(1)} %slice.12.refs_0_, f32[4,32,128]{2,1,0:T(8,128)S(1)} %collective-permute-done.9.refs_1_, f32[32,128]{1,0:T(8,128)S(1)} %get-tuple-element.31.refs_2_, ...), custom_call_target="tpu_custom_call" | custom-call | flops 268435456 | bytes 4194304 | tf_op jit(solution)/shard_map/pallas_call | solution.py:216
  71.1 3.3 %collective-permute-start.10 = (f32[2,8,128]{2,1,0:T(8,128)S(1)}, f32[2,8,128]{2,1,0:T(8,128)S(1)}, u32[]{:S(2)}, u32[]{:S(2)}) collective-permute-start(f32[2,8,128]{2,1,0:T(8,128)S(1)} %get-tuple-element.36), channel_id=1, source_target_pairs={{0,1},{1,0},{2,3},{3,2},{4,5},{5,4},{6,7},{7,6},{8,9},{9,8},{10,11... | collective-permute-start | bytes 24584 | tf_op jit(solution)/shard_map/ppermute | solution.py:273
  74.5 0.7 maximum_bitcast_fusion
  75.2 0.1 collective-permute-done.10
  75.3 2.7 %collective-permute-start.13 = (f32[2,8,128]{2,1,0:T(8,128)S(1)}, f32[2,8,128]{2,1,0:T(8,128)S(1)}, u32[]{:S(2)}, u32[]{:S(2)}) collective-permute-start(f32[2,8,128]{2,1,0:T(8,128)S(1)} %add.12), channel_id=1, source_target_pairs={{0,6},{2,4},{4,2},{6,0},{1,7},{3,5},{5,3},{7,1},{8,14},{10,12},{12... | collective-permute-start | bytes 24584 | tf_op jit(solution)/shard_map/ppermute | solution.py:276
  78.0 0.4 collective-permute-start.12
  78.4 0.2 collective-permute-start.11
  78.6 0.7 maximum_bitcast_fusion.1
  79.3 0.0 collective-permute-done.13
  79.3 2.8 %collective-permute-done.12 = f32[2,8,128]{2,1,0:T(8,128)S(1)} collective-permute-done((f32[2,8,128]{2,1,0:T(8,128)S(1)}, f32[2,8,128]{2,1,0:T(8,128)S(1)}, u32[]{:S(2)}, u32[]{:S(2)}) %collective-permute-start.12) | collective-permute-done | bytes 8224 | tf_op jit(solution)/shard_map/ppermute | solution.py:276
  82.0 0.0 collective-permute-done.11
  82.0 0.6 fusion.1
  (4 shorter events, 0.0 us)
Async XLA Ops:
  0.6 0.9 %copy-start.6 = (f32[8,1,128,32]{2,3,1,0:T(8,128)S(1)}, f32[8,1,128,32]{2,3,1,0:T(8,128)}, u32[]{:S(2)}) copy-start(f32[8,1,128,32]{2,3,1,0:T(8,128)} %param.4) | copy-start | bytes 393220
  1.5 20.6 %collective-permute-start.3 = (f32[1,32,128]{2,1,0:T(8,128)S(1)}, f32[1,32,128]{2,1,0:T(8,128)S(1)}, u32[]{:S(2)}, u32[]{:S(2)}) collective-permute-start(f32[1,32,128]{2,1,0:T(8,128)S(1)} %bitcast.21), channel_id=1, source_target_pairs={{0,32},{8,40},{16,48},{24,56},{1,33},{9,41},{17,49},{25,57},{2,34}... | collective-permute-start | bytes 49160 | tf_op jit(solution)/shard_map/ppermute | solution.py:230
  11.2 11.0 %collective-permute-start.2 = (f32[1,32,128]{2,1,0:T(8,128)S(1)}, f32[1,32,128]{2,1,0:T(8,128)S(1)}, u32[]{:S(2)}, u32[]{:S(2)}) collective-permute-start(f32[1,32,128]{2,1,0:T(8,128)S(1)} %bitcast.22), channel_id=1, source_target_pairs={{0,40},{8,32},{16,56},{24,48},{1,41},{9,33},{17,57},{25,49},{2,42}... | collective-permute-start | bytes 49160 | tf_op jit(solution)/shard_map/ppermute | solution.py:230
  12.5 9.7 %collective-permute-start.1 = (f32[1,32,128]{2,1,0:T(8,128)S(1)}, f32[1,32,128]{2,1,0:T(8,128)S(1)}, u32[]{:S(2)}, u32[]{:S(2)}) collective-permute-start(f32[1,32,128]{2,1,0:T(8,128)S(1)} %bitcast.23), channel_id=1, source_target_pairs={{0,56},{8,48},{16,40},{24,32},{1,57},{9,49},{17,41},{25,33},{2,58}... | collective-permute-start | bytes 49160 | tf_op jit(solution)/shard_map/ppermute | solution.py:230
  13.8 8.4 %collective-permute-start = (f32[1,32,128]{2,1,0:T(8,128)S(1)}, f32[1,32,128]{2,1,0:T(8,128)S(1)}, u32[]{:S(2)}, u32[]{:S(2)}) collective-permute-start(f32[1,32,128]{2,1,0:T(8,128)S(1)} %bitcast.24), channel_id=1, source_target_pairs={{0,48},{8,56},{16,32},{24,40},{1,49},{9,57},{17,33},{25,41},{2,50}... | collective-permute-start | bytes 49160 | tf_op jit(solution)/shard_map/ppermute | solution.py:230
  15.1 3.4 %copy-start = (f32[8,1,128,2048]{3,2,1,0:T(8,128)S(1)}, f32[8,1,128,2048]{3,2,1,0:T(8,128)}, u32[]{:S(2)}) copy-start(f32[8,1,128,2048]{3,2,1,0:T(8,128)} %param.3) | copy-start | bytes 25165828
  18.4 2.2 %copy-start.3 = (f32[4,512,512]{2,1,0:T(8,128)S(1)}, f32[4,512,512]{2,1,0:T(8,128)}, u32[]{:S(2)}) copy-start(f32[4,512,512]{2,1,0:T(8,128)} %refs_5_.1) | copy-start | bytes 12582916
  22.2 35.5 %copy-start.7 = (f32[8,1,128,32]{2,3,1,0:T(8,128)S(1)}, f32[8,1,128,32]{2,3,1,0:T(8,128)}, u32[]{:S(2)}) copy-start(f32[8,1,128,32]{2,3,1,0:T(8,128)} %param.4) | copy-start | bytes 393220
  22.4 2.7 %collective-permute-start.7 = (f32[2,32,128]{2,1,0:T(8,128)S(1)}, f32[2,32,128]{2,1,0:T(8,128)S(1)}, u32[]{:S(2)}, u32[]{:S(2)}) collective-permute-start(f32[2,32,128]{2,1,0:T(8,128)S(1)} %shard_map.59.own_ref), channel_id=1, source_target_pairs={{32,64},{40,72},{48,80},{56,88},{33,65},{41,73},{49,81},{57,89},{3... | collective-permute-start | bytes 98312 | tf_op jit(solution)/shard_map/ppermute | solution.py:230
  23.0 2.0 %collective-permute-start.6 = (f32[2,32,128]{2,1,0:T(8,128)S(1)}, f32[2,32,128]{2,1,0:T(8,128)S(1)}, u32[]{:S(2)}, u32[]{:S(2)}) collective-permute-start(f32[2,32,128]{2,1,0:T(8,128)S(1)} %shard_map.59.own_ref), channel_id=1, source_target_pairs={{32,72},{40,64},{48,88},{56,80},{33,73},{41,65},{49,89},{57,81},{3... | collective-permute-start | bytes 98312 | tf_op jit(solution)/shard_map/ppermute | solution.py:230
  23.7 1.4 %collective-permute-start.5 = (f32[2,32,128]{2,1,0:T(8,128)S(1)}, f32[2,32,128]{2,1,0:T(8,128)S(1)}, u32[]{:S(2)}, u32[]{:S(2)}) collective-permute-start(f32[2,32,128]{2,1,0:T(8,128)S(1)} %shard_map.59.own_ref), channel_id=1, source_target_pairs={{32,88},{40,80},{48,72},{56,64},{33,89},{41,81},{49,73},{57,65},{3... | collective-permute-start | bytes 98312 | tf_op jit(solution)/shard_map/ppermute | solution.py:230
  24.4 0.7 collective-permute-start.4
  43.0 13.4 %all-to-all-start.1 = ((f32[16,32,128]{2,1,0:T(8,128)}), f32[16,32,128]{2,1,0:T(8,128)S(1)}, u32[]{:S(2)}, u32[]{:S(2)}) async-start(f32[16,32,128]{2,1,0:T(8,128)} %get-tuple-element.25), calls=%async_computation.1 | async-start | bytes 524288 | tf_op jit(solution)/shard_map/all_to_all | solution.py:259
  48.5 9.2 %collective-permute-start.8 = (f32[12,32,128]{2,1,0:T(8,128)S(1)}, f32[12,32,128]{2,1,0:T(8,128)S(1)}, u32[]{:S(2)}, u32[]{:S(2)}) collective-permute-start(f32[12,32,128]{2,1,0:T(8,128)S(1)} %get-tuple-element.27.refs_0_), channel_id=1, source_target_pairs={{0,128},{64,192},{1,129},{65,193},{2,130},{66,194},{3,131},{67,195... | collective-permute-start | bytes 589832 | tf_op jit(solution)/shard_map/ppermute | solution.py:38
  56.4 10.1 %collective-permute-start.9 = (f32[4,32,128]{2,1,0:T(8,128)S(1)}, f32[4,32,128]{2,1,0:T(8,128)S(1)}, u32[]{:S(2)}, u32[]{:S(2)}) collective-permute-start(f32[4,32,128]{2,1,0:T(8,128)S(1)} %slice.12.refs_0_), channel_id=1, source_target_pairs={{0,192},{64,128},{1,193},{65,129},{2,194},{66,130},{3,195},{67,131... | collective-permute-start | bytes 196616 | tf_op jit(solution)/shard_map/ppermute | solution.py:38
  57.7 3.4 %copy-start.1 = (f32[8,1,128,2048]{3,2,1,0:T(8,128)S(1)}, f32[8,1,128,2048]{3,2,1,0:T(8,128)}, u32[]{:S(2)}) copy-start(f32[8,1,128,2048]{3,2,1,0:T(8,128)} %param.3) | copy-start | bytes 25165828
  61.1 2.2 %copy-start.4 = (f32[4,512,512]{2,1,0:T(8,128)S(1)}, f32[4,512,512]{2,1,0:T(8,128)}, u32[]{:S(2)}) copy-start(f32[4,512,512]{2,1,0:T(8,128)} %refs_5_.1) | copy-start | bytes 12582916
  63.3 3.2 %copy-start.5 = (f32[4,512,512]{2,1,0:T(8,128)S(1)}, f32[4,512,512]{2,1,0:T(8,128)}, u32[]{:S(2)}) copy-start(f32[4,512,512]{2,1,0:T(8,128)} %refs_5_.1) | copy-start | bytes 12582916
  66.5 3.4 %copy-start.2 = (f32[8,1,128,2048]{3,2,1,0:T(8,128)S(1)}, f32[8,1,128,2048]{3,2,1,0:T(8,128)}, u32[]{:S(2)}) copy-start(f32[8,1,128,2048]{3,2,1,0:T(8,128)} %param.3) | copy-start | bytes 25165828
  71.1 4.1 %collective-permute-start.10 = (f32[2,8,128]{2,1,0:T(8,128)S(1)}, f32[2,8,128]{2,1,0:T(8,128)S(1)}, u32[]{:S(2)}, u32[]{:S(2)}) collective-permute-start(f32[2,8,128]{2,1,0:T(8,128)S(1)} %get-tuple-element.36), channel_id=1, source_target_pairs={{0,1},{1,0},{2,3},{3,2},{4,5},{5,4},{6,7},{7,6},{8,9},{9,8},{10,11... | collective-permute-start | bytes 24584 | tf_op jit(solution)/shard_map/ppermute | solution.py:273
  75.3 4.0 %collective-permute-start.13 = (f32[2,8,128]{2,1,0:T(8,128)S(1)}, f32[2,8,128]{2,1,0:T(8,128)S(1)}, u32[]{:S(2)}, u32[]{:S(2)}) collective-permute-start(f32[2,8,128]{2,1,0:T(8,128)S(1)} %add.12), channel_id=1, source_target_pairs={{0,6},{2,4},{4,2},{6,0},{1,7},{3,5},{5,3},{7,1},{8,14},{10,12},{12... | collective-permute-start | bytes 24584 | tf_op jit(solution)/shard_map/ppermute | solution.py:276
  78.0 4.0 %collective-permute-start.12 = (f32[2,8,128]{2,1,0:T(8,128)S(1)}, f32[2,8,128]{2,1,0:T(8,128)S(1)}, u32[]{:S(2)}, u32[]{:S(2)}) collective-permute-start(f32[2,8,128]{2,1,0:T(8,128)S(1)} %add.12), channel_id=1, source_target_pairs={{0,4},{2,6},{4,0},{6,2},{1,5},{3,7},{5,1},{7,3},{8,12},{10,14},{12... | collective-permute-start | bytes 24584 | tf_op jit(solution)/shard_map/ppermute | solution.py:276
  78.4 3.7 %collective-permute-start.11 = (f32[2,8,128]{2,1,0:T(8,128)S(1)}, f32[2,8,128]{2,1,0:T(8,128)S(1)}, u32[]{:S(2)}, u32[]{:S(2)}) collective-permute-start(f32[2,8,128]{2,1,0:T(8,128)S(1)} %add.12), channel_id=1, source_target_pairs={{0,2},{2,0},{4,6},{6,4},{1,3},{3,1},{5,7},{7,5},{8,10},{10,8},{12,... | collective-permute-start | bytes 24584 | tf_op jit(solution)/shard_map/ppermute | solution.py:276

commit v11 on v10

--- a/solution.py
+++ b/solution.py
@@ -69,55 +69,23 @@
     return value
 
 
-def begin_body(right_ref, own_ref):
-    own_ref[...] = right_ref[0]
-
-
-def prepare_body(panel_ref, inverses_ref, high_ref, low_ref, part_ref, inverse_ref, sems):
-    copies = []
-    for step in range(STEPS - 1):
-        columns = pl.ds(step * WIDTH, WIDTH)
-        copies.append((
-            pltpu.make_async_copy(
-                panel_ref.at[0, :, columns], part_ref.at[step], sems.at[0, step]
-            ),
-            pltpu.make_async_copy(
-                inverses_ref.at[step], inverse_ref.at[step], sems.at[1, step]
-            ),
-        ))
-    for pair in copies:
-        for copy in pair:
-            copy.start()
-    for step, pair in enumerate(copies):
-        for copy in pair:
-            copy.wait()
-        high, low = split(part_ref[step])
-        inverse_high, inverse_low = split(inverse_ref[step])
-        wide = dot16(jnp.concatenate([high, low], axis=0), inverse_high, NN)
-        rows = high.shape[0]
-        factor = wide[:rows] + wide[rows:] + dot16(high, inverse_low, NN)
-        columns = slice(step * WIDTH, (step + 1) * WIDTH)
-        high_ref[:, columns], low_ref[:, columns] = split(factor)
-
-
-def prepare(panel, inverses):
-    rows = panel.shape[1]
-    number = STEPS - 1
-    half = jax.ShapeDtypeStruct((rows, number * WIDTH), bf16)
-    return pl.pallas_call(
-        prepare_body,
-        out_shape=[half, half],
-        in_specs=[pl.BlockSpec(memory_space=pl.ANY)] * 2,
-        out_specs=[VMEM] * 2,
-        scratch_shapes=[
-            pltpu.VMEM((number, rows, WIDTH), f32),
-            pltpu.VMEM((number, WIDTH, WIDTH), f32),
-            pltpu.SemaphoreType.DMA((2, number)),
-        ],
-        compiler_params=params(16),
-        cost_estimate=cost(1 << 30, 4 << 20),
-        name="prepare",
-    )(panel, inverses)
+def product_halves(part, inverse):
+    high, low = split(part)
+    inverse_high, inverse_low = split(inverse)
+    wide = dot16(jnp.concatenate([high, low], axis=0), inverse_high, NN)
+    rows = high.shape[0]
+    return split(wide[:rows] + wide[rows:] + dot16(high, inverse_low, NN))
+
+
+def prepare_body(part_ref, inverse_ref, high_ref, low_ref):
+    high_ref[...], low_ref[...] = product_halves(part_ref[...], inverse_ref[...])
+
+
+def complete_body(panel_ref, inverses_ref, high_ref, low_ref):
+    for step in range(1, STEPS - 1):
+        part = panel_ref[0, :, step * WIDTH:(step + 1) * WIDTH]
+        columns = slice((step - 1) * WIDTH, step * WIDTH)
+        high_ref[:, columns], low_ref[:, columns] = product_halves(part, inverses_ref[step])
 
 
 def arrived(lane, refs, at):
@@ -131,32 +99,33 @@
     return tiles
 
 
-def advanced(own_ref, high_ref, low_ref, tiles):
+def advanced(own_ref, high_refs, low_refs, tiles):
     steps = len(tiles) // TILES
-    change = times_halves(
-        jnp.concatenate(tiles, axis=1), high_ref[:, :steps * WIDTH], low_ref[:, :steps * WIDTH]
-    )
+    high, low = (
+        jnp.concatenate([ref[...] for ref in refs], axis=1)[:, :steps * WIDTH]
+        for refs in (high_refs, low_refs)
+    )
+    change = times_halves(jnp.concatenate(tiles, axis=1), high, low)
     return jnp.where(step_of() == steps, own_ref[...] - change, own_ref[...])
 
 
 def first_body(r0, r1, r2, r3, own_ref, high_ref, low_ref, own_out_ref):
-    own = advanced(own_ref, high_ref, low_ref, arrived(lax.axis_index("zl"), (r0, r1, r2, r3), 0))
-    own_out_ref[0] = own
-    own_out_ref[1] = r3[0]
-
-
-def second_body(r0, r1, r2, r3, own_ref, high_ref, low_ref, copies_ref, own_out_ref):
-    refs = (r0, r1, r2, r3)
-    tiles = arrived(lax.axis_index("zl"), refs, 1) + arrived(lax.axis_index("zl"), refs, 0)
-    own = advanced(own_ref.at[0], high_ref, low_ref, tiles)
+    tiles = arrived(lax.axis_index("zl"), (r0, r1, r2, r3), 0)
+    own_out_ref[0] = advanced(own_ref, [high_ref], [low_ref], tiles)
+
+
+def second_body(r0, r1, r2, r3, f0, f1, f2, f3, own_ref, h0, l0, h1, l1, copies_ref, own_out_ref):
+    lane = lax.axis_index("zl")
+    tiles = arrived(lane, (f0, f1, f2, f3), 0) + arrived(lane, (r0, r1, r2, r3), 0)
+    own = advanced(own_ref.at[0], [h0, h1], [l0, l1], tiles)
     own_out_ref[...] = own
     for i in range(GROUP):
         copies_ref[i] = own
 
 
-def third_body(tiles_ref, own_ref, high_ref, low_ref, copies_ref, own_out_ref, packed_ref):
+def third_body(tiles_ref, own_ref, h0, l0, h1, l1, copies_ref, own_out_ref, packed_ref):
     tiles = [tiles_ref[i] for i in range((STEPS - 1) * TILES)]
-    own = advanced(own_ref, high_ref, low_ref, tiles)
+    own = advanced(own_ref, [h0, h1], [l0, l1], tiles)
     own_out_ref[...] = own
     for i in range(GROUP):
         copies_ref[i] = own
@@ -223,12 +192,11 @@
     )(*args)
 
 
-def forward(value, step):
-    ahead = (step + 1) * TILES
+def forward(value, source, target):
     pieces = []
     for change in ORDER:
         pieces.append(lax.ppermute(
-            value, ROWS, [(ahead - TILES + i, ahead + (i ^ change)) for i in range(TILES)]
+            value, ROWS, [(source + i, target + (i ^ change)) for i in range(TILES)]
         ))
     return pieces
 
@@ -241,15 +209,23 @@
     tile = shape(members, rows)
     group = shape(GROUP, members, rows)
 
-    own, = local(begin_body, 8, [tile], 1 << 20, 1 << 20, right)
-    tiles = forward(own[None], 0)
-    factor = prepare(panel, inverses)
+    own = right[0]
+    own = own[None]
+    tiles = forward(own, 0, TILES)
+    far = forward(own, 0, 2 * TILES)
+    half = jax.ShapeDtypeStruct((rows, WIDTH), bf16)
+    factor = local(
+        prepare_body, 16, [half, half], 1 << 28, 2 << 20,
+        panel[0, :, :WIDTH], inverses[0],
+    )
     own, = local(
-        first_body, 8, [shape(2, members, rows)], 1 << 34, 1 << 20,
-        *tiles, own, *factor,
-    )
-    tiles = forward(own, 1)
-    copies, own = local(second_body, 8, [group, tile], 1 << 27, 1 << 20, *tiles, own, *factor)
+        first_body, 8, [shape(1, members, rows)], 1 << 33, 1 << 20,
+        *tiles, own[0], *factor,
+    )
+    tiles = forward(own, TILES, 2 * TILES)
+    half = jax.ShapeDtypeStruct((rows, (STEPS - 2) * WIDTH), bf16)
+    factor += local(complete_body, 16, [half, half], 1 << 29, 12 << 20, panel, inverses)
+    copies, own = local(second_body, 8, [group, tile], 1 << 27, 1 << 20, *tiles, *far, own, *factor)
     tiles = lax.all_to_all(copies, OWNERS, 0, 0)
     copies, own, packed = local(
         third_body, 8, [group, tile, shape(3 * TILES, members, rows)],

time: 83.5 us -> 85 us (1.018)
  starting transfers between devices: 30.8 us -> 38.4 us
  local copies, waits for them, and re-layouts: 15.4 us -> 8.71 us
  blocking collectives: 16.5 us -> 18 us
    unnamed x16 -> x12, local copies, waits for them, and re-layouts: 15.4 us -> 5.71 us
    ppermute x8 -> x12, starting transfers between devices: 16.2 us -> 22 us  [forward(): lax.ppermute(value, ROWS, [(source + i, target + (i ^ change)) for i in r...]
    ppermute x1, starting transfers between devices: 3.31 us -> 5.87 us  [shards(): sums = sums + lax.ppermute(sums, 'core', [(0, 1), (1, 0)])]
    squeeze x0 -> x2, local copies, waits for them, and re-layouts: none -> 2.27 us  [the longest x1 1.3 us: shards(): inverses[0]]
    all_to_all x1, blocking collectives: 16.5 us -> 18 us  [shards(): tiles = lax.all_to_all(copies, OWNERS, 0, 0)]
    pallas_call x1 -> x0, Pallas kernels: 1.48 us -> none  [prepare(): pl.pallas_call(prepare_body, out_shape=[half, half], in_specs=[pl.BlockSp...]
    all_to_all x1, starting transfers between devices: 5.48 us -> 4.34 us  [shards(): received = lax.all_to_all(copies, OWNERS, 0, 0)]
    pallas_call x6 -> x7, Pallas kernels: 5.99 us -> 7 us  [local(): pl.pallas_call(body, out_shape=outs, in_specs=[VMEM] * len(args), out_spe...]
  transfers between devices with their start and end apart: 15 -> 19, of which waited for: 3 -> 3; matrix products, arithmetic and copies ran while one was open for 2% -> 4% of each run, Pallas kernels for 6% -> 5%
where the time goes in v11:
time: 85 us; the launch traced here: 84 us
  starting transfers between devices  38.4 us (45%)
  blocking collectives  18 us (21%)
  waiting for transfers between devices  8.89 us (10%)
  local copies, waits for them, and re-layouts  8.71 us (10%)
  Pallas kernels  7 us (8%)
  other arithmetic  1.99 us (2%)
  between operations  0.98 us (1%)
    ppermute x12, starting transfers between devices, forward(): lax.ppermute(value, ROWS, [(source + i, target + (i ^ change)) for i in r...  22 us
    all_to_all x1, blocking collectives, shards(): tiles = lax.all_to_all(copies, OWNERS, 0, 0)  18 us
    pallas_call x7, Pallas kernels, local(): pl.pallas_call(body, out_shape=outs, in_specs=[VMEM] * len(args), out_spe...  7 us
    all_to_all x1, waiting for transfers between devices, shards(): received = lax.all_to_all(copies, OWNERS, 0, 0)  6.46 us
    ppermute x1, starting transfers between devices, shards(): sums = sums + lax.ppermute(sums, 'core', [(0, 1), (1, 0)])  5.87 us
    unnamed x12, local copies, waits for them, and re-layouts  5.71 us
    all_to_all x1, starting transfers between devices, shards(): received = lax.all_to_all(copies, OWNERS, 0, 0)  4.34 us
    ppermute x3, starting transfers between devices, shards(): others.append(lax.ppermute(sums, 'y', [(i, i ^ change) for i in range(4)]))  3.69 us
  transfers between devices with their start and end apart: 19, of which 3 were waited for; matrix products, arithmetic and copies ran while one was open for 4% of the time, Pallas kernels for 5%

profile of v11, /device:TPU:1, one launch (start us, length us, event | category | flops | bytes accessed | tf_op | source)
XLA Modules:
  0.0 84.0 jit_solution(4277016411338712541)
XLA Ops:
  0.6 0.7 slice_bitcast_fusion.2
  1.4 8.7 %collective-permute-start = (f32[1,32,128]{2,1,0:T(8,128)S(1)}, f32[1,32,128]{2,1,0:T(8,128)S(1)}, u32[]{:S(2)}, u32[]{:S(2)}) collective-permute-start(f32[1,32,128]{2,1,0:T(8,128)S(1)} %get-tuple-element.45), channel_id=1, source_target_pairs={{0,48},{8,56},{16,32},{24,40},{1,49},{9,57},{17,33},{25,41},{2,50}... | collective-permute-start | bytes 49160 | tf_op jit(solution)/shard_map/ppermute | solution.py:198
  10.1 1.3 %collective-permute-start.1 = (f32[1,32,128]{2,1,0:T(8,128)S(1)}, f32[1,32,128]{2,1,0:T(8,128)S(1)}, u32[]{:S(2)}, u32[]{:S(2)}) collective-permute-start(f32[1,32,128]{2,1,0:T(8,128)S(1)} %get-tuple-element.45), channel_id=1, source_target_pairs={{0,56},{8,48},{16,40},{24,32},{1,57},{9,49},{17,41},{25,33},{2,58}... | collective-permute-start | bytes 49160 | tf_op jit(solution)/shard_map/ppermute | solution.py:198
  11.4 1.7 %collective-permute-start.2 = (f32[1,32,128]{2,1,0:T(8,128)S(1)}, f32[1,32,128]{2,1,0:T(8,128)S(1)}, u32[]{:S(2)}, u32[]{:S(2)}) collective-permute-start(f32[1,32,128]{2,1,0:T(8,128)S(1)} %get-tuple-element.45), channel_id=1, source_target_pairs={{0,40},{8,32},{16,56},{24,48},{1,41},{9,33},{17,57},{25,49},{2,42}... | collective-permute-start | bytes 49160 | tf_op jit(solution)/shard_map/ppermute | solution.py:198
  13.1 1.7 %collective-permute-start.3 = (f32[1,32,128]{2,1,0:T(8,128)S(1)}, f32[1,32,128]{2,1,0:T(8,128)S(1)}, u32[]{:S(2)}, u32[]{:S(2)}) collective-permute-start(f32[1,32,128]{2,1,0:T(8,128)S(1)} %get-tuple-element.45), channel_id=1, source_target_pairs={{0,32},{8,40},{16,48},{24,56},{1,33},{9,41},{17,49},{25,57},{2,34}... | collective-permute-start | bytes 49160 | tf_op jit(solution)/shard_map/ppermute | solution.py:198
  14.9 1.3 %collective-permute-start.8 = (f32[1,32,128]{2,1,0:T(8,128)S(1)}, f32[1,32,128]{2,1,0:T(8,128)S(1)}, u32[]{:S(2)}, u32[]{:S(2)}) collective-permute-start(f32[1,32,128]{2,1,0:T(8,128)S(1)} %get-tuple-element.45), channel_id=1, source_target_pairs={{0,80},{8,88},{16,64},{24,72},{1,81},{9,89},{17,65},{25,73},{2,82}... | collective-permute-start | bytes 49160 | tf_op jit(solution)/shard_map/ppermute | solution.py:198
  16.2 1.0 %slice_bitcast_fusion.1.part_ref = f32[128,512]{1,0:T(8,128)S(1)} fusion(f32[8,128,2048]{2,1,0:T(8,128)} %bitcast.21), kind=kLoop, calls=%fused_computation.1 | loop fusion | bytes 524288 | tf_op jit(solution)/shard_map/squeeze | solution.py:219
  17.2 1.3 %slice_bitcast_fusion.inverse_ref = f32[512,512]{1,0:T(8,128)S(1)} fusion(f32[4,512,512]{2,1,0:T(8,128)} %refs_5_.1), kind=kLoop, calls=%fused_computation | loop fusion | bytes 2097152 | tf_op jit(solution)/shard_map/squeeze | solution.py:219
  18.5 0.0 slice-start
  18.5 0.4 shard_map.58
  18.8 0.0 collective-permute-done.r0
  18.9 1.6 %collective-permute-start.9 = (f32[1,32,128]{2,1,0:T(8,128)S(1)}, f32[1,32,128]{2,1,0:T(8,128)S(1)}, u32[]{:S(2)}, u32[]{:S(2)}) collective-permute-start(f32[1,32,128]{2,1,0:T(8,128)S(1)} %get-tuple-element.45), channel_id=1, source_target_pairs={{0,88},{8,80},{16,72},{24,64},{1,89},{9,81},{17,73},{25,65},{2,90}... | collective-permute-start | bytes 49160 | tf_op jit(solution)/shard_map/ppermute | solution.py:198
  20.4 0.0 collective-permute-done.1.r1
  20.4 1.3 %collective-permute-start.10 = (f32[1,32,128]{2,1,0:T(8,128)S(1)}, f32[1,32,128]{2,1,0:T(8,128)S(1)}, u32[]{:S(2)}, u32[]{:S(2)}) collective-permute-start(f32[1,32,128]{2,1,0:T(8,128)S(1)} %get-tuple-element.45), channel_id=1, source_target_pairs={{0,72},{8,64},{16,88},{24,80},{1,73},{9,65},{17,89},{25,81},{2,74}... | collective-permute-start | bytes 49160 | tf_op jit(solution)/shard_map/ppermute | solution.py:198
  21.7 0.0 collective-permute-done.2.r2
  21.7 1.3 %collective-permute-start.11 = (f32[1,32,128]{2,1,0:T(8,128)S(1)}, f32[1,32,128]{2,1,0:T(8,128)S(1)}, u32[]{:S(2)}, u32[]{:S(2)}) collective-permute-start(f32[1,32,128]{2,1,0:T(8,128)S(1)} %get-tuple-element.45), channel_id=1, source_target_pairs={{0,64},{8,72},{16,80},{24,88},{1,65},{9,73},{17,81},{25,89},{2,66}... | collective-permute-start | bytes 49160 | tf_op jit(solution)/shard_map/ppermute | solution.py:198
  23.0 0.0 collective-permute-done.3.r3
  23.1 0.0 slice-start.1
  23.1 0.0 copy-start.1
  23.1 0.2 shard_map.59.own_ref
  23.3 0.0 copy-start.3
  23.3 0.8 collective-permute-start.4
  24.1 0.0 collective-permute-done.8.f0
  24.1 0.8 collective-permute-start.5
  24.9 0.0 collective-permute-done.9.f1
  24.9 0.8 collective-permute-start.6
  25.7 0.0 collective-permute-done.10.f2
  25.7 0.7 collective-permute-start.7
  26.4 0.0 slice-done
  26.4 0.0 slice-done.1
  26.4 0.1 copy-done.1
  26.5 0.6 shard_map.60
  27.1 0.0 collective-permute-done.11.f3
  27.1 0.0 collective-permute-done.4.r0
  27.2 0.0 collective-permute-done.5.r1
  27.2 0.0 collective-permute-done.6.r2
  27.2 0.0 collective-permute-done.7.r3
  27.2 0.3 shard_map.61
  27.5 18.0 %all_to_all.10.tiles_ref = f32[16,32,128]{2,1,0:T(8,128)S(1)} all-to-all(f32[16,32,128]{2,1,0:T(8,128)S(1)} %get-tuple-element.26), channel_id=1, replica_groups=mesh['xh'=2,'xl'=2,'zh'=2,'zl'=4,'y'=4,'core'=2] {'xl','zh','zl'}, dimensions={0} | all-to-all | bytes 524288 | tf_op jit(solution)/shard_map/all_to_all | solution.py:229
  45.5 1.1 %shard_map.62 = (f32[16,32,128]{2,1,0:T(8,128)}, f32[32,128]{1,0:T(8,128)S(1)}, f32[12,32,128]{2,1,0:T(8,128)S(1)}) custom-call(f32[16,32,128]{2,1,0:T(8,128)S(1)} %all_to_all.10.tiles_ref, f32[32,128]{1,0:T(8,128)S(1)} %get-tuple-element.27.own_ref, bf16[128,512]{1,0:T(8,128)(2,1)S(1)} %get-tuple-element.22.high_ref.h0, ...), custom_call_target="tpu_custom_call" | custom-call | flops 134217728 | bytes 2097152 | tf_op jit(solution)/shard_map/pallas_call | solution.py:185
  46.6 4.3 %all-to-all-start.1 = ((f32[16,32,128]{2,1,0:T(8,128)}), f32[16,32,128]{2,1,0:T(8,128)S(1)}, u32[]{:S(2)}, u32[]{:S(2)}) async-start(f32[16,32,128]{2,1,0:T(8,128)} %get-tuple-element.29), calls=%async_computation.1 | async-start | bytes 524288 | tf_op jit(solution)/shard_map/all_to_all | solution.py:235
  51.0 1.3 %collective-permute-start.12 = (f32[12,32,128]{2,1,0:T(8,128)S(1)}, f32[12,32,128]{2,1,0:T(8,128)S(1)}, u32[]{:S(2)}, u32[]{:S(2)}) collective-permute-start(f32[12,32,128]{2,1,0:T(8,128)S(1)} %get-tuple-element.31.refs_0_), channel_id=1, source_target_pairs={{0,128},{64,192},{1,129},{65,193},{2,130},{66,194},{3,131},{67,195... | collective-permute-start | bytes 589832 | tf_op jit(solution)/shard_map/ppermute | solution.py:38
  52.3 6.5 %all-to-all-done.1 = f32[16,32,128]{2,1,0:T(8,128)S(1)} async-done(((f32[16,32,128]{2,1,0:T(8,128)}), f32[16,32,128]{2,1,0:T(8,128)S(1)}, u32[]{:S(2)}, u32[]{:S(2)}) %all-to-all-start.1) | async-done | bytes 262176 | tf_op jit(solution)/shard_map/all_to_all | solution.py:235
  58.8 1.3 %collective-permute-start.13 = (f32[4,32,128]{2,1,0:T(8,128)S(1)}, f32[4,32,128]{2,1,0:T(8,128)S(1)}, u32[]{:S(2)}, u32[]{:S(2)}) collective-permute-start(f32[4,32,128]{2,1,0:T(8,128)S(1)} %slice.26.refs_0_), channel_id=1, source_target_pairs={{0,192},{64,128},{1,193},{65,129},{2,194},{66,130},{3,195},{67,131... | collective-permute-start | bytes 196616 | tf_op jit(solution)/shard_map/ppermute | solution.py:38
  60.0 0.0 collective-permute-done.12.refs_1_
  60.1 0.0 copy-done.3
  60.1 0.0 copy-start
  60.1 3.4 %copy-done = f32[8,1,128,2048]{3,2,1,0:T(8,128)S(1)} copy-done((f32[8,1,128,2048]{3,2,1,0:T(8,128)S(1)}, f32[8,1,128,2048]{3,2,1,0:T(8,128)}, u32[]{:S(2)}) %copy-start) | copy-done | bytes 8388632
  63.5 0.0 copy-start.2
  63.5 2.2 %copy-done.2 = f32[4,512,512]{2,1,0:T(8,128)S(1)} copy-done((f32[4,512,512]{2,1,0:T(8,128)S(1)}, f32[4,512,512]{2,1,0:T(8,128)}, u32[]{:S(2)}) %copy-start.2) | copy-done | bytes 4194328
  65.6 3.2 %shard_map.63 = (f32[32,1536]{1,0:T(8,128)S(1)}, f32[8,32,128]{2,1,0:T(8,128)S(1)}) custom-call(f32[12,32,128]{2,1,0:T(8,128)S(1)} %get-tuple-element.31.refs_0_, f32[12,32,128]{2,1,0:T(8,128)S(1)} %collective-permute-done.12.refs_1_, f32[8,32,128]{2,1,0:T(8,128)S(1)} %bitcast.28, f32[8,128,2048]{2,1,0:T(8,128)S(1)} %bitcast.25, f32[4,512,512]{2,1,0:T(8,128)S(1)} %copy-done.2), custom_call_target="tpu_custom_call" | custom-call | flops 1073741824 | bytes 12582912 | tf_op jit(solution)/shard_map/pallas_call | solution.py:185
  68.8 0.0 collective-permute-done.13.refs_1_
  68.9 1.2 %shard_map.64 = (f32[32,512]{1,0:T(8,128)S(1)}, f32[4,32,128]{2,1,0:T(8,128)S(1)}, f32[4,32,128]{2,1,0:T(8,128)S(1)}, f32[2,8,128]{2,1,0:T(8,128)S(1)}) custom-call(f32[4,32,128]{2,1,0:T(8,128)S(1)} %slice.26.refs_0_, f32[4,32,128]{2,1,0:T(8,128)S(1)} %collective-permute-done.13.refs_1_, f32[32,128]{1,0:T(8,128)S(1)} %get-tuple-element.35.refs_2_, ...), custom_call_target="tpu_custom_call" | custom-call | flops 268435456 | bytes 4194304 | tf_op jit(solution)/shard_map/pallas_call | solution.py:185
  70.1 5.9 %collective-permute-start.14 = (f32[2,8,128]{2,1,0:T(8,128)S(1)}, f32[2,8,128]{2,1,0:T(8,128)S(1)}, u32[]{:S(2)}, u32[]{:S(2)}) collective-permute-start(f32[2,8,128]{2,1,0:T(8,128)S(1)} %get-tuple-element.40), channel_id=1, source_target_pairs={{0,1},{1,0},{2,3},{3,2},{4,5},{5,4},{6,7},{7,6},{8,9},{9,8},{10,11... | collective-permute-start | bytes 24584 | tf_op jit(solution)/shard_map/ppermute | solution.py:249
  76.0 0.7 maximum_bitcast_fusion
  76.7 0.1 collective-permute-done.14
  76.8 2.9 %collective-permute-start.16 = (f32[2,8,128]{2,1,0:T(8,128)S(1)}, f32[2,8,128]{2,1,0:T(8,128)S(1)}, u32[]{:S(2)}, u32[]{:S(2)}) collective-permute-start(f32[2,8,128]{2,1,0:T(8,128)S(1)} %add.12), channel_id=1, source_target_pairs={{0,4},{2,6},{4,0},{6,2},{1,5},{3,7},{5,1},{7,3},{8,12},{10,14},{12... | collective-permute-start | bytes 24584 | tf_op jit(solution)/shard_map/ppermute | solution.py:252
  79.7 0.8 collective-permute-start.17
  80.5 0.0 collective-permute-start.15
  80.5 0.7 maximum_bitcast_fusion.1
  81.2 0.0 collective-permute-done.16
  81.2 2.3 %collective-permute-done.17 = f32[2,8,128]{2,1,0:T(8,128)S(1)} collective-permute-done((f32[2,8,128]{2,1,0:T(8,128)S(1)}, f32[2,8,128]{2,1,0:T(8,128)S(1)}, u32[]{:S(2)}, u32[]{:S(2)}) %collective-permute-start.17) | collective-permute-done | bytes 8224 | tf_op jit(solution)/shard_map/ppermute | solution.py:252
  83.4 0.0 collective-permute-done.15
  83.4 0.6 fusion.1
  (4 shorter events, 0.0 us)
Async XLA Ops:
  1.4 17.5 %collective-permute-start = (f32[1,32,128]{2,1,0:T(8,128)S(1)}, f32[1,32,128]{2,1,0:T(8,128)S(1)}, u32[]{:S(2)}, u32[]{:S(2)}) collective-permute-start(f32[1,32,128]{2,1,0:T(8,128)S(1)} %get-tuple-element.45), channel_id=1, source_target_pairs={{0,48},{8,56},{16,32},{24,40},{1,49},{9,57},{17,33},{25,41},{2,50}... | collective-permute-start | bytes 49160 | tf_op jit(solution)/shard_map/ppermute | solution.py:198
  10.1 10.3 %collective-permute-start.1 = (f32[1,32,128]{2,1,0:T(8,128)S(1)}, f32[1,32,128]{2,1,0:T(8,128)S(1)}, u32[]{:S(2)}, u32[]{:S(2)}) collective-permute-start(f32[1,32,128]{2,1,0:T(8,128)S(1)} %get-tuple-element.45), channel_id=1, source_target_pairs={{0,56},{8,48},{16,40},{24,32},{1,57},{9,49},{17,41},{25,33},{2,58}... | collective-permute-start | bytes 49160 | tf_op jit(solution)/shard_map/ppermute | solution.py:198
  11.4 10.3 %collective-permute-start.2 = (f32[1,32,128]{2,1,0:T(8,128)S(1)}, f32[1,32,128]{2,1,0:T(8,128)S(1)}, u32[]{:S(2)}, u32[]{:S(2)}) collective-permute-start(f32[1,32,128]{2,1,0:T(8,128)S(1)} %get-tuple-element.45), channel_id=1, source_target_pairs={{0,40},{8,32},{16,56},{24,48},{1,41},{9,33},{17,57},{25,49},{2,42}... | collective-permute-start | bytes 49160 | tf_op jit(solution)/shard_map/ppermute | solution.py:198
  13.1 9.9 %collective-permute-start.3 = (f32[1,32,128]{2,1,0:T(8,128)S(1)}, f32[1,32,128]{2,1,0:T(8,128)S(1)}, u32[]{:S(2)}, u32[]{:S(2)}) collective-permute-start(f32[1,32,128]{2,1,0:T(8,128)S(1)} %get-tuple-element.45), channel_id=1, source_target_pairs={{0,32},{8,40},{16,48},{24,56},{1,33},{9,41},{17,49},{25,57},{2,34}... | collective-permute-start | bytes 49160 | tf_op jit(solution)/shard_map/ppermute | solution.py:198
  14.9 9.2 %collective-permute-start.8 = (f32[1,32,128]{2,1,0:T(8,128)S(1)}, f32[1,32,128]{2,1,0:T(8,128)S(1)}, u32[]{:S(2)}, u32[]{:S(2)}) collective-permute-start(f32[1,32,128]{2,1,0:T(8,128)S(1)} %get-tuple-element.45), channel_id=1, source_target_pairs={{0,80},{8,88},{16,64},{24,72},{1,81},{9,89},{17,65},{25,73},{2,82}... | collective-permute-start | bytes 49160 | tf_op jit(solution)/shard_map/ppermute | solution.py:198
  18.5 7.9 %slice-start = ((s8[8388608]{0:T(1024)(128)(4,1)}), s8[4194304]{0:T(1024)(128)(4,1)S(1)}, s32[]{:S(2)}) async-start(s8[8388608]{0:T(1024)(128)(4,1)} %bitcast.22), calls=%async_computation.2 | async-start | bytes 8388608
  18.9 6.0 %collective-permute-start.9 = (f32[1,32,128]{2,1,0:T(8,128)S(1)}, f32[1,32,128]{2,1,0:T(8,128)S(1)}, u32[]{:S(2)}, u32[]{:S(2)}) collective-permute-start(f32[1,32,128]{2,1,0:T(8,128)S(1)} %get-tuple-element.45), channel_id=1, source_target_pairs={{0,88},{8,80},{16,72},{24,64},{1,89},{9,81},{17,73},{25,65},{2,90}... | collective-permute-start | bytes 49160 | tf_op jit(solution)/shard_map/ppermute | solution.py:198
  20.4 5.3 %collective-permute-start.10 = (f32[1,32,128]{2,1,0:T(8,128)S(1)}, f32[1,32,128]{2,1,0:T(8,128)S(1)}, u32[]{:S(2)}, u32[]{:S(2)}) collective-permute-start(f32[1,32,128]{2,1,0:T(8,128)S(1)} %get-tuple-element.45), channel_id=1, source_target_pairs={{0,72},{8,64},{16,88},{24,80},{1,73},{9,65},{17,89},{25,81},{2,74}... | collective-permute-start | bytes 49160 | tf_op jit(solution)/shard_map/ppermute | solution.py:198
  21.7 5.4 %collective-permute-start.11 = (f32[1,32,128]{2,1,0:T(8,128)S(1)}, f32[1,32,128]{2,1,0:T(8,128)S(1)}, u32[]{:S(2)}, u32[]{:S(2)}) collective-permute-start(f32[1,32,128]{2,1,0:T(8,128)S(1)} %get-tuple-element.45), channel_id=1, source_target_pairs={{0,64},{8,72},{16,80},{24,88},{1,65},{9,73},{17,81},{25,89},{2,66}... | collective-permute-start | bytes 49160 | tf_op jit(solution)/shard_map/ppermute | solution.py:198
  23.1 3.4 %slice-start.1 = ((s8[8388608]{0:T(1024)(128)(4,1)}), s8[4194304]{0:T(1024)(128)(4,1)S(1)}, s32[]{:S(2)}) async-start(s8[8388608]{0:T(1024)(128)(4,1)} %bitcast.22), calls=%async_computation.3 | async-start | bytes 8388608
  23.1 3.5 %copy-start.1 = (f32[4,512,512]{2,1,0:T(8,128)S(1)}, f32[4,512,512]{2,1,0:T(8,128)}, u32[]{:S(2)}) copy-start(f32[4,512,512]{2,1,0:T(8,128)} %refs_5_.1) | copy-start | bytes 12582916
  23.3 36.8 %copy-start.3 = (f32[8,1,128,32]{2,3,1,0:T(8,128)S(1)}, f32[8,1,128,32]{2,3,1,0:T(8,128)}, u32[]{:S(2)}) copy-start(f32[8,1,128,32]{2,3,1,0:T(8,128)} %param.4) | copy-start | bytes 393220
  23.3 3.9 %collective-permute-start.4 = (f32[1,32,128]{2,1,0:T(8,128)S(1)}, f32[1,32,128]{2,1,0:T(8,128)S(1)}, u32[]{:S(2)}, u32[]{:S(2)}) collective-permute-start(f32[1,32,128]{2,1,0:T(8,128)S(1)} %shard_map.59.own_ref), channel_id=1, source_target_pairs={{32,80},{40,88},{48,64},{56,72},{33,81},{41,89},{49,65},{57,73},{3... | collective-permute-start | bytes 49160 | tf_op jit(solution)/shard_map/ppermute | solution.py:198
  24.1 3.1 %collective-permute-start.5 = (f32[1,32,128]{2,1,0:T(8,128)S(1)}, f32[1,32,128]{2,1,0:T(8,128)S(1)}, u32[]{:S(2)}, u32[]{:S(2)}) collective-permute-start(f32[1,32,128]{2,1,0:T(8,128)S(1)} %shard_map.59.own_ref), channel_id=1, source_target_pairs={{32,88},{40,80},{48,72},{56,64},{33,89},{41,81},{49,73},{57,65},{3... | collective-permute-start | bytes 49160 | tf_op jit(solution)/shard_map/ppermute | solution.py:198
  24.9 2.3 %collective-permute-start.6 = (f32[1,32,128]{2,1,0:T(8,128)S(1)}, f32[1,32,128]{2,1,0:T(8,128)S(1)}, u32[]{:S(2)}, u32[]{:S(2)}) collective-permute-start(f32[1,32,128]{2,1,0:T(8,128)S(1)} %shard_map.59.own_ref), channel_id=1, source_target_pairs={{32,72},{40,64},{48,88},{56,80},{33,73},{41,65},{49,89},{57,81},{3... | collective-permute-start | bytes 49160 | tf_op jit(solution)/shard_map/ppermute | solution.py:198
  25.7 1.5 %collective-permute-start.7 = (f32[1,32,128]{2,1,0:T(8,128)S(1)}, f32[1,32,128]{2,1,0:T(8,128)S(1)}, u32[]{:S(2)}, u32[]{:S(2)}) collective-permute-start(f32[1,32,128]{2,1,0:T(8,128)S(1)} %shard_map.59.own_ref), channel_id=1, source_target_pairs={{32,64},{40,72},{48,80},{56,88},{33,65},{41,73},{49,81},{57,89},{3... | collective-permute-start | bytes 49160 | tf_op jit(solution)/shard_map/ppermute | solution.py:198
  46.6 12.1 %all-to-all-start.1 = ((f32[16,32,128]{2,1,0:T(8,128)}), f32[16,32,128]{2,1,0:T(8,128)S(1)}, u32[]{:S(2)}, u32[]{:S(2)}) async-start(f32[16,32,128]{2,1,0:T(8,128)} %get-tuple-element.29), calls=%async_computation.1 | async-start | bytes 524288 | tf_op jit(solution)/shard_map/all_to_all | solution.py:235
  51.0 9.1 %collective-permute-start.12 = (f32[12,32,128]{2,1,0:T(8,128)S(1)}, f32[12,32,128]{2,1,0:T(8,128)S(1)}, u32[]{:S(2)}, u32[]{:S(2)}) collective-permute-start(f32[12,32,128]{2,1,0:T(8,128)S(1)} %get-tuple-element.31.refs_0_), channel_id=1, source_target_pairs={{0,128},{64,192},{1,129},{65,193},{2,130},{66,194},{3,131},{67,195... | collective-permute-start | bytes 589832 | tf_op jit(solution)/shard_map/ppermute | solution.py:38
  58.8 10.1 %collective-permute-start.13 = (f32[4,32,128]{2,1,0:T(8,128)S(1)}, f32[4,32,128]{2,1,0:T(8,128)S(1)}, u32[]{:S(2)}, u32[]{:S(2)}) collective-permute-start(f32[4,32,128]{2,1,0:T(8,128)S(1)} %slice.26.refs_0_), channel_id=1, source_target_pairs={{0,192},{64,128},{1,193},{65,129},{2,194},{66,130},{3,195},{67,131... | collective-permute-start | bytes 196616 | tf_op jit(solution)/shard_map/ppermute | solution.py:38
  60.1 3.4 %copy-start = (f32[8,1,128,2048]{3,2,1,0:T(8,128)S(1)}, f32[8,1,128,2048]{3,2,1,0:T(8,128)}, u32[]{:S(2)}) copy-start(f32[8,1,128,2048]{3,2,1,0:T(8,128)} %param.3) | copy-start | bytes 25165828
  63.5 2.2 %copy-start.2 = (f32[4,512,512]{2,1,0:T(8,128)S(1)}, f32[4,512,512]{2,1,0:T(8,128)}, u32[]{:S(2)}) copy-start(f32[4,512,512]{2,1,0:T(8,128)} %refs_5_.1) | copy-start | bytes 12582916
  70.1 6.7 %collective-permute-start.14 = (f32[2,8,128]{2,1,0:T(8,128)S(1)}, f32[2,8,128]{2,1,0:T(8,128)S(1)}, u32[]{:S(2)}, u32[]{:S(2)}) collective-permute-start(f32[2,8,128]{2,1,0:T(8,128)S(1)} %get-tuple-element.40), channel_id=1, source_target_pairs={{0,1},{1,0},{2,3},{3,2},{4,5},{5,4},{6,7},{7,6},{8,9},{9,8},{10,11... | collective-permute-start | bytes 24584 | tf_op jit(solution)/shard_map/ppermute | solution.py:249
  76.8 4.4 %collective-permute-start.16 = (f32[2,8,128]{2,1,0:T(8,128)S(1)}, f32[2,8,128]{2,1,0:T(8,128)S(1)}, u32[]{:S(2)}, u32[]{:S(2)}) collective-permute-start(f32[2,8,128]{2,1,0:T(8,128)S(1)} %add.12), channel_id=1, source_target_pairs={{0,4},{2,6},{4,0},{6,2},{1,5},{3,7},{5,1},{7,3},{8,12},{10,14},{12... | collective-permute-start | bytes 24584 | tf_op jit(solution)/shard_map/ppermute | solution.py:252
  79.7 3.7 %collective-permute-start.17 = (f32[2,8,128]{2,1,0:T(8,128)S(1)}, f32[2,8,128]{2,1,0:T(8,128)S(1)}, u32[]{:S(2)}, u32[]{:S(2)}) collective-permute-start(f32[2,8,128]{2,1,0:T(8,128)S(1)} %add.12), channel_id=1, source_target_pairs={{0,6},{2,4},{4,2},{6,0},{1,7},{3,5},{5,3},{7,1},{8,14},{10,12},{12... | collective-permute-start | bytes 24584 | tf_op jit(solution)/shard_map/ppermute | solution.py:252
  80.5 2.9 %collective-permute-start.15 = (f32[2,8,128]{2,1,0:T(8,128)S(1)}, f32[2,8,128]{2,1,0:T(8,128)S(1)}, u32[]{:S(2)}, u32[]{:S(2)}) collective-permute-start(f32[2,8,128]{2,1,0:T(8,128)S(1)} %add.12), channel_id=1, source_target_pairs={{0,2},{2,0},{4,6},{6,4},{1,3},{3,1},{5,7},{7,5},{8,10},{10,8},{12,... | collective-permute-start | bytes 24584 | tf_op jit(solution)/shard_map/ppermute | solution.py:252

commit v12 on v11

--- a/solution.py
+++ b/solution.py
@@ -247,10 +247,8 @@
         1 << 28, 4 << 20, ends, *late, own, partly, panel, inverses,
     )
     sums = sums + lax.ppermute(sums, "core", [(0, 1), (1, 0)])
-    others = []
-    for change in (1, 2, 3):
-        others.append(lax.ppermute(sums, "y", [(i, i ^ change) for i in range(4)]))
-    sums = sums + others[0] + (others[1] + others[2])
+    for change in (1, 3):
+        sums = sums + lax.ppermute(sums, "y", [(i, i ^ change) for i in range(4)])
     solved = jnp.concatenate([before, last], axis=1)
     left = jnp.concatenate([low, high], axis=0)
     size = members * 8

time: 85 us -> 85.5 us (level)
  the two profiles are of different devices: /device:TPU:1 before, /device:TPU:32 now
where the time goes in v12:
time: 85.5 us; the launch traced here: 84.9 us
  starting transfers between devices  32 us (37%)
  blocking collectives  22.8 us (27%)
  waiting for transfers between devices  11.5 us (13%)
  local copies, waits for them, and re-layouts  8.71 us (10%)
  Pallas kernels  6.99 us (8%)
  other arithmetic  1.99 us (2%)
  between operations  0.98 us (1%)
    all_to_all x1, blocking collectives, shards(): tiles = lax.all_to_all(copies, OWNERS, 0, 0)  22.8 us
    ppermute x12, starting transfers between devices, forward(): lax.ppermute(value, ROWS, [(source + i, target + (i ^ change)) for i in r...  20.5 us
    all_to_all x1, waiting for transfers between devices, shards(): received = lax.all_to_all(copies, OWNERS, 0, 0)  7.75 us
    pallas_call x7, Pallas kernels, local(): pl.pallas_call(body, out_shape=outs, in_specs=[VMEM] * len(args), out_spe...  6.99 us
    unnamed x12, local copies, waits for them, and re-layouts  5.71 us
    ppermute x2, starting transfers between devices, shards(): sums = sums + lax.ppermute(sums, 'y', [(i, i ^ change) for i in range(4)])  4.58 us
    all_to_all x1, starting transfers between devices, shards(): received = lax.all_to_all(copies, OWNERS, 0, 0)  4.2 us
    ppermute x2, starting transfers between devices, crossings(): return [lax.ppermute(value, ROWS[:2], pairs)]  2.57 us
  transfers between devices with their start and end apart: 18, of which 4 were waited for; matrix products, arithmetic and copies ran while one was open for 4% of the time, Pallas kernels for 5%

profile of v12, /device:TPU:32, one launch (start us, length us, event | category | flops | bytes accessed | tf_op | source)
XLA Modules:
  0.0 84.9 jit_solution(8996056670079217586)
XLA Ops:
  0.6 0.7 slice_bitcast_fusion.2
  1.4 7.3 %collective-permute-start = (f32[1,32,128]{2,1,0:T(8,128)S(1)}, f32[1,32,128]{2,1,0:T(8,128)S(1)}, u32[]{:S(2)}, u32[]{:S(2)}) collective-permute-start(f32[1,32,128]{2,1,0:T(8,128)S(1)} %get-tuple-element.45), channel_id=1, source_target_pairs={{0,48},{8,56},{16,32},{24,40},{1,49},{9,57},{17,33},{25,41},{2,50}... | collective-permute-start | bytes 49160 | tf_op jit(solution)/shard_map/ppermute | solution.py:198
  8.7 1.7 %collective-permute-start.1 = (f32[1,32,128]{2,1,0:T(8,128)S(1)}, f32[1,32,128]{2,1,0:T(8,128)S(1)}, u32[]{:S(2)}, u32[]{:S(2)}) collective-permute-start(f32[1,32,128]{2,1,0:T(8,128)S(1)} %get-tuple-element.45), channel_id=1, source_target_pairs={{0,56},{8,48},{16,40},{24,32},{1,57},{9,49},{17,41},{25,33},{2,58}... | collective-permute-start | bytes 49160 | tf_op jit(solution)/shard_map/ppermute | solution.py:198
  10.4 1.3 %collective-permute-start.2 = (f32[1,32,128]{2,1,0:T(8,128)S(1)}, f32[1,32,128]{2,1,0:T(8,128)S(1)}, u32[]{:S(2)}, u32[]{:S(2)}) collective-permute-start(f32[1,32,128]{2,1,0:T(8,128)S(1)} %get-tuple-element.45), channel_id=1, source_target_pairs={{0,40},{8,32},{16,56},{24,48},{1,41},{9,33},{17,57},{25,49},{2,42}... | collective-permute-start | bytes 49160 | tf_op jit(solution)/shard_map/ppermute | solution.py:198
  11.7 1.7 %collective-permute-start.3 = (f32[1,32,128]{2,1,0:T(8,128)S(1)}, f32[1,32,128]{2,1,0:T(8,128)S(1)}, u32[]{:S(2)}, u32[]{:S(2)}) collective-permute-start(f32[1,32,128]{2,1,0:T(8,128)S(1)} %get-tuple-element.45), channel_id=1, source_target_pairs={{0,32},{8,40},{16,48},{24,56},{1,33},{9,41},{17,49},{25,57},{2,34}... | collective-permute-start | bytes 49160 | tf_op jit(solution)/shard_map/ppermute | solution.py:198
  13.4 1.3 %collective-permute-start.8 = (f32[1,32,128]{2,1,0:T(8,128)S(1)}, f32[1,32,128]{2,1,0:T(8,128)S(1)}, u32[]{:S(2)}, u32[]{:S(2)}) collective-permute-start(f32[1,32,128]{2,1,0:T(8,128)S(1)} %get-tuple-element.45), channel_id=1, source_target_pairs={{0,80},{8,88},{16,64},{24,72},{1,81},{9,89},{17,65},{25,73},{2,82}... | collective-permute-start | bytes 49160 | tf_op jit(solution)/shard_map/ppermute | solution.py:198
  14.7 1.0 %slice_bitcast_fusion.1.part_ref = f32[128,512]{1,0:T(8,128)S(1)} fusion(f32[8,128,2048]{2,1,0:T(8,128)} %bitcast.21), kind=kLoop, calls=%fused_computation.1 | loop fusion | bytes 524288 | tf_op jit(solution)/shard_map/squeeze | solution.py:219
  15.7 1.3 %slice_bitcast_fusion.inverse_ref = f32[512,512]{1,0:T(8,128)S(1)} fusion(f32[4,512,512]{2,1,0:T(8,128)} %refs_5_.1), kind=kLoop, calls=%fused_computation | loop fusion | bytes 2097152 | tf_op jit(solution)/shard_map/squeeze | solution.py:219
  17.0 0.0 slice-start
  17.0 0.4 shard_map.58
  17.4 0.0 collective-permute-done.r0
  17.4 1.6 %collective-permute-start.9 = (f32[1,32,128]{2,1,0:T(8,128)S(1)}, f32[1,32,128]{2,1,0:T(8,128)S(1)}, u32[]{:S(2)}, u32[]{:S(2)}) collective-permute-start(f32[1,32,128]{2,1,0:T(8,128)S(1)} %get-tuple-element.45), channel_id=1, source_target_pairs={{0,88},{8,80},{16,72},{24,64},{1,89},{9,81},{17,73},{25,65},{2,90}... | collective-permute-start | bytes 49160 | tf_op jit(solution)/shard_map/ppermute | solution.py:198
  19.0 0.0 collective-permute-done.1.r1
  19.0 1.3 %collective-permute-start.10 = (f32[1,32,128]{2,1,0:T(8,128)S(1)}, f32[1,32,128]{2,1,0:T(8,128)S(1)}, u32[]{:S(2)}, u32[]{:S(2)}) collective-permute-start(f32[1,32,128]{2,1,0:T(8,128)S(1)} %get-tuple-element.45), channel_id=1, source_target_pairs={{0,72},{8,64},{16,88},{24,80},{1,73},{9,65},{17,89},{25,81},{2,74}... | collective-permute-start | bytes 49160 | tf_op jit(solution)/shard_map/ppermute | solution.py:198
  20.3 0.0 collective-permute-done.2.r2
  20.3 1.3 %collective-permute-start.11 = (f32[1,32,128]{2,1,0:T(8,128)S(1)}, f32[1,32,128]{2,1,0:T(8,128)S(1)}, u32[]{:S(2)}, u32[]{:S(2)}) collective-permute-start(f32[1,32,128]{2,1,0:T(8,128)S(1)} %get-tuple-element.45), channel_id=1, source_target_pairs={{0,64},{8,72},{16,80},{24,88},{1,65},{9,73},{17,81},{25,89},{2,66}... | collective-permute-start | bytes 49160 | tf_op jit(solution)/shard_map/ppermute | solution.py:198
  21.6 0.0 collective-permute-done.3.r3
  21.6 0.0 slice-start.1
  21.6 0.0 copy-start.1
  21.6 0.2 shard_map.59.own_ref
  21.8 0.0 copy-start.3
  21.8 0.8 collective-permute-start.4
  22.6 0.0 collective-permute-done.8.f0
  22.7 0.8 collective-permute-start.5
  23.5 0.0 collective-permute-done.9.f1
  23.5 0.8 collective-permute-start.6
  24.3 0.0 collective-permute-done.10.f2
  24.3 0.7 collective-permute-start.7
  25.0 0.0 slice-done
  25.0 0.0 slice-done.1
  25.0 0.1 copy-done.1
  25.1 0.6 shard_map.60
  25.7 0.0 collective-permute-done.11.f3
  25.7 0.0 collective-permute-done.4.r0
  25.7 0.0 collective-permute-done.5.r1
  25.7 0.0 collective-permute-done.6.r2
  25.7 0.0 collective-permute-done.7.r3
  25.7 0.3 shard_map.61
  26.1 22.8 %all_to_all.10.tiles_ref = f32[16,32,128]{2,1,0:T(8,128)S(1)} all-to-all(f32[16,32,128]{2,1,0:T(8,128)S(1)} %get-tuple-element.26), channel_id=1, replica_groups=mesh['xh'=2,'xl'=2,'zh'=2,'zl'=4,'y'=4,'core'=2] {'xl','zh','zl'}, dimensions={0} | all-to-all | bytes 524288 | tf_op jit(solution)/shard_map/all_to_all | solution.py:229
  48.9 1.1 %shard_map.62 = (f32[16,32,128]{2,1,0:T(8,128)}, f32[32,128]{1,0:T(8,128)S(1)}, f32[12,32,128]{2,1,0:T(8,128)S(1)}) custom-call(f32[16,32,128]{2,1,0:T(8,128)S(1)} %all_to_all.10.tiles_ref, f32[32,128]{1,0:T(8,128)S(1)} %get-tuple-element.27.own_ref, bf16[128,512]{1,0:T(8,128)(2,1)S(1)} %get-tuple-element.22.high_ref.h0, ...), custom_call_target="tpu_custom_call" | custom-call | flops 134217728 | bytes 2097152 | tf_op jit(solution)/shard_map/pallas_call | solution.py:185
  50.0 4.2 %all-to-all-start.1 = ((f32[16,32,128]{2,1,0:T(8,128)}), f32[16,32,128]{2,1,0:T(8,128)S(1)}, u32[]{:S(2)}, u32[]{:S(2)}) async-start(f32[16,32,128]{2,1,0:T(8,128)} %get-tuple-element.29), calls=%async_computation.1 | async-start | bytes 524288 | tf_op jit(solution)/shard_map/all_to_all | solution.py:235
  54.1 1.3 %collective-permute-start.12 = (f32[12,32,128]{2,1,0:T(8,128)S(1)}, f32[12,32,128]{2,1,0:T(8,128)S(1)}, u32[]{:S(2)}, u32[]{:S(2)}) collective-permute-start(f32[12,32,128]{2,1,0:T(8,128)S(1)} %get-tuple-element.31.refs_0_), channel_id=1, source_target_pairs={{0,128},{64,192},{1,129},{65,193},{2,130},{66,194},{3,131},{67,195... | collective-permute-start | bytes 589832 | tf_op jit(solution)/shard_map/ppermute | solution.py:38
  55.4 7.8 %all-to-all-done.1 = f32[16,32,128]{2,1,0:T(8,128)S(1)} async-done(((f32[16,32,128]{2,1,0:T(8,128)}), f32[16,32,128]{2,1,0:T(8,128)S(1)}, u32[]{:S(2)}, u32[]{:S(2)}) %all-to-all-start.1) | async-done | bytes 262176 | tf_op jit(solution)/shard_map/all_to_all | solution.py:235
  63.2 1.3 %collective-permute-start.13 = (f32[4,32,128]{2,1,0:T(8,128)S(1)}, f32[4,32,128]{2,1,0:T(8,128)S(1)}, u32[]{:S(2)}, u32[]{:S(2)}) collective-permute-start(f32[4,32,128]{2,1,0:T(8,128)S(1)} %slice.26.refs_0_), channel_id=1, source_target_pairs={{0,192},{64,128},{1,193},{65,129},{2,194},{66,130},{3,195},{67,131... | collective-permute-start | bytes 196616 | tf_op jit(solution)/shard_map/ppermute | solution.py:38
  64.5 0.0 collective-permute-done.12.refs_1_
  64.5 0.0 copy-done.3
  64.5 0.0 copy-start
  64.5 3.4 %copy-done = f32[8,1,128,2048]{3,2,1,0:T(8,128)S(1)} copy-done((f32[8,1,128,2048]{3,2,1,0:T(8,128)S(1)}, f32[8,1,128,2048]{3,2,1,0:T(8,128)}, u32[]{:S(2)}) %copy-start) | copy-done | bytes 8388632
  67.9 0.0 copy-start.2
  67.9 2.2 %copy-done.2 = f32[4,512,512]{2,1,0:T(8,128)S(1)} copy-done((f32[4,512,512]{2,1,0:T(8,128)S(1)}, f32[4,512,512]{2,1,0:T(8,128)}, u32[]{:S(2)}) %copy-start.2) | copy-done | bytes 4194328
  70.1 3.2 %shard_map.63 = (f32[32,1536]{1,0:T(8,128)S(1)}, f32[8,32,128]{2,1,0:T(8,128)S(1)}) custom-call(f32[12,32,128]{2,1,0:T(8,128)S(1)} %get-tuple-element.31.refs_0_, f32[12,32,128]{2,1,0:T(8,128)S(1)} %collective-permute-done.12.refs_1_, f32[8,32,128]{2,1,0:T(8,128)S(1)} %bitcast.28, f32[8,128,2048]{2,1,0:T(8,128)S(1)} %bitcast.25, f32[4,512,512]{2,1,0:T(8,128)S(1)} %copy-done.2), custom_call_target="tpu_custom_call" | custom-call | flops 1073741824 | bytes 12582912 | tf_op jit(solution)/shard_map/pallas_call | solution.py:185
  73.3 0.0 collective-permute-done.13.refs_1_
  73.3 1.2 %shard_map.64 = (f32[32,512]{1,0:T(8,128)S(1)}, f32[4,32,128]{2,1,0:T(8,128)S(1)}, f32[4,32,128]{2,1,0:T(8,128)S(1)}, f32[2,8,128]{2,1,0:T(8,128)S(1)}) custom-call(f32[4,32,128]{2,1,0:T(8,128)S(1)} %slice.26.refs_0_, f32[4,32,128]{2,1,0:T(8,128)S(1)} %collective-permute-done.13.refs_1_, f32[32,128]{1,0:T(8,128)S(1)} %get-tuple-element.35.refs_2_, ...), custom_call_target="tpu_custom_call" | custom-call | flops 268435456 | bytes 4194304 | tf_op jit(solution)/shard_map/pallas_call | solution.py:185
  74.5 0.1 collective-permute-start.14
  74.6 1.2 %collective-permute-done.14 = f32[2,8,128]{2,1,0:T(8,128)S(1)} collective-permute-done((f32[2,8,128]{2,1,0:T(8,128)S(1)}, f32[2,8,128]{2,1,0:T(8,128)S(1)}, u32[]{:S(2)}, u32[]{:S(2)}) %collective-permute-start.14) | collective-permute-done | bytes 8224 | tf_op jit(solution)/shard_map/ppermute | solution.py:249
  75.8 1.6 %collective-permute-start.15 = (f32[2,8,128]{2,1,0:T(8,128)S(1)}, f32[2,8,128]{2,1,0:T(8,128)S(1)}, u32[]{:S(2)}, u32[]{:S(2)}) collective-permute-start(f32[2,8,128]{2,1,0:T(8,128)S(1)} %add.9), channel_id=1, source_target_pairs={{0,2},{2,0},{4,6},{6,4},{1,3},{3,1},{5,7},{7,5},{8,10},{10,8},{12,... | collective-permute-start | bytes 24584 | tf_op jit(solution)/shard_map/ppermute | solution.py:251
  77.4 0.7 maximum_bitcast_fusion
  78.1 1.4 %collective-permute-done.15 = f32[2,8,128]{2,1,0:T(8,128)S(1)} collective-permute-done((f32[2,8,128]{2,1,0:T(8,128)S(1)}, f32[2,8,128]{2,1,0:T(8,128)S(1)}, u32[]{:S(2)}, u32[]{:S(2)}) %collective-permute-start.15) | collective-permute-done | bytes 8224 | tf_op jit(solution)/shard_map/ppermute | solution.py:251
  79.5 3.0 %collective-permute-start.16 = (f32[2,8,128]{2,1,0:T(8,128)S(1)}, f32[2,8,128]{2,1,0:T(8,128)S(1)}, u32[]{:S(2)}, u32[]{:S(2)}) collective-permute-start(f32[2,8,128]{2,1,0:T(8,128)S(1)} %add.10), channel_id=1, source_target_pairs={{0,6},{2,4},{4,2},{6,0},{1,7},{3,5},{5,3},{7,1},{8,14},{10,12},{12... | collective-permute-start | bytes 24584 | tf_op jit(solution)/shard_map/ppermute | solution.py:251
  82.5 0.7 maximum_bitcast_fusion.1
  83.1 1.2 %collective-permute-done.16 = f32[2,8,128]{2,1,0:T(8,128)S(1)} collective-permute-done((f32[2,8,128]{2,1,0:T(8,128)S(1)}, f32[2,8,128]{2,1,0:T(8,128)S(1)}, u32[]{:S(2)}, u32[]{:S(2)}) %collective-permute-start.16) | collective-permute-done | bytes 8224 | tf_op jit(solution)/shard_map/ppermute | solution.py:251
  84.3 0.6 fusion.1
  (5 shorter events, 0.0 us)
Async XLA Ops:
  1.4 16.1 %collective-permute-start = (f32[1,32,128]{2,1,0:T(8,128)S(1)}, f32[1,32,128]{2,1,0:T(8,128)S(1)}, u32[]{:S(2)}, u32[]{:S(2)}) collective-permute-start(f32[1,32,128]{2,1,0:T(8,128)S(1)} %get-tuple-element.45), channel_id=1, source_target_pairs={{0,48},{8,56},{16,32},{24,40},{1,49},{9,57},{17,33},{25,41},{2,50}... | collective-permute-start | bytes 49160 | tf_op jit(solution)/shard_map/ppermute | solution.py:198
  8.7 10.3 %collective-permute-start.1 = (f32[1,32,128]{2,1,0:T(8,128)S(1)}, f32[1,32,128]{2,1,0:T(8,128)S(1)}, u32[]{:S(2)}, u32[]{:S(2)}) collective-permute-start(f32[1,32,128]{2,1,0:T(8,128)S(1)} %get-tuple-element.45), channel_id=1, source_target_pairs={{0,56},{8,48},{16,40},{24,32},{1,57},{9,49},{17,41},{25,33},{2,58}... | collective-permute-start | bytes 49160 | tf_op jit(solution)/shard_map/ppermute | solution.py:198
  10.4 9.9 %collective-permute-start.2 = (f32[1,32,128]{2,1,0:T(8,128)S(1)}, f32[1,32,128]{2,1,0:T(8,128)S(1)}, u32[]{:S(2)}, u32[]{:S(2)}) collective-permute-start(f32[1,32,128]{2,1,0:T(8,128)S(1)} %get-tuple-element.45), channel_id=1, source_target_pairs={{0,40},{8,32},{16,56},{24,48},{1,41},{9,33},{17,57},{25,49},{2,42}... | collective-permute-start | bytes 49160 | tf_op jit(solution)/shard_map/ppermute | solution.py:198
  11.7 9.9 %collective-permute-start.3 = (f32[1,32,128]{2,1,0:T(8,128)S(1)}, f32[1,32,128]{2,1,0:T(8,128)S(1)}, u32[]{:S(2)}, u32[]{:S(2)}) collective-permute-start(f32[1,32,128]{2,1,0:T(8,128)S(1)} %get-tuple-element.45), channel_id=1, source_target_pairs={{0,32},{8,40},{16,48},{24,56},{1,33},{9,41},{17,49},{25,57},{2,34}... | collective-permute-start | bytes 49160 | tf_op jit(solution)/shard_map/ppermute | solution.py:198
  13.4 9.2 %collective-permute-start.8 = (f32[1,32,128]{2,1,0:T(8,128)S(1)}, f32[1,32,128]{2,1,0:T(8,128)S(1)}, u32[]{:S(2)}, u32[]{:S(2)}) collective-permute-start(f32[1,32,128]{2,1,0:T(8,128)S(1)} %get-tuple-element.45), channel_id=1, source_target_pairs={{0,80},{8,88},{16,64},{24,72},{1,81},{9,89},{17,65},{25,73},{2,82}... | collective-permute-start | bytes 49160 | tf_op jit(solution)/shard_map/ppermute | solution.py:198
  17.0 7.9 %slice-start = ((s8[8388608]{0:T(1024)(128)(4,1)}), s8[4194304]{0:T(1024)(128)(4,1)S(1)}, s32[]{:S(2)}) async-start(s8[8388608]{0:T(1024)(128)(4,1)} %bitcast.22), calls=%async_computation.2 | async-start | bytes 8388608
  17.4 6.0 %collective-permute-start.9 = (f32[1,32,128]{2,1,0:T(8,128)S(1)}, f32[1,32,128]{2,1,0:T(8,128)S(1)}, u32[]{:S(2)}, u32[]{:S(2)}) collective-permute-start(f32[1,32,128]{2,1,0:T(8,128)S(1)} %get-tuple-element.45), channel_id=1, source_target_pairs={{0,88},{8,80},{16,72},{24,64},{1,89},{9,81},{17,73},{25,65},{2,90}... | collective-permute-start | bytes 49160 | tf_op jit(solution)/shard_map/ppermute | solution.py:198
  19.0 5.3 %collective-permute-start.10 = (f32[1,32,128]{2,1,0:T(8,128)S(1)}, f32[1,32,128]{2,1,0:T(8,128)S(1)}, u32[]{:S(2)}, u32[]{:S(2)}) collective-permute-start(f32[1,32,128]{2,1,0:T(8,128)S(1)} %get-tuple-element.45), channel_id=1, source_target_pairs={{0,72},{8,64},{16,88},{24,80},{1,73},{9,65},{17,89},{25,81},{2,74}... | collective-permute-start | bytes 49160 | tf_op jit(solution)/shard_map/ppermute | solution.py:198
  20.3 5.4 %collective-permute-start.11 = (f32[1,32,128]{2,1,0:T(8,128)S(1)}, f32[1,32,128]{2,1,0:T(8,128)S(1)}, u32[]{:S(2)}, u32[]{:S(2)}) collective-permute-start(f32[1,32,128]{2,1,0:T(8,128)S(1)} %get-tuple-element.45), channel_id=1, source_target_pairs={{0,64},{8,72},{16,80},{24,88},{1,65},{9,73},{17,81},{25,89},{2,66}... | collective-permute-start | bytes 49160 | tf_op jit(solution)/shard_map/ppermute | solution.py:198
  21.6 3.4 %slice-start.1 = ((s8[8388608]{0:T(1024)(128)(4,1)}), s8[4194304]{0:T(1024)(128)(4,1)S(1)}, s32[]{:S(2)}) async-start(s8[8388608]{0:T(1024)(128)(4,1)} %bitcast.22), calls=%async_computation.3 | async-start | bytes 8388608
  21.6 3.5 %copy-start.1 = (f32[4,512,512]{2,1,0:T(8,128)S(1)}, f32[4,512,512]{2,1,0:T(8,128)}, u32[]{:S(2)}) copy-start(f32[4,512,512]{2,1,0:T(8,128)} %refs_5_.1) | copy-start | bytes 12582916
  21.8 42.7 %copy-start.3 = (f32[8,1,128,32]{2,3,1,0:T(8,128)S(1)}, f32[8,1,128,32]{2,3,1,0:T(8,128)}, u32[]{:S(2)}) copy-start(f32[8,1,128,32]{2,3,1,0:T(8,128)} %param.4) | copy-start | bytes 393220
  21.8 3.9 %collective-permute-start.4 = (f32[1,32,128]{2,1,0:T(8,128)S(1)}, f32[1,32,128]{2,1,0:T(8,128)S(1)}, u32[]{:S(2)}, u32[]{:S(2)}) collective-permute-start(f32[1,32,128]{2,1,0:T(8,128)S(1)} %shard_map.59.own_ref), channel_id=1, source_target_pairs={{32,80},{40,88},{48,64},{56,72},{33,81},{41,89},{49,65},{57,73},{3... | collective-permute-start | bytes 49160 | tf_op jit(solution)/shard_map/ppermute | solution.py:198
  22.7 3.1 %collective-permute-start.5 = (f32[1,32,128]{2,1,0:T(8,128)S(1)}, f32[1,32,128]{2,1,0:T(8,128)S(1)}, u32[]{:S(2)}, u32[]{:S(2)}) collective-permute-start(f32[1,32,128]{2,1,0:T(8,128)S(1)} %shard_map.59.own_ref), channel_id=1, source_target_pairs={{32,88},{40,80},{48,72},{56,64},{33,89},{41,81},{49,73},{57,65},{3... | collective-permute-start | bytes 49160 | tf_op jit(solution)/shard_map/ppermute | solution.py:198
  23.5 2.3 %collective-permute-start.6 = (f32[1,32,128]{2,1,0:T(8,128)S(1)}, f32[1,32,128]{2,1,0:T(8,128)S(1)}, u32[]{:S(2)}, u32[]{:S(2)}) collective-permute-start(f32[1,32,128]{2,1,0:T(8,128)S(1)} %shard_map.59.own_ref), channel_id=1, source_target_pairs={{32,72},{40,64},{48,88},{56,80},{33,73},{41,65},{49,89},{57,81},{3... | collective-permute-start | bytes 49160 | tf_op jit(solution)/shard_map/ppermute | solution.py:198
  24.3 1.5 %collective-permute-start.7 = (f32[1,32,128]{2,1,0:T(8,128)S(1)}, f32[1,32,128]{2,1,0:T(8,128)S(1)}, u32[]{:S(2)}, u32[]{:S(2)}) collective-permute-start(f32[1,32,128]{2,1,0:T(8,128)S(1)} %shard_map.59.own_ref), channel_id=1, source_target_pairs={{32,64},{40,72},{48,80},{56,88},{33,65},{41,73},{49,81},{57,89},{3... | collective-permute-start | bytes 49160 | tf_op jit(solution)/shard_map/ppermute | solution.py:198
  50.0 13.2 %all-to-all-start.1 = ((f32[16,32,128]{2,1,0:T(8,128)}), f32[16,32,128]{2,1,0:T(8,128)S(1)}, u32[]{:S(2)}, u32[]{:S(2)}) async-start(f32[16,32,128]{2,1,0:T(8,128)} %get-tuple-element.29), calls=%async_computation.1 | async-start | bytes 524288 | tf_op jit(solution)/shard_map/all_to_all | solution.py:235
  54.1 10.3 %collective-permute-start.12 = (f32[12,32,128]{2,1,0:T(8,128)S(1)}, f32[12,32,128]{2,1,0:T(8,128)S(1)}, u32[]{:S(2)}, u32[]{:S(2)}) collective-permute-start(f32[12,32,128]{2,1,0:T(8,128)S(1)} %get-tuple-element.31.refs_0_), channel_id=1, source_target_pairs={{0,128},{64,192},{1,129},{65,193},{2,130},{66,194},{3,131},{67,195... | collective-permute-start | bytes 589832 | tf_op jit(solution)/shard_map/ppermute | solution.py:38
  63.2 10.1 %collective-permute-start.13 = (f32[4,32,128]{2,1,0:T(8,128)S(1)}, f32[4,32,128]{2,1,0:T(8,128)S(1)}, u32[]{:S(2)}, u32[]{:S(2)}) collective-permute-start(f32[4,32,128]{2,1,0:T(8,128)S(1)} %slice.26.refs_0_), channel_id=1, source_target_pairs={{0,192},{64,128},{1,193},{65,129},{2,194},{66,130},{3,195},{67,131... | collective-permute-start | bytes 196616 | tf_op jit(solution)/shard_map/ppermute | solution.py:38
  64.5 3.4 %copy-start = (f32[8,1,128,2048]{3,2,1,0:T(8,128)S(1)}, f32[8,1,128,2048]{3,2,1,0:T(8,128)}, u32[]{:S(2)}) copy-start(f32[8,1,128,2048]{3,2,1,0:T(8,128)} %param.3) | copy-start | bytes 25165828
  67.9 2.2 %copy-start.2 = (f32[4,512,512]{2,1,0:T(8,128)S(1)}, f32[4,512,512]{2,1,0:T(8,128)}, u32[]{:S(2)}) copy-start(f32[4,512,512]{2,1,0:T(8,128)} %refs_5_.1) | copy-start | bytes 12582916
  74.5 1.3 %collective-permute-start.14 = (f32[2,8,128]{2,1,0:T(8,128)S(1)}, f32[2,8,128]{2,1,0:T(8,128)S(1)}, u32[]{:S(2)}, u32[]{:S(2)}) collective-permute-start(f32[2,8,128]{2,1,0:T(8,128)S(1)} %get-tuple-element.40), channel_id=1, source_target_pairs={{0,1},{1,0},{2,3},{3,2},{4,5},{5,4},{6,7},{7,6},{8,9},{9,8},{10,11... | collective-permute-start | bytes 24584 | tf_op jit(solution)/shard_map/ppermute | solution.py:249
  75.8 3.7 %collective-permute-start.15 = (f32[2,8,128]{2,1,0:T(8,128)S(1)}, f32[2,8,128]{2,1,0:T(8,128)S(1)}, u32[]{:S(2)}, u32[]{:S(2)}) collective-permute-start(f32[2,8,128]{2,1,0:T(8,128)S(1)} %add.9), channel_id=1, source_target_pairs={{0,2},{2,0},{4,6},{6,4},{1,3},{3,1},{5,7},{7,5},{8,10},{10,8},{12,... | collective-permute-start | bytes 24584 | tf_op jit(solution)/shard_map/ppermute | solution.py:251
  79.5 4.9 %collective-permute-start.16 = (f32[2,8,128]{2,1,0:T(8,128)S(1)}, f32[2,8,128]{2,1,0:T(8,128)S(1)}, u32[]{:S(2)}, u32[]{:S(2)}) collective-permute-start(f32[2,8,128]{2,1,0:T(8,128)S(1)} %add.10), channel_id=1, source_target_pairs={{0,6},{2,4},{4,2},{6,0},{1,7},{3,5},{5,3},{7,1},{8,14},{10,12},{12... | collective-permute-start | bytes 24584 | tf_op jit(solution)/shard_map/ppermute | solution.py:251

commit v13 on v12

--- a/solution.py
+++ b/solution.py
@@ -20,6 +20,7 @@
 SOURCES = 2
 GROUP = 16
 ORDER = (2, 3, 1, 0)
+PAIRS = (2, 0)
 
 
 def line_of():
@@ -109,14 +110,26 @@
     return jnp.where(step_of() == steps, own_ref[...] - change, own_ref[...])
 
 
-def first_body(r0, r1, r2, r3, own_ref, high_ref, low_ref, own_out_ref):
-    tiles = arrived(lax.axis_index("zl"), (r0, r1, r2, r3), 0)
+def paired(lane, near_ref, across_ref):
+    tiles = []
+    for tile in range(TILES):
+        wanted = jnp.bitwise_xor(lane, tile)
+        value = near_ref[0]
+        for change, other in ((1, near_ref[1]), (2, across_ref[0]), (3, across_ref[1])):
+            value = jnp.where(wanted == change, other, value)
+        tiles.append(value)
+    return tiles
+
+
+def first_body(across_ref, near_ref, own_ref, high_ref, low_ref, own_out_ref):
+    tiles = paired(lax.axis_index("zl"), near_ref, across_ref)
     own_out_ref[0] = advanced(own_ref, [high_ref], [low_ref], tiles)
 
 
-def second_body(r0, r1, r2, r3, f0, f1, f2, f3, own_ref, h0, l0, h1, l1, copies_ref, own_out_ref):
+def second_body(r0, r1, r2, r3, across_ref, near_ref, own_ref, h0, l0, h1, l1, copies_ref,
+                own_out_ref):
     lane = lax.axis_index("zl")
-    tiles = arrived(lane, (f0, f1, f2, f3), 0) + arrived(lane, (r0, r1, r2, r3), 0)
+    tiles = paired(lane, near_ref, across_ref) + arrived(lane, (r0, r1, r2, r3), 0)
     own = advanced(own_ref.at[0], [h0, h1], [l0, l1], tiles)
     own_out_ref[...] = own
     for i in range(GROUP):
@@ -192,9 +205,9 @@
     )(*args)
 
 
-def forward(value, source, target):
+def forward(value, source, target, order):
     pieces = []
-    for change in ORDER:
+    for change in order:
         pieces.append(lax.ppermute(
             value, ROWS, [(source + i, target + (i ^ change)) for i in range(TILES)]
         ))
@@ -210,19 +223,21 @@
     group = shape(GROUP, members, rows)
 
     own = right[0]
-    own = own[None]
-    tiles = forward(own, 0, TILES)
-    far = forward(own, 0, 2 * TILES)
+    partner = lax.ppermute(own, ROWS, [(i, i ^ 1) for i in range(TILES)])
+    pair = jnp.stack([own, partner])
+    tiles = forward(pair, 0, TILES, PAIRS)
+    far = forward(pair, 0, 2 * TILES, PAIRS)
     half = jax.ShapeDtypeStruct((rows, WIDTH), bf16)
+    part, inverse = panel[0, :, :WIDTH], inverses[0]
     factor = local(
         prepare_body, 16, [half, half], 1 << 28, 2 << 20,
-        panel[0, :, :WIDTH], inverses[0],
+        part, inverse,
     )
     own, = local(
         first_body, 8, [shape(1, members, rows)], 1 << 33, 1 << 20,
-        *tiles, own[0], *factor,
-    )
-    tiles = forward(own, TILES, 2 * TILES)
+        *tiles, own, *factor,
+    )
+    tiles = forward(own, TILES, 2 * TILES, ORDER)
     half = jax.ShapeDtypeStruct((rows, (STEPS - 2) * WIDTH), bf16)
     factor += local(complete_body, 16, [half, half], 1 << 29, 12 << 20, panel, inverses)
     copies, own = local(second_body, 8, [group, tile], 1 << 27, 1 << 20, *tiles, *far, own, *factor)

time: 85.5 us -> 80.4 us (0.940)
  the two profiles are of different devices: /device:TPU:32 before, /device:TPU:56 now
where the time goes in v13:
time: 80.4 us; the launch traced here: 79.9 us
  blocking collectives  22.3 us (28%)
  starting transfers between devices  21.6 us (27%)
  waiting for transfers between devices  17.4 us (22%)
  local copies, waits for them, and re-layouts  8.73 us (11%)
  Pallas kernels  7 us (9%)
  other arithmetic  2 us (2%)
  between operations  0.92 us (1%)
    all_to_all x1, blocking collectives, shards(): tiles = lax.all_to_all(copies, OWNERS, 0, 0)  22.3 us
    ppermute x8, starting transfers between devices, forward(): lax.ppermute(value, ROWS, [(source + i, target + (i ^ change)) for i in r...  11.7 us
    all_to_all x1, waiting for transfers between devices, shards(): received = lax.all_to_all(copies, OWNERS, 0, 0)  7.75 us
    pallas_call x7, Pallas kernels, local(): pl.pallas_call(body, out_shape=outs, in_specs=[VMEM] * len(args), out_spe...  7 us
    ppermute x2, waiting for transfers between devices, shards(): sums = sums + lax.ppermute(sums, 'y', [(i, i ^ change) for i in range(4)])  6.16 us
    unnamed x12, local copies, waits for them, and re-layouts  5.73 us
    all_to_all x1, starting transfers between devices, shards(): received = lax.all_to_all(copies, OWNERS, 0, 0)  4.19 us
    ppermute x2, starting transfers between devices, crossings(): return [lax.ppermute(value, ROWS[:2], pairs)]  2.57 us
  transfers between devices with their start and end apart: 15, of which 5 were waited for; matrix products, arithmetic and copies ran while one was open for 5% of the time, Pallas kernels for 5%

profile of v13, /device:TPU:56, one launch (start us, length us, event | category | flops | bytes accessed | tf_op | source)
XLA Modules:
  0.0 79.9 jit_solution(8502493906802790510)
XLA Ops:
  0.6 0.7 fusion.2
  1.4 2.0 %collective-permute-start = (f32[32,128]{1,0:T(8,128)S(1)}, f32[32,128]{1,0:T(8,128)S(1)}, u32[]{:S(2)}, u32[]{:S(2)}) collective-permute-start(f32[32,128]{1,0:T(8,128)S(1)} %get-tuple-element.45.own_ref), channel_id=1, source_target_pairs={{0,8},{8,0},{16,24},{24,16},{1,9},{9,1},{17,25},{25,17},{2,10},{10... | collective-permute-start | bytes 49160 | tf_op jit(solution)/shard_map/ppermute | solution.py:226
  3.4 1.3 %slice_bitcast_fusion.inverse_ref = f32[512,512]{1,0:T(8,128)S(1)} fusion(f32[4,512,512]{2,1,0:T(8,128)} %refs_5_.1), kind=kLoop, calls=%fused_computation | loop fusion | bytes 2097152 | tf_op jit(solution)/shard_map/squeeze | solution.py:231
  4.7 2.3 %collective-permute-done = f32[32,128]{1,0:T(8,128)S(1)} collective-permute-done((f32[32,128]{1,0:T(8,128)S(1)}, f32[32,128]{1,0:T(8,128)S(1)}, u32[]{:S(2)}, u32[]{:S(2)}) %collective-permute-start) | collective-permute-done | bytes 16416 | tf_op jit(solution)/shard_map/ppermute | solution.py:226
  7.0 3.7 %collective-permute-start.1 = (f32[2,32,128]{2,1,0:T(8,128)S(1)}, f32[2,32,128]{2,1,0:T(8,128)S(1)}, u32[]{:S(2)}, u32[]{:S(2)}) collective-permute-start(f32[2,32,128]{2,1,0:T(8,128)S(1)} %pad_maximum_fusion), channel_id=1, source_target_pairs={{0,48},{8,56},{16,32},{24,40},{1,49},{9,57},{17,33},{25,41},{2,50}... | collective-permute-start | bytes 98312 | tf_op jit(solution)/shard_map/ppermute | solution.py:211
  10.6 2.2 %collective-permute-start.2 = (f32[2,32,128]{2,1,0:T(8,128)S(1)}, f32[2,32,128]{2,1,0:T(8,128)S(1)}, u32[]{:S(2)}, u32[]{:S(2)}) collective-permute-start(f32[2,32,128]{2,1,0:T(8,128)S(1)} %pad_maximum_fusion), channel_id=1, source_target_pairs={{0,32},{8,40},{16,48},{24,56},{1,33},{9,41},{17,49},{25,57},{2,34}... | collective-permute-start | bytes 98312 | tf_op jit(solution)/shard_map/ppermute | solution.py:211
  12.8 1.0 %slice_bitcast_fusion.1.part_ref = f32[128,512]{1,0:T(8,128)S(1)} fusion(f32[8,128,2048]{2,1,0:T(8,128)} %bitcast.22), kind=kLoop, calls=%fused_computation.1 | loop fusion | bytes 524288 | tf_op jit(solution)/shard_map/squeeze | solution.py:231
  13.8 0.0 slice-start
  13.8 0.4 shard_map.58
  14.2 1.6 %collective-permute-start.7 = (f32[2,32,128]{2,1,0:T(8,128)S(1)}, f32[2,32,128]{2,1,0:T(8,128)S(1)}, u32[]{:S(2)}, u32[]{:S(2)}) collective-permute-start(f32[2,32,128]{2,1,0:T(8,128)S(1)} %pad_maximum_fusion), channel_id=1, source_target_pairs={{0,80},{8,88},{16,64},{24,72},{1,81},{9,89},{17,65},{25,73},{2,82}... | collective-permute-start | bytes 98312 | tf_op jit(solution)/shard_map/ppermute | solution.py:211
  15.8 1.3 %collective-permute-start.8 = (f32[2,32,128]{2,1,0:T(8,128)S(1)}, f32[2,32,128]{2,1,0:T(8,128)S(1)}, u32[]{:S(2)}, u32[]{:S(2)}) collective-permute-start(f32[2,32,128]{2,1,0:T(8,128)S(1)} %pad_maximum_fusion), channel_id=1, source_target_pairs={{0,64},{8,72},{16,80},{24,88},{1,65},{9,73},{17,81},{25,89},{2,66}... | collective-permute-start | bytes 98312 | tf_op jit(solution)/shard_map/ppermute | solution.py:211
  17.1 0.0 collective-permute-done.1.across_ref
  17.1 0.0 collective-permute-done.2.near_ref
  17.1 0.0 slice-start.1
  17.1 0.0 copy-start.1
  17.1 0.2 shard_map.59.own_ref
  17.3 0.0 copy-start.3
  17.3 0.8 collective-permute-start.3
  18.1 0.8 collective-permute-start.4
  18.9 0.8 collective-permute-start.5
  19.7 0.0 collective-permute-done.7.across_ref
  19.7 0.7 collective-permute-start.6
  20.4 0.0 slice-done
  20.4 0.0 slice-done.1
  20.4 0.1 copy-done.1
  20.6 0.6 shard_map.60
  21.2 0.0 collective-permute-done.8.near_ref
  21.2 0.0 collective-permute-done.3.r0
  21.2 0.0 collective-permute-done.4.r1
  21.2 0.0 collective-permute-done.5.r2
  21.2 0.0 collective-permute-done.6.r3
  21.2 0.3 shard_map.61
  21.5 22.3 %all_to_all.10.tiles_ref = f32[16,32,128]{2,1,0:T(8,128)S(1)} all-to-all(f32[16,32,128]{2,1,0:T(8,128)S(1)} %get-tuple-element.26), channel_id=1, replica_groups=mesh['xh'=2,'xl'=2,'zh'=2,'zl'=4,'y'=4,'core'=2] {'xl','zh','zl'}, dimensions={0} | all-to-all | bytes 524288 | tf_op jit(solution)/shard_map/all_to_all | solution.py:244
  43.8 1.1 %shard_map.62 = (f32[16,32,128]{2,1,0:T(8,128)}, f32[32,128]{1,0:T(8,128)S(1)}, f32[12,32,128]{2,1,0:T(8,128)S(1)}) custom-call(f32[16,32,128]{2,1,0:T(8,128)S(1)} %all_to_all.10.tiles_ref, f32[32,128]{1,0:T(8,128)S(1)} %get-tuple-element.27.own_ref, bf16[128,512]{1,0:T(8,128)(2,1)S(1)} %get-tuple-element.22.high_ref.h0, ...), custom_call_target="tpu_custom_call" | custom-call | flops 134217728 | bytes 2097152 | tf_op jit(solution)/shard_map/pallas_call | solution.py:198
  44.9 4.2 %all-to-all-start.1 = ((f32[16,32,128]{2,1,0:T(8,128)}), f32[16,32,128]{2,1,0:T(8,128)S(1)}, u32[]{:S(2)}, u32[]{:S(2)}) async-start(f32[16,32,128]{2,1,0:T(8,128)} %get-tuple-element.29), calls=%async_computation.1 | async-start | bytes 524288 | tf_op jit(solution)/shard_map/all_to_all | solution.py:250
  49.1 1.3 %collective-permute-start.9 = (f32[12,32,128]{2,1,0:T(8,128)S(1)}, f32[12,32,128]{2,1,0:T(8,128)S(1)}, u32[]{:S(2)}, u32[]{:S(2)}) collective-permute-start(f32[12,32,128]{2,1,0:T(8,128)S(1)} %get-tuple-element.31.refs_0_), channel_id=1, source_target_pairs={{0,128},{64,192},{1,129},{65,193},{2,130},{66,194},{3,131},{67,195... | collective-permute-start | bytes 589832 | tf_op jit(solution)/shard_map/ppermute | solution.py:39
  50.4 7.8 %all-to-all-done.1 = f32[16,32,128]{2,1,0:T(8,128)S(1)} async-done(((f32[16,32,128]{2,1,0:T(8,128)}), f32[16,32,128]{2,1,0:T(8,128)S(1)}, u32[]{:S(2)}, u32[]{:S(2)}) %all-to-all-start.1) | async-done | bytes 262176 | tf_op jit(solution)/shard_map/all_to_all | solution.py:250
  58.2 1.3 %collective-permute-start.10 = (f32[4,32,128]{2,1,0:T(8,128)S(1)}, f32[4,32,128]{2,1,0:T(8,128)S(1)}, u32[]{:S(2)}, u32[]{:S(2)}) collective-permute-start(f32[4,32,128]{2,1,0:T(8,128)S(1)} %slice.26.refs_0_), channel_id=1, source_target_pairs={{0,192},{64,128},{1,193},{65,129},{2,194},{66,130},{3,195},{67,131... | collective-permute-start | bytes 196616 | tf_op jit(solution)/shard_map/ppermute | solution.py:39
  59.4 0.0 collective-permute-done.9.refs_1_
  59.5 0.0 copy-done.3
  59.5 0.0 copy-start
  59.5 3.4 %copy-done = f32[8,1,128,2048]{3,2,1,0:T(8,128)S(1)} copy-done((f32[8,1,128,2048]{3,2,1,0:T(8,128)S(1)}, f32[8,1,128,2048]{3,2,1,0:T(8,128)}, u32[]{:S(2)}) %copy-start) | copy-done | bytes 8388632
  62.9 0.0 copy-start.2
  62.9 2.2 %copy-done.2 = f32[4,512,512]{2,1,0:T(8,128)S(1)} copy-done((f32[4,512,512]{2,1,0:T(8,128)S(1)}, f32[4,512,512]{2,1,0:T(8,128)}, u32[]{:S(2)}) %copy-start.2) | copy-done | bytes 4194328
  65.0 3.2 %shard_map.63 = (f32[32,1536]{1,0:T(8,128)S(1)}, f32[8,32,128]{2,1,0:T(8,128)S(1)}) custom-call(f32[12,32,128]{2,1,0:T(8,128)S(1)} %get-tuple-element.31.refs_0_, f32[12,32,128]{2,1,0:T(8,128)S(1)} %collective-permute-done.9.refs_1_, f32[8,32,128]{2,1,0:T(8,128)S(1)} %bitcast.29, f32[8,128,2048]{2,1,0:T(8,128)S(1)} %bitcast.26, f32[4,512,512]{2,1,0:T(8,128)S(1)} %copy-done.2), custom_call_target="tpu_custom_call" | custom-call | flops 1073741824 | bytes 12582912 | tf_op jit(solution)/shard_map/pallas_call | solution.py:198
  68.2 0.0 collective-permute-done.10.refs_1_
  68.3 1.2 %shard_map.64 = (f32[32,512]{1,0:T(8,128)S(1)}, f32[4,32,128]{2,1,0:T(8,128)S(1)}, f32[4,32,128]{2,1,0:T(8,128)S(1)}, f32[2,8,128]{2,1,0:T(8,128)S(1)}) custom-call(f32[4,32,128]{2,1,0:T(8,128)S(1)} %slice.26.refs_0_, f32[4,32,128]{2,1,0:T(8,128)S(1)} %collective-permute-done.10.refs_1_, f32[32,128]{1,0:T(8,128)S(1)} %get-tuple-element.35.refs_2_, ...), custom_call_target="tpu_custom_call" | custom-call | flops 268435456 | bytes 4194304 | tf_op jit(solution)/shard_map/pallas_call | solution.py:198
  69.5 0.1 collective-permute-start.11
  69.6 1.2 %collective-permute-done.11 = f32[2,8,128]{2,1,0:T(8,128)S(1)} collective-permute-done((f32[2,8,128]{2,1,0:T(8,128)S(1)}, f32[2,8,128]{2,1,0:T(8,128)S(1)}, u32[]{:S(2)}, u32[]{:S(2)}) %collective-permute-start.11) | collective-permute-done | bytes 8224 | tf_op jit(solution)/shard_map/ppermute | solution.py:264
  70.8 0.7 collective-permute-start.12
  71.5 0.7 maximum_bitcast_fusion
  72.2 2.2 %collective-permute-done.12 = f32[2,8,128]{2,1,0:T(8,128)S(1)} collective-permute-done((f32[2,8,128]{2,1,0:T(8,128)S(1)}, f32[2,8,128]{2,1,0:T(8,128)S(1)}, u32[]{:S(2)}, u32[]{:S(2)}) %collective-permute-start.12) | collective-permute-done | bytes 8224 | tf_op jit(solution)/shard_map/ppermute | solution.py:266
  74.4 0.2 collective-permute-start.13
  74.6 0.7 maximum_bitcast_fusion.1
  75.3 4.0 %collective-permute-done.13 = f32[2,8,128]{2,1,0:T(8,128)S(1)} collective-permute-done((f32[2,8,128]{2,1,0:T(8,128)S(1)}, f32[2,8,128]{2,1,0:T(8,128)S(1)}, u32[]{:S(2)}, u32[]{:S(2)}) %collective-permute-start.13) | collective-permute-done | bytes 8224 | tf_op jit(solution)/shard_map/ppermute | solution.py:266
  79.3 0.6 fusion.1
  (6 shorter events, 0.0 us)
Async XLA Ops:
  1.4 5.6 %collective-permute-start = (f32[32,128]{1,0:T(8,128)S(1)}, f32[32,128]{1,0:T(8,128)S(1)}, u32[]{:S(2)}, u32[]{:S(2)}) collective-permute-start(f32[32,128]{1,0:T(8,128)S(1)} %get-tuple-element.45.own_ref), channel_id=1, source_target_pairs={{0,8},{8,0},{16,24},{24,16},{1,9},{9,1},{17,25},{25,17},{2,10},{10... | collective-permute-start | bytes 49160 | tf_op jit(solution)/shard_map/ppermute | solution.py:226
  7.0 10.1 %collective-permute-start.1 = (f32[2,32,128]{2,1,0:T(8,128)S(1)}, f32[2,32,128]{2,1,0:T(8,128)S(1)}, u32[]{:S(2)}, u32[]{:S(2)}) collective-permute-start(f32[2,32,128]{2,1,0:T(8,128)S(1)} %pad_maximum_fusion), channel_id=1, source_target_pairs={{0,48},{8,56},{16,32},{24,40},{1,49},{9,57},{17,33},{25,41},{2,50}... | collective-permute-start | bytes 98312 | tf_op jit(solution)/shard_map/ppermute | solution.py:211
  10.6 6.4 %collective-permute-start.2 = (f32[2,32,128]{2,1,0:T(8,128)S(1)}, f32[2,32,128]{2,1,0:T(8,128)S(1)}, u32[]{:S(2)}, u32[]{:S(2)}) collective-permute-start(f32[2,32,128]{2,1,0:T(8,128)S(1)} %pad_maximum_fusion), channel_id=1, source_target_pairs={{0,32},{8,40},{16,48},{24,56},{1,33},{9,41},{17,49},{25,57},{2,34}... | collective-permute-start | bytes 98312 | tf_op jit(solution)/shard_map/ppermute | solution.py:211
  13.8 6.6 %slice-start = ((s8[8388608]{0:T(1024)(128)(4,1)}), s8[4194304]{0:T(1024)(128)(4,1)S(1)}, s32[]{:S(2)}) async-start(s8[8388608]{0:T(1024)(128)(4,1)} %bitcast.23), calls=%async_computation.2 | async-start | bytes 8388608
  14.2 5.5 %collective-permute-start.7 = (f32[2,32,128]{2,1,0:T(8,128)S(1)}, f32[2,32,128]{2,1,0:T(8,128)S(1)}, u32[]{:S(2)}, u32[]{:S(2)}) collective-permute-start(f32[2,32,128]{2,1,0:T(8,128)S(1)} %pad_maximum_fusion), channel_id=1, source_target_pairs={{0,80},{8,88},{16,64},{24,72},{1,81},{9,89},{17,65},{25,73},{2,82}... | collective-permute-start | bytes 98312 | tf_op jit(solution)/shard_map/ppermute | solution.py:211
  15.8 5.4 %collective-permute-start.8 = (f32[2,32,128]{2,1,0:T(8,128)S(1)}, f32[2,32,128]{2,1,0:T(8,128)S(1)}, u32[]{:S(2)}, u32[]{:S(2)}) collective-permute-start(f32[2,32,128]{2,1,0:T(8,128)S(1)} %pad_maximum_fusion), channel_id=1, source_target_pairs={{0,64},{8,72},{16,80},{24,88},{1,65},{9,73},{17,81},{25,89},{2,66}... | collective-permute-start | bytes 98312 | tf_op jit(solution)/shard_map/ppermute | solution.py:211
  17.1 3.3 %slice-start.1 = ((s8[8388608]{0:T(1024)(128)(4,1)}), s8[4194304]{0:T(1024)(128)(4,1)S(1)}, s32[]{:S(2)}) async-start(s8[8388608]{0:T(1024)(128)(4,1)} %bitcast.23), calls=%async_computation.3 | async-start | bytes 8388608
  17.1 3.5 %copy-start.1 = (f32[4,512,512]{2,1,0:T(8,128)S(1)}, f32[4,512,512]{2,1,0:T(8,128)}, u32[]{:S(2)}) copy-start(f32[4,512,512]{2,1,0:T(8,128)} %refs_5_.1) | copy-start | bytes 12582916
  17.3 42.1 %copy-start.3 = (f32[8,1,128,32]{2,3,1,0:T(8,128)S(1)}, f32[8,1,128,32]{2,3,1,0:T(8,128)}, u32[]{:S(2)}) copy-start(f32[8,1,128,32]{2,3,1,0:T(8,128)} %param.4) | copy-start | bytes 393220
  17.3 3.9 %collective-permute-start.3 = (f32[1,32,128]{2,1,0:T(8,128)S(1)}, f32[1,32,128]{2,1,0:T(8,128)S(1)}, u32[]{:S(2)}, u32[]{:S(2)}) collective-permute-start(f32[1,32,128]{2,1,0:T(8,128)S(1)} %shard_map.59.own_ref), channel_id=1, source_target_pairs={{32,80},{40,88},{48,64},{56,72},{33,81},{41,89},{49,65},{57,73},{3... | collective-permute-start | bytes 49160 | tf_op jit(solution)/shard_map/ppermute | solution.py:211
  18.1 3.1 %collective-permute-start.4 = (f32[1,32,128]{2,1,0:T(8,128)S(1)}, f32[1,32,128]{2,1,0:T(8,128)S(1)}, u32[]{:S(2)}, u32[]{:S(2)}) collective-permute-start(f32[1,32,128]{2,1,0:T(8,128)S(1)} %shard_map.59.own_ref), channel_id=1, source_target_pairs={{32,88},{40,80},{48,72},{56,64},{33,89},{41,81},{49,73},{57,65},{3... | collective-permute-start | bytes 49160 | tf_op jit(solution)/shard_map/ppermute | solution.py:211
  18.9 2.3 %collective-permute-start.5 = (f32[1,32,128]{2,1,0:T(8,128)S(1)}, f32[1,32,128]{2,1,0:T(8,128)S(1)}, u32[]{:S(2)}, u32[]{:S(2)}) collective-permute-start(f32[1,32,128]{2,1,0:T(8,128)S(1)} %shard_map.59.own_ref), channel_id=1, source_target_pairs={{32,72},{40,64},{48,88},{56,80},{33,73},{41,65},{49,89},{57,81},{3... | collective-permute-start | bytes 49160 | tf_op jit(solution)/shard_map/ppermute | solution.py:211
  19.7 1.5 %collective-permute-start.6 = (f32[1,32,128]{2,1,0:T(8,128)S(1)}, f32[1,32,128]{2,1,0:T(8,128)S(1)}, u32[]{:S(2)}, u32[]{:S(2)}) collective-permute-start(f32[1,32,128]{2,1,0:T(8,128)S(1)} %shard_map.59.own_ref), channel_id=1, source_target_pairs={{32,64},{40,72},{48,80},{56,88},{33,65},{41,73},{49,81},{57,89},{3... | collective-permute-start | bytes 49160 | tf_op jit(solution)/shard_map/ppermute | solution.py:211
  44.9 13.2 %all-to-all-start.1 = ((f32[16,32,128]{2,1,0:T(8,128)}), f32[16,32,128]{2,1,0:T(8,128)S(1)}, u32[]{:S(2)}, u32[]{:S(2)}) async-start(f32[16,32,128]{2,1,0:T(8,128)} %get-tuple-element.29), calls=%async_computation.1 | async-start | bytes 524288 | tf_op jit(solution)/shard_map/all_to_all | solution.py:250
  49.1 10.3 %collective-permute-start.9 = (f32[12,32,128]{2,1,0:T(8,128)S(1)}, f32[12,32,128]{2,1,0:T(8,128)S(1)}, u32[]{:S(2)}, u32[]{:S(2)}) collective-permute-start(f32[12,32,128]{2,1,0:T(8,128)S(1)} %get-tuple-element.31.refs_0_), channel_id=1, source_target_pairs={{0,128},{64,192},{1,129},{65,193},{2,130},{66,194},{3,131},{67,195... | collective-permute-start | bytes 589832 | tf_op jit(solution)/shard_map/ppermute | solution.py:39
  58.2 10.1 %collective-permute-start.10 = (f32[4,32,128]{2,1,0:T(8,128)S(1)}, f32[4,32,128]{2,1,0:T(8,128)S(1)}, u32[]{:S(2)}, u32[]{:S(2)}) collective-permute-start(f32[4,32,128]{2,1,0:T(8,128)S(1)} %slice.26.refs_0_), channel_id=1, source_target_pairs={{0,192},{64,128},{1,193},{65,129},{2,194},{66,130},{3,195},{67,131... | collective-permute-start | bytes 196616 | tf_op jit(solution)/shard_map/ppermute | solution.py:39
  59.5 3.4 %copy-start = (f32[8,1,128,2048]{3,2,1,0:T(8,128)S(1)}, f32[8,1,128,2048]{3,2,1,0:T(8,128)}, u32[]{:S(2)}) copy-start(f32[8,1,128,2048]{3,2,1,0:T(8,128)} %param.3) | copy-start | bytes 25165828
  62.9 2.2 %copy-start.2 = (f32[4,512,512]{2,1,0:T(8,128)S(1)}, f32[4,512,512]{2,1,0:T(8,128)}, u32[]{:S(2)}) copy-start(f32[4,512,512]{2,1,0:T(8,128)} %refs_5_.1) | copy-start | bytes 12582916
  69.5 1.3 %collective-permute-start.11 = (f32[2,8,128]{2,1,0:T(8,128)S(1)}, f32[2,8,128]{2,1,0:T(8,128)S(1)}, u32[]{:S(2)}, u32[]{:S(2)}) collective-permute-start(f32[2,8,128]{2,1,0:T(8,128)S(1)} %get-tuple-element.40), channel_id=1, source_target_pairs={{0,1},{1,0},{2,3},{3,2},{4,5},{5,4},{6,7},{7,6},{8,9},{9,8},{10,11... | collective-permute-start | bytes 24584 | tf_op jit(solution)/shard_map/ppermute | solution.py:264
  70.8 3.7 %collective-permute-start.12 = (f32[2,8,128]{2,1,0:T(8,128)S(1)}, f32[2,8,128]{2,1,0:T(8,128)S(1)}, u32[]{:S(2)}, u32[]{:S(2)}) collective-permute-start(f32[2,8,128]{2,1,0:T(8,128)S(1)} %add.9), channel_id=1, source_target_pairs={{0,2},{2,0},{4,6},{6,4},{1,3},{3,1},{5,7},{7,5},{8,10},{10,8},{12,... | collective-permute-start | bytes 24584 | tf_op jit(solution)/shard_map/ppermute | solution.py:266
  74.4 4.9 %collective-permute-start.13 = (f32[2,8,128]{2,1,0:T(8,128)S(1)}, f32[2,8,128]{2,1,0:T(8,128)S(1)}, u32[]{:S(2)}, u32[]{:S(2)}) collective-permute-start(f32[2,8,128]{2,1,0:T(8,128)S(1)} %add.10), channel_id=1, source_target_pairs={{0,6},{2,4},{4,2},{6,0},{1,7},{3,5},{5,3},{7,1},{8,14},{10,12},{12... | collective-permute-start | bytes 24584 | tf_op jit(solution)/shard_map/ppermute | solution.py:266

commit v14 on v13

--- a/solution.py
+++ b/solution.py
@@ -82,11 +82,15 @@
     high_ref[...], low_ref[...] = product_halves(part_ref[...], inverse_ref[...])
 
 
-def complete_body(panel_ref, inverses_ref, high_ref, low_ref):
+def complete_body(panel_ref, inverses_ref, high_ref, low_ref, tail_high_ref, tail_low_ref):
     for step in range(1, STEPS - 1):
         part = panel_ref[0, :, step * WIDTH:(step + 1) * WIDTH]
         columns = slice((step - 1) * WIDTH, step * WIDTH)
         high_ref[:, columns], low_ref[:, columns] = product_halves(part, inverses_ref[step])
+    last = STEPS - 1
+    for block in range(panel_ref.shape[0]):
+        part = panel_ref[block, :, last * WIDTH:]
+        tail_high_ref[block], tail_low_ref[block] = product_halves(part, inverses_ref[last])
 
 
 def arrived(lane, refs, at):
@@ -161,15 +165,18 @@
         left_ref[block] = right_ref[block] - product
 
 
+def last_body(*refs):
+    *sources, inverses_ref, solved_ref = refs
+    solved_ref[...] = times_split(chosen(line_of(), sources, 0), inverses_ref[STEPS - 1])
+
+
 def finish_body(*refs):
     sources = refs[:SOURCES]
-    own_ref, partly_ref, panel_ref, inverses_ref = refs[SOURCES:SOURCES + 4]
-    solved_ref, low_ref, high_ref, sums_ref = refs[-4:]
-    step = STEPS - 1
-    solved = times_split(chosen(line_of(), sources, 0), inverses_ref[step])
-    solved_ref[...] = solved
+    own_ref, partly_ref, tail_high_ref, tail_low_ref = refs[SOURCES:SOURCES + 4]
+    low_ref, high_ref, sums_ref = refs[-3:]
+    residual = chosen(line_of(), sources, 0)
     for block in range(partly_ref.shape[0]):
-        product = times_split(solved, panel_ref[block, :, step * WIDTH:])
+        product = times_halves(residual, tail_high_ref[block], tail_low_ref[block])
         left = partly_ref[block] - product
         if block == 0:
             left = jnp.where(step_of() < STEPS, own_ref[...], left)
@@ -239,7 +246,12 @@
     )
     tiles = forward(own, TILES, 2 * TILES, ORDER)
     half = jax.ShapeDtypeStruct((rows, (STEPS - 2) * WIDTH), bf16)
-    factor += local(complete_body, 16, [half, half], 1 << 29, 12 << 20, panel, inverses)
+    tail = jax.ShapeDtypeStruct((blocks, rows, WIDTH), bf16)
+    high, low, *tails = local(
+        complete_body, 24, [half, half, tail, tail], 1 << 31, 14 << 20,
+        panel, inverses,
+    )
+    factor = [*factor, high, low]
     copies, own = local(second_body, 8, [group, tile], 1 << 27, 1 << 20, *tiles, *far, own, *factor)
     tiles = lax.all_to_all(copies, OWNERS, 0, 0)
     copies, own, packed = local(
@@ -256,12 +268,17 @@
         [shape(members, (STEPS - 1) * WIDTH), shape(blocks, members, rows)],
         1 << 30, 12 << 20, *early, right, panel, inverses,
     )
-    last, low, high, sums = local(
+    low, high, sums = local(
         finish_body, 16,
-        [shape(members, WIDTH)] + [shape(blocks // 2, members, rows)] * 2 + [shape(2, blocks, rows)],
-        1 << 28, 4 << 20, ends, *late, own, partly, panel, inverses,
-    )
-    sums = sums + lax.ppermute(sums, "core", [(0, 1), (1, 0)])
+        [shape(blocks // 2, members, rows)] * 2 + [shape(2, blocks, rows)],
+        1 << 28, 4 << 20, ends, *late, own, partly, *tails,
+    )
+    other = lax.ppermute(sums, "core", [(0, 1), (1, 0)])
+    last, = local(
+        last_body, 8, [shape(members, WIDTH)], 1 << 28, 1 << 20,
+        ends, *late, inverses,
+    )
+    sums = sums + other
     for change in (1, 3):
         sums = sums + lax.ppermute(sums, "y", [(i, i ^ change) for i in range(4)])
     solved = jnp.concatenate([before, last], axis=1)

time: 80.4 us -> 79 us (0.983)
  blocking collectives: 22.3 us -> 18.9 us
  Pallas kernels: 7 us -> 8.73 us
    all_to_all x1, blocking collectives: 22.3 us -> 18.9 us  [shards(): tiles = lax.all_to_all(copies, OWNERS, 0, 0)]
    pallas_call x7 -> x8, Pallas kernels: 7 us -> 8.73 us  [local(): pl.pallas_call(body, out_shape=outs, in_specs=[VMEM] * len(args), out_spe...]
  transfers between devices with their start and end apart: 15 -> 15, of which waited for: 5 -> 5; matrix products, arithmetic and copies ran while one was open for 5% -> 5% of each run, Pallas kernels for 5% -> 8%
where the time goes in v14:
time: 79 us; the launch traced here: 78.5 us
  starting transfers between devices  21.7 us (27%)
  blocking collectives  18.9 us (24%)
  waiting for transfers between devices  17.5 us (22%)
  local copies, waits for them, and re-layouts  8.73 us (11%)
  Pallas kernels  8.73 us (11%)
  other arithmetic  2 us (3%)
  between operations  0.93 us (1%)
    all_to_all x1, blocking collectives, shards(): tiles = lax.all_to_all(copies, OWNERS, 0, 0)  18.9 us
    ppermute x8, starting transfers between devices, forward(): lax.ppermute(value, ROWS, [(source + i, target + (i ^ change)) for i in r...  11.7 us
    pallas_call x8, Pallas kernels, local(): pl.pallas_call(body, out_shape=outs, in_specs=[VMEM] * len(args), out_spe...  8.73 us
    all_to_all x1, waiting for transfers between devices, shards(): received = lax.all_to_all(copies, OWNERS, 0, 0)  8.29 us
    ppermute x2, waiting for transfers between devices, shards(): sums = sums + lax.ppermute(sums, 'y', [(i, i ^ change) for i in range(4)])  6.16 us
    unnamed x12, local copies, waits for them, and re-layouts  5.73 us
    all_to_all x1, starting transfers between devices, shards(): received = lax.all_to_all(copies, OWNERS, 0, 0)  4.31 us
    ppermute x2, starting transfers between devices, crossings(): return [lax.ppermute(value, ROWS[:2], pairs)]  2.57 us
  transfers between devices with their start and end apart: 15, of which 5 were waited for; matrix products, arithmetic and copies ran while one was open for 5% of the time, Pallas kernels for 8%

profile of v14, /device:TPU:56, one launch (start us, length us, event | category | flops | bytes accessed | tf_op | source)
XLA Modules:
  0.0 78.5 jit_solution(7490365971119009224)
XLA Ops:
  0.6 0.7 fusion.2
  1.4 2.0 %collective-permute-start = (f32[32,128]{1,0:T(8,128)S(1)}, f32[32,128]{1,0:T(8,128)S(1)}, u32[]{:S(2)}, u32[]{:S(2)}) collective-permute-start(f32[32,128]{1,0:T(8,128)S(1)} %get-tuple-element.47.own_ref), channel_id=1, source_target_pairs={{0,8},{8,0},{16,24},{24,16},{1,9},{9,1},{17,25},{25,17},{2,10},{10... | collective-permute-start | bytes 49160 | tf_op jit(solution)/shard_map/ppermute | solution.py:233
  3.4 1.3 %slice_bitcast_fusion.inverse_ref = f32[512,512]{1,0:T(8,128)S(1)} fusion(f32[4,512,512]{2,1,0:T(8,128)} %refs_2_.1), kind=kLoop, calls=%fused_computation | loop fusion | bytes 2097152 | tf_op jit(solution)/shard_map/squeeze | solution.py:238
  4.7 2.3 %collective-permute-done = f32[32,128]{1,0:T(8,128)S(1)} collective-permute-done((f32[32,128]{1,0:T(8,128)S(1)}, f32[32,128]{1,0:T(8,128)S(1)}, u32[]{:S(2)}, u32[]{:S(2)}) %collective-permute-start) | collective-permute-done | bytes 16416 | tf_op jit(solution)/shard_map/ppermute | solution.py:233
  7.0 4.6 %collective-permute-start.2 = (f32[2,32,128]{2,1,0:T(8,128)S(1)}, f32[2,32,128]{2,1,0:T(8,128)S(1)}, u32[]{:S(2)}, u32[]{:S(2)}) collective-permute-start(f32[2,32,128]{2,1,0:T(8,128)S(1)} %pad_maximum_fusion), channel_id=1, source_target_pairs={{0,32},{8,40},{16,48},{24,56},{1,33},{9,41},{17,49},{25,57},{2,34}... | collective-permute-start | bytes 98312 | tf_op jit(solution)/shard_map/ppermute | solution.py:218
  11.5 1.3 %collective-permute-start.1 = (f32[2,32,128]{2,1,0:T(8,128)S(1)}, f32[2,32,128]{2,1,0:T(8,128)S(1)}, u32[]{:S(2)}, u32[]{:S(2)}) collective-permute-start(f32[2,32,128]{2,1,0:T(8,128)S(1)} %pad_maximum_fusion), channel_id=1, source_target_pairs={{0,48},{8,56},{16,32},{24,40},{1,49},{9,57},{17,33},{25,41},{2,50}... | collective-permute-start | bytes 98312 | tf_op jit(solution)/shard_map/ppermute | solution.py:218
  12.8 1.0 %slice_bitcast_fusion.1.part_ref = f32[128,512]{1,0:T(8,128)S(1)} fusion(f32[8,128,2048]{2,1,0:T(8,128)} %bitcast.22), kind=kLoop, calls=%fused_computation.1 | loop fusion | bytes 524288 | tf_op jit(solution)/shard_map/squeeze | solution.py:238
  13.8 0.0 slice-start
  13.8 0.4 shard_map.58
  14.2 1.6 %collective-permute-start.8 = (f32[2,32,128]{2,1,0:T(8,128)S(1)}, f32[2,32,128]{2,1,0:T(8,128)S(1)}, u32[]{:S(2)}, u32[]{:S(2)}) collective-permute-start(f32[2,32,128]{2,1,0:T(8,128)S(1)} %pad_maximum_fusion), channel_id=1, source_target_pairs={{0,64},{8,72},{16,80},{24,88},{1,65},{9,73},{17,81},{25,89},{2,66}... | collective-permute-start | bytes 98312 | tf_op jit(solution)/shard_map/ppermute | solution.py:218
  15.8 1.3 %collective-permute-start.7 = (f32[2,32,128]{2,1,0:T(8,128)S(1)}, f32[2,32,128]{2,1,0:T(8,128)S(1)}, u32[]{:S(2)}, u32[]{:S(2)}) collective-permute-start(f32[2,32,128]{2,1,0:T(8,128)S(1)} %pad_maximum_fusion), channel_id=1, source_target_pairs={{0,80},{8,88},{16,64},{24,72},{1,81},{9,89},{17,65},{25,73},{2,82}... | collective-permute-start | bytes 98312 | tf_op jit(solution)/shard_map/ppermute | solution.py:218
  17.1 0.0 collective-permute-done.2.near_ref
  17.1 0.0 collective-permute-done.1.across_ref
  17.1 0.0 copy-start
  17.1 0.0 slice-start.1
  17.1 0.2 shard_map.59.own_ref
  17.3 0.0 copy-start.3
  17.3 0.8 %collective-permute-start.6 = (f32[1,32,128]{2,1,0:T(8,128)S(1)}, f32[1,32,128]{2,1,0:T(8,128)S(1)}, u32[]{:S(2)}, u32[]{:S(2)}) collective-permute-start(f32[1,32,128]{2,1,0:T(8,128)S(1)} %shard_map.59.own_ref), channel_id=1, source_target_pairs={{32,64},{40,72},{48,80},{56,88},{33,65},{41,73},{49,81},{57,89},{3... | collective-permute-start | bytes 49160 | tf_op jit(solution)/shard_map/ppermute | solution.py:218
  18.1 0.8 %collective-permute-start.5 = (f32[1,32,128]{2,1,0:T(8,128)S(1)}, f32[1,32,128]{2,1,0:T(8,128)S(1)}, u32[]{:S(2)}, u32[]{:S(2)}) collective-permute-start(f32[1,32,128]{2,1,0:T(8,128)S(1)} %shard_map.59.own_ref), channel_id=1, source_target_pairs={{32,72},{40,64},{48,88},{56,80},{33,73},{41,65},{49,89},{57,81},{3... | collective-permute-start | bytes 49160 | tf_op jit(solution)/shard_map/ppermute | solution.py:218
  18.9 0.8 %collective-permute-start.4 = (f32[1,32,128]{2,1,0:T(8,128)S(1)}, f32[1,32,128]{2,1,0:T(8,128)S(1)}, u32[]{:S(2)}, u32[]{:S(2)}) collective-permute-start(f32[1,32,128]{2,1,0:T(8,128)S(1)} %shard_map.59.own_ref), channel_id=1, source_target_pairs={{32,88},{40,80},{48,72},{56,64},{33,89},{41,81},{49,73},{57,65},{3... | collective-permute-start | bytes 49160 | tf_op jit(solution)/shard_map/ppermute | solution.py:218
  19.7 0.0 collective-permute-done.8.near_ref
  19.7 0.7 collective-permute-start.3
  20.4 0.0 slice-done
  20.4 0.0 copy-done
  20.4 0.1 slice-done.1
  20.6 2.3 %shard_map.60 = (bf16[128,1024]{1,0:T(8,128)(2,1)S(1)}, bf16[128,1024]{1,0:T(8,128)(2,1)S(1)}, bf16[8,128,512]{2,1,0:T(8,128)(2,1)S(1)}, bf16[8,128,512]{2,1,0:T(8,128)(2,1)S(1)}) custom-call(f32[8,128,2048]{2,1,0:T(8,128)S(1)} %bitcast.25, f32[4,512,512]{2,1,0:T(8,128)S(1)} %copy-done), custom_call_target="tpu_custom_call" | custom-call | flops 2147483648 | bytes 14680064 | tf_op jit(solution)/shard_map/pallas_call | solution.py:205
  22.9 0.0 collective-permute-done.7.across_ref
  22.9 0.0 collective-permute-done.6.r3
  22.9 0.0 collective-permute-done.5.r2
  22.9 0.0 collective-permute-done.4.r1
  23.0 0.0 collective-permute-done.3.r0
  23.0 0.3 shard_map.61
  23.3 18.9 %all_to_all.10.tiles_ref = f32[16,32,128]{2,1,0:T(8,128)S(1)} all-to-all(f32[16,32,128]{2,1,0:T(8,128)S(1)} %get-tuple-element.27), channel_id=1, replica_groups=mesh['xh'=2,'xl'=2,'zh'=2,'zl'=4,'y'=4,'core'=2] {'xl','zh','zl'}, dimensions={0} | all-to-all | bytes 524288 | tf_op jit(solution)/shard_map/all_to_all | solution.py:256
  42.1 1.1 %shard_map.62 = (f32[16,32,128]{2,1,0:T(8,128)}, f32[32,128]{1,0:T(8,128)S(1)}, f32[12,32,128]{2,1,0:T(8,128)S(1)}) custom-call(f32[16,32,128]{2,1,0:T(8,128)S(1)} %all_to_all.10.tiles_ref, f32[32,128]{1,0:T(8,128)S(1)} %get-tuple-element.28.own_ref, bf16[128,512]{1,0:T(8,128)(2,1)S(1)} %get-tuple-element.23.high_ref.h0, ...), custom_call_target="tpu_custom_call" | custom-call | flops 134217728 | bytes 2097152 | tf_op jit(solution)/shard_map/pallas_call | solution.py:205
  43.2 4.3 %all-to-all-start.1 = ((f32[16,32,128]{2,1,0:T(8,128)}), f32[16,32,128]{2,1,0:T(8,128)S(1)}, u32[]{:S(2)}, u32[]{:S(2)}) async-start(f32[16,32,128]{2,1,0:T(8,128)} %get-tuple-element.30), calls=%async_computation.1 | async-start | bytes 524288 | tf_op jit(solution)/shard_map/all_to_all | solution.py:262
  47.6 1.3 %collective-permute-start.9 = (f32[12,32,128]{2,1,0:T(8,128)S(1)}, f32[12,32,128]{2,1,0:T(8,128)S(1)}, u32[]{:S(2)}, u32[]{:S(2)}) collective-permute-start(f32[12,32,128]{2,1,0:T(8,128)S(1)} %get-tuple-element.32.refs_0_), channel_id=1, source_target_pairs={{0,128},{64,192},{1,129},{65,193},{2,130},{66,194},{3,131},{67,195... | collective-permute-start | bytes 589832 | tf_op jit(solution)/shard_map/ppermute | solution.py:39
  48.9 8.3 %all-to-all-done.1 = f32[16,32,128]{2,1,0:T(8,128)S(1)} async-done(((f32[16,32,128]{2,1,0:T(8,128)}), f32[16,32,128]{2,1,0:T(8,128)S(1)}, u32[]{:S(2)}, u32[]{:S(2)}) %all-to-all-start.1) | async-done | bytes 262176 | tf_op jit(solution)/shard_map/all_to_all | solution.py:262
  57.1 1.3 %collective-permute-start.10 = (f32[4,32,128]{2,1,0:T(8,128)S(1)}, f32[4,32,128]{2,1,0:T(8,128)S(1)}, u32[]{:S(2)}, u32[]{:S(2)}) collective-permute-start(f32[4,32,128]{2,1,0:T(8,128)S(1)} %slice.26.refs_0_), channel_id=1, source_target_pairs={{0,192},{64,128},{1,193},{65,129},{2,194},{66,130},{3,195},{67,131... | collective-permute-start | bytes 196616 | tf_op jit(solution)/shard_map/ppermute | solution.py:39
  58.4 0.0 collective-permute-done.9.refs_1_
  58.4 0.0 copy-done.3
  58.5 0.0 copy-start.1
  58.5 2.2 %copy-done.1 = f32[4,512,512]{2,1,0:T(8,128)S(1)} copy-done((f32[4,512,512]{2,1,0:T(8,128)S(1)}, f32[4,512,512]{2,1,0:T(8,128)}, u32[]{:S(2)}) %copy-start.1) | copy-done | bytes 4194328
  60.6 0.0 copy-start.2
  60.6 3.4 %copy-done.2 = f32[8,1,128,2048]{3,2,1,0:T(8,128)S(1)} copy-done((f32[8,1,128,2048]{3,2,1,0:T(8,128)S(1)}, f32[8,1,128,2048]{3,2,1,0:T(8,128)}, u32[]{:S(2)}) %copy-start.2) | copy-done | bytes 8388632
  64.0 3.2 %shard_map.63 = (f32[32,1536]{1,0:T(8,128)S(1)}, f32[8,32,128]{2,1,0:T(8,128)S(1)}) custom-call(f32[12,32,128]{2,1,0:T(8,128)S(1)} %get-tuple-element.32.refs_0_, f32[12,32,128]{2,1,0:T(8,128)S(1)} %collective-permute-done.9.refs_1_, f32[8,32,128]{2,1,0:T(8,128)S(1)} %bitcast.28, f32[8,128,2048]{2,1,0:T(8,128)S(1)} %bitcast.26, f32[4,512,512]{2,1,0:T(8,128)S(1)} %copy-done.1), custom_call_target="tpu_custom_call" | custom-call | flops 1073741824 | bytes 12582912 | tf_op jit(solution)/shard_map/pallas_call | solution.py:205
  67.2 0.0 collective-permute-done.10.refs_1_
  67.3 0.8 %shard_map.65 = (f32[4,32,128]{2,1,0:T(8,128)S(1)}, f32[4,32,128]{2,1,0:T(8,128)S(1)}, f32[2,8,128]{2,1,0:T(8,128)S(1)}) custom-call(f32[4,32,128]{2,1,0:T(8,128)S(1)} %slice.26.refs_0_, f32[4,32,128]{2,1,0:T(8,128)S(1)} %collective-permute-done.10.refs_1_, f32[32,128]{1,0:T(8,128)S(1)} %get-tuple-element.36.refs_2_, ...), custom_call_target="tpu_custom_call" | custom-call | flops 268435456 | bytes 4194304 | tf_op jit(solution)/shard_map/pallas_call | solution.py:205
  68.1 0.1 collective-permute-start.11
  68.2 0.4 shard_map.64
  68.6 0.7 collective-permute-done.11
  69.3 0.7 collective-permute-start.12
  70.1 0.7 maximum_bitcast_fusion
  70.8 2.2 %collective-permute-done.12 = f32[2,8,128]{2,1,0:T(8,128)S(1)} collective-permute-done((f32[2,8,128]{2,1,0:T(8,128)S(1)}, f32[2,8,128]{2,1,0:T(8,128)S(1)}, u32[]{:S(2)}, u32[]{:S(2)}) %collective-permute-start.12) | collective-permute-done | bytes 8224 | tf_op jit(solution)/shard_map/ppermute | solution.py:283
  73.0 0.2 collective-permute-start.13
  73.2 0.7 maximum_bitcast_fusion.1
  73.9 4.0 %collective-permute-done.13 = f32[2,8,128]{2,1,0:T(8,128)S(1)} collective-permute-done((f32[2,8,128]{2,1,0:T(8,128)S(1)}, f32[2,8,128]{2,1,0:T(8,128)S(1)}, u32[]{:S(2)}, u32[]{:S(2)}) %collective-permute-start.13) | collective-permute-done | bytes 8224 | tf_op jit(solution)/shard_map/ppermute | solution.py:283
  77.9 0.6 fusion.1
  (6 shorter events, 0.0 us)
Async XLA Ops:
  1.4 5.6 %collective-permute-start = (f32[32,128]{1,0:T(8,128)S(1)}, f32[32,128]{1,0:T(8,128)S(1)}, u32[]{:S(2)}, u32[]{:S(2)}) collective-permute-start(f32[32,128]{1,0:T(8,128)S(1)} %get-tuple-element.47.own_ref), channel_id=1, source_target_pairs={{0,8},{8,0},{16,24},{24,16},{1,9},{9,1},{17,25},{25,17},{2,10},{10... | collective-permute-start | bytes 49160 | tf_op jit(solution)/shard_map/ppermute | solution.py:233
  7.0 10.1 %collective-permute-start.2 = (f32[2,32,128]{2,1,0:T(8,128)S(1)}, f32[2,32,128]{2,1,0:T(8,128)S(1)}, u32[]{:S(2)}, u32[]{:S(2)}) collective-permute-start(f32[2,32,128]{2,1,0:T(8,128)S(1)} %pad_maximum_fusion), channel_id=1, source_target_pairs={{0,32},{8,40},{16,48},{24,56},{1,33},{9,41},{17,49},{25,57},{2,34}... | collective-permute-start | bytes 98312 | tf_op jit(solution)/shard_map/ppermute | solution.py:218
  11.5 5.6 %collective-permute-start.1 = (f32[2,32,128]{2,1,0:T(8,128)S(1)}, f32[2,32,128]{2,1,0:T(8,128)S(1)}, u32[]{:S(2)}, u32[]{:S(2)}) collective-permute-start(f32[2,32,128]{2,1,0:T(8,128)S(1)} %pad_maximum_fusion), channel_id=1, source_target_pairs={{0,48},{8,56},{16,32},{24,40},{1,49},{9,57},{17,33},{25,41},{2,50}... | collective-permute-start | bytes 98312 | tf_op jit(solution)/shard_map/ppermute | solution.py:218
  13.8 6.6 %slice-start = ((s8[8388608]{0:T(1024)(128)(4,1)}), s8[4194304]{0:T(1024)(128)(4,1)S(1)}, s32[]{:S(2)}) async-start(s8[8388608]{0:T(1024)(128)(4,1)} %bitcast.23), calls=%async_computation.2 | async-start | bytes 8388608
  14.2 5.5 %collective-permute-start.8 = (f32[2,32,128]{2,1,0:T(8,128)S(1)}, f32[2,32,128]{2,1,0:T(8,128)S(1)}, u32[]{:S(2)}, u32[]{:S(2)}) collective-permute-start(f32[2,32,128]{2,1,0:T(8,128)S(1)} %pad_maximum_fusion), channel_id=1, source_target_pairs={{0,64},{8,72},{16,80},{24,88},{1,65},{9,73},{17,81},{25,89},{2,66}... | collective-permute-start | bytes 98312 | tf_op jit(solution)/shard_map/ppermute | solution.py:218
  15.8 7.1 %collective-permute-start.7 = (f32[2,32,128]{2,1,0:T(8,128)S(1)}, f32[2,32,128]{2,1,0:T(8,128)S(1)}, u32[]{:S(2)}, u32[]{:S(2)}) collective-permute-start(f32[2,32,128]{2,1,0:T(8,128)S(1)} %pad_maximum_fusion), channel_id=1, source_target_pairs={{0,80},{8,88},{16,64},{24,72},{1,81},{9,89},{17,65},{25,73},{2,82}... | collective-permute-start | bytes 98312 | tf_op jit(solution)/shard_map/ppermute | solution.py:218
  17.1 3.3 %copy-start = (f32[4,512,512]{2,1,0:T(8,128)S(1)}, f32[4,512,512]{2,1,0:T(8,128)}, u32[]{:S(2)}) copy-start(f32[4,512,512]{2,1,0:T(8,128)} %refs_2_.1) | copy-start | bytes 12582916
  17.1 3.5 %slice-start.1 = ((s8[8388608]{0:T(1024)(128)(4,1)}), s8[4194304]{0:T(1024)(128)(4,1)S(1)}, s32[]{:S(2)}) async-start(s8[8388608]{0:T(1024)(128)(4,1)} %bitcast.23), calls=%async_computation.3 | async-start | bytes 8388608
  17.3 41.1 %copy-start.3 = (f32[8,1,128,32]{2,3,1,0:T(8,128)S(1)}, f32[8,1,128,32]{2,3,1,0:T(8,128)}, u32[]{:S(2)}) copy-start(f32[8,1,128,32]{2,3,1,0:T(8,128)} %param.4) | copy-start | bytes 393220
  17.3 5.6 %collective-permute-start.6 = (f32[1,32,128]{2,1,0:T(8,128)S(1)}, f32[1,32,128]{2,1,0:T(8,128)S(1)}, u32[]{:S(2)}, u32[]{:S(2)}) collective-permute-start(f32[1,32,128]{2,1,0:T(8,128)S(1)} %shard_map.59.own_ref), channel_id=1, source_target_pairs={{32,64},{40,72},{48,80},{56,88},{33,65},{41,73},{49,81},{57,89},{3... | collective-permute-start | bytes 49160 | tf_op jit(solution)/shard_map/ppermute | solution.py:218
  18.1 4.8 %collective-permute-start.5 = (f32[1,32,128]{2,1,0:T(8,128)S(1)}, f32[1,32,128]{2,1,0:T(8,128)S(1)}, u32[]{:S(2)}, u32[]{:S(2)}) collective-permute-start(f32[1,32,128]{2,1,0:T(8,128)S(1)} %shard_map.59.own_ref), channel_id=1, source_target_pairs={{32,72},{40,64},{48,88},{56,80},{33,73},{41,65},{49,89},{57,81},{3... | collective-permute-start | bytes 49160 | tf_op jit(solution)/shard_map/ppermute | solution.py:218
  18.9 4.0 %collective-permute-start.4 = (f32[1,32,128]{2,1,0:T(8,128)S(1)}, f32[1,32,128]{2,1,0:T(8,128)S(1)}, u32[]{:S(2)}, u32[]{:S(2)}) collective-permute-start(f32[1,32,128]{2,1,0:T(8,128)S(1)} %shard_map.59.own_ref), channel_id=1, source_target_pairs={{32,88},{40,80},{48,72},{56,64},{33,89},{41,81},{49,73},{57,65},{3... | collective-permute-start | bytes 49160 | tf_op jit(solution)/shard_map/ppermute | solution.py:218
  19.7 3.2 %collective-permute-start.3 = (f32[1,32,128]{2,1,0:T(8,128)S(1)}, f32[1,32,128]{2,1,0:T(8,128)S(1)}, u32[]{:S(2)}, u32[]{:S(2)}) collective-permute-start(f32[1,32,128]{2,1,0:T(8,128)S(1)} %shard_map.59.own_ref), channel_id=1, source_target_pairs={{32,80},{40,88},{48,64},{56,72},{33,81},{41,89},{49,65},{57,73},{3... | collective-permute-start | bytes 49160 | tf_op jit(solution)/shard_map/ppermute | solution.py:218
  43.2 13.9 %all-to-all-start.1 = ((f32[16,32,128]{2,1,0:T(8,128)}), f32[16,32,128]{2,1,0:T(8,128)S(1)}, u32[]{:S(2)}, u32[]{:S(2)}) async-start(f32[16,32,128]{2,1,0:T(8,128)} %get-tuple-element.30), calls=%async_computation.1 | async-start | bytes 524288 | tf_op jit(solution)/shard_map/all_to_all | solution.py:262
  47.6 10.9 %collective-permute-start.9 = (f32[12,32,128]{2,1,0:T(8,128)S(1)}, f32[12,32,128]{2,1,0:T(8,128)S(1)}, u32[]{:S(2)}, u32[]{:S(2)}) collective-permute-start(f32[12,32,128]{2,1,0:T(8,128)S(1)} %get-tuple-element.32.refs_0_), channel_id=1, source_target_pairs={{0,128},{64,192},{1,129},{65,193},{2,130},{66,194},{3,131},{67,195... | collective-permute-start | bytes 589832 | tf_op jit(solution)/shard_map/ppermute | solution.py:39
  57.1 10.1 %collective-permute-start.10 = (f32[4,32,128]{2,1,0:T(8,128)S(1)}, f32[4,32,128]{2,1,0:T(8,128)S(1)}, u32[]{:S(2)}, u32[]{:S(2)}) collective-permute-start(f32[4,32,128]{2,1,0:T(8,128)S(1)} %slice.26.refs_0_), channel_id=1, source_target_pairs={{0,192},{64,128},{1,193},{65,129},{2,194},{66,130},{3,195},{67,131... | collective-permute-start | bytes 196616 | tf_op jit(solution)/shard_map/ppermute | solution.py:39
  58.5 2.2 %copy-start.1 = (f32[4,512,512]{2,1,0:T(8,128)S(1)}, f32[4,512,512]{2,1,0:T(8,128)}, u32[]{:S(2)}) copy-start(f32[4,512,512]{2,1,0:T(8,128)} %refs_2_.1) | copy-start | bytes 12582916
  60.6 3.4 %copy-start.2 = (f32[8,1,128,2048]{3,2,1,0:T(8,128)S(1)}, f32[8,1,128,2048]{3,2,1,0:T(8,128)}, u32[]{:S(2)}) copy-start(f32[8,1,128,2048]{3,2,1,0:T(8,128)} %param.3) | copy-start | bytes 25165828
  68.1 1.3 %collective-permute-start.11 = (f32[2,8,128]{2,1,0:T(8,128)S(1)}, f32[2,8,128]{2,1,0:T(8,128)S(1)}, u32[]{:S(2)}, u32[]{:S(2)}) collective-permute-start(f32[2,8,128]{2,1,0:T(8,128)S(1)} %get-tuple-element.42), channel_id=1, source_target_pairs={{0,1},{1,0},{2,3},{3,2},{4,5},{5,4},{6,7},{7,6},{8,9},{9,8},{10,11... | collective-permute-start | bytes 24584 | tf_op jit(solution)/shard_map/ppermute | solution.py:276
  69.3 3.7 %collective-permute-start.12 = (f32[2,8,128]{2,1,0:T(8,128)S(1)}, f32[2,8,128]{2,1,0:T(8,128)S(1)}, u32[]{:S(2)}, u32[]{:S(2)}) collective-permute-start(f32[2,8,128]{2,1,0:T(8,128)S(1)} %add.9), channel_id=1, source_target_pairs={{0,2},{2,0},{4,6},{6,4},{1,3},{3,1},{5,7},{7,5},{8,10},{10,8},{12,... | collective-permute-start | bytes 24584 | tf_op jit(solution)/shard_map/ppermute | solution.py:283
  73.0 4.9 %collective-permute-start.13 = (f32[2,8,128]{2,1,0:T(8,128)S(1)}, f32[2,8,128]{2,1,0:T(8,128)S(1)}, u32[]{:S(2)}, u32[]{:S(2)}) collective-permute-start(f32[2,8,128]{2,1,0:T(8,128)S(1)} %add.10), channel_id=1, source_target_pairs={{0,6},{2,4},{4,2},{6,0},{1,7},{3,5},{5,3},{7,1},{8,14},{10,12},{12... | collective-permute-start | bytes 24584 | tf_op jit(solution)/shard_map/ppermute | solution.py:283
